TPU v7x, 32 devices: a whole 2x2x4 slice. The times are simulated.
32 devices in a mesh: space: 8 (over z, x), section: 2 (over core), dp: 2 (over y).
Axes of the slice: x: 2, y: 2, z: 4, core: 2. Of those that a mesh axis runs over, the one named last changes fastest.
Arguments:
- input_field: bfloat16 [2, 2, 16, 8, 8, 256], P(None, 'dp', 'space'), may hold values from -6 to 6
- first_weight: bfloat16 [864, 64], replicated, may hold values from -0.21875 to 0.21875
- second_weight: bfloat16 [1728, 128], replicated, may hold values from -0.15625 to 0.15625
- upstream_grad: bfloat16 [2, 2, 4, 8, 2, 256], P(None, 'dp', None, 'space'), may hold values from -0.25 to 0.25
Outputs:
- first_weight_grad: float32 [864, 64], P('space', 'section')
- second_weight_grad: float32 [1728, 128], P('space', 'section')
All inputs are finite; a program needn't handle non-finite values.
Results may differ from a plain program's by a relative error of at most 0.023.
Values may be sent and summed in bfloat16 or wider, within the bound.
No kernel may reach another device: no remote copies, remote signals or barrier semaphores. Data moves between devices by JAX's collectives and lax.ppermute only.
A program may use at most 64 MiB of HBM per device.

v0:
```python
import jax
import jax.numpy as jnp
from jax import lax
from jax.sharding import PartitionSpec as P

CA = 32
CB = 64
CC = 128
TAPS = 27


SLOPE = 0.3


def passed_along(block, axis, distance):
    devices = range(lax.axis_size(axis))
    route = [(i - distance, i) for i in devices if i - distance in devices]
    return lax.ppermute(block, axis, route)


def from_partner(block, axis, bit):
    count = lax.axis_size(axis)
    route = []
    for low in range(count):
        high = low | 1 << bit
        if high != low and high < count:
            route += [(low, high), (high, low)]
    return lax.ppermute(block, axis, route)


def split_three(volume, position, front_plane):
    half_count = volume.shape[position] // 2
    paired = volume.reshape(
        volume.shape[:position] + (half_count, 2) + volume.shape[position + 1 :]
    )
    even_cells = lax.index_in_dim(paired, 0, position + 1, keepdims=False)
    odd_cells = lax.index_in_dim(paired, 1, position + 1, keepdims=False)
    earlier = jnp.concatenate(
        [front_plane, lax.slice_in_dim(odd_cells, 0, half_count - 1, axis=position)], axis=position
    )
    return [earlier, even_cells, odd_cells]


def edge_zeros(volume, position):
    target_shape = volume.shape[:position] + (1,) + volume.shape[position + 1 :]
    return jnp.zeros(target_shape, volume.dtype)


def patches(volume, front_plane):
    pieces = []
    for along_x in split_three(volume, 0, front_plane):
        for along_y in split_three(along_x, 2, edge_zeros(along_x, 2)):
            for along_z in split_three(along_y, 3, edge_zeros(along_y, 3)):
                pieces.append(along_z)
    return jnp.concatenate(pieces, axis=-1)


def scatter_back(column_grad, target_shape):
    zero_field = jnp.zeros(target_shape, jnp.float32)
    front_plane = jnp.zeros((1,) + tuple(target_shape[1:]), jnp.float32)
    result, pullback = jax.vjp(lambda volume: patches(volume, front_plane), zero_field)
    return pullback(column_grad)[0]


def first_columns(volume, front_plane):
    planes, local_count, rows_y, packed = volume.shape
    cells_z = packed // CA
    shaped = volume.reshape(planes, local_count, rows_y, cells_z, CA)
    edge_plane = front_plane.reshape(1, local_count, rows_y, cells_z, CA)
    return patches(shaped, edge_plane).reshape(-1, TAPS * CA)


def first_forward(columns, first_weight):
    preact = jnp.dot(columns, first_weight, preferred_element_type=jnp.float32)
    return jnp.where(preact > 0, preact, SLOPE * preact).astype(jnp.bfloat16)


def first_grad(columns, hidden, arrived):
    grad_rows = arrived.reshape(-1, CB).astype(jnp.float32)
    delta_rows = jnp.where(hidden.reshape(-1, CB) > 0, grad_rows, SLOPE * grad_rows).astype(
        jnp.bfloat16
    )
    return lax.dot_general(
        columns, delta_rows, (((0,), (0,)), ((), ())), preferred_element_type=jnp.float32
    )


def second_step(arrived, grad_out, second_weight):
    planes, local_count, rows_y, packed = arrived.shape
    cells_z = packed // CB
    volume = arrived.reshape(planes, local_count, rows_y, cells_z, CB)
    front_plane = jnp.zeros((1, local_count, rows_y, cells_z, CB), jnp.bfloat16)
    columns = patches(volume, front_plane).reshape(-1, TAPS * CB)
    preact = jnp.dot(columns, second_weight, preferred_element_type=jnp.float32)
    grad_rows = grad_out.reshape(-1, CC).astype(jnp.float32)
    delta_rows = jnp.where(preact > 0, grad_rows, SLOPE * grad_rows).astype(jnp.bfloat16)
    weight_grad = lax.dot_general(
        columns, delta_rows, (((0,), (0,)), ((), ())), preferred_element_type=jnp.float32
    )
    column_grad = lax.dot_general(
        delta_rows, second_weight, (((1,), (1,)), ((), ())), preferred_element_type=jnp.float32
    )
    column_grad = column_grad.reshape(
        planes // 2, local_count, rows_y // 2, cells_z // 2, TAPS * CB
    )
    back_grad = scatter_back(column_grad, volume.shape).astype(jnp.bfloat16)
    return (weight_grad, back_grad.reshape(arrived.shape))


def regroup(outgoing):
    return lax.all_to_all(outgoing, "space", split_axis=1, concat_axis=1, tiled=True)


def shards(input_field, first_weight, second_weight, upstream_grad):
    micro_count, replica_one, planes, volumes, rows_y, packed = input_field.shape
    spread = lax.axis_size("space")
    per_dev = volumes // spread
    half_planes = planes // 2
    hidden_cols = packed // CA // 2 * CB
    slab_view = (half_planes, spread, per_dev, rows_y // 2, hidden_cols)
    whole_view = (spread * half_planes, per_dev, rows_y // 2, hidden_cols)
    section_index = lax.axis_index("section")
    fields = input_field[:, 0]
    grads_out = upstream_grad[:, 0]

    def to_whole(received):
        return jnp.swapaxes(received, 0, 1).reshape(whole_view)

    def to_sent(back_grad):
        return jnp.swapaxes(
            back_grad.reshape(spread, half_planes, per_dev, rows_y // 2, hidden_cols), 0, 1
        )

    local_micro = fields.shape[0]
    rim_planes = passed_along(fields[:, planes - 1 :], "space", 1)
    first_sources = [
        (fields[micro_index], rim_planes[micro_index]) for micro_index in range(local_micro)
    ]
    first_sum = jnp.zeros((TAPS * CA, CB), jnp.float32)
    second_sum = jnp.zeros((TAPS * CB, CC), jnp.float32)
    arrived = jnp.zeros(slab_view, jnp.bfloat16)
    kept_hidden = []
    for tick_index in range(local_micro + 2):

        def lead_work():
            if tick_index < local_micro:
                source, front_plane = first_sources[tick_index]
                outgoing = first_forward(first_columns(source, front_plane), first_weight).reshape(
                    slab_view
                )
            else:
                outgoing = jnp.zeros(slab_view, jnp.bfloat16)
            summed = first_sum
            if tick_index >= 2:
                source, front_plane = first_sources[tick_index - 2]
                summed = first_sum + first_grad(
                    first_columns(source, front_plane), kept_hidden[tick_index - 2], arrived
                )
            return (outgoing, summed, second_sum)

        def tail_work():
            if 1 <= tick_index <= local_micro:
                weight_grad, back_grad = second_step(
                    to_whole(arrived), grads_out[tick_index - 1], second_weight
                )
                return (to_sent(back_grad), first_sum, second_sum + weight_grad)
            return (jnp.zeros(slab_view, jnp.bfloat16), first_sum, second_sum)

        outgoing, first_sum, second_sum = lax.cond(section_index == 0, lead_work, tail_work)
        kept_hidden.append(outgoing)
        if tick_index <= local_micro:
            outgoing = regroup(outgoing)
            arrived = from_partner(outgoing, "section", 0)
    halves = (
        lax.psum_scatter(first_sum, "section", scatter_dimension=1, tiled=True),
        lax.psum_scatter(second_sum, "section", scatter_dimension=1, tiled=True),
    )
    blocks = (
        lax.psum_scatter(halves[0], "space", scatter_dimension=0, tiled=True),
        lax.psum_scatter(halves[1], "space", scatter_dimension=0, tiled=True),
    )
    totals = lax.psum((blocks[0], blocks[1]), "dp")
    return (totals[0], totals[1])


def solution(mesh):
    return jax.shard_map(
        shards,
        mesh=mesh,
        in_specs=(
            P(None, "dp", "space", None, None, None),
            P(),
            P(),
            P(None, "dp", None, "space", None, None),
        ),
        out_specs=(P("space", "section"), P("space", "section")),
        check_vma=False,
    )
```

profile of v0, /device:TPU:0, one launch (start us, length us, event | category | flops | bytes accessed | tf_op | source)
XLA Modules:
  0.0 192.2 jit_solution(16341084309462589891)
XLA Ops:
  7.2 0.9 slice.982
  8.1 4.8 %collective-permute-start = (bf16[2,1,8,8,256]{4,3,2,1,0:T(8,128)(2,1)S(1)}, bf16[2,1,8,8,256]{4,3,2,1,0:T(8,128)(2,1)S(1)}, u32[]{:S(2)}, u32[]{:S(2)}) collective-permute-start(bf16[2,1,8,8,256]{4,3,2,1,0:T(8,128)(2,1)S(1)} %slice.982), channel_id=1, source_target_pairs={{0,4},{4,8},{8,12},{12,16},{16,20},{20,24},{24,28},{1,5},{5,9},{9,... | collective-permute-start | bytes 196616 | tf_op jit(solution)/shard_map/ppermute | solution.py:18
  13.0 1.8 collective-permute-done
  14.8 3.5 %conditional.4 = (bf16[1,8,1,4,256]{4,3,1,2,0:T(4,128)(2,1)S(1)}) conditional(s32[]{:T(128)} %convert_element_type.78, () %tuple.36, (bf16[1,1,8,8,256]{4,3,2,1,0:T(8,128)(2,1)S(1)}, bf16[1,2,8,8,256]{4,3,2,1,0:T(8,128)(2,1)S(1)}, bf16[864,64]{0,1:T(8,128)(2,1)S(1)}) %tuple.268), branch_computations={%region_0.0_spmd, %region_1.2_spmd} | conditional | flops 14188544 | bytes 2701344 | solution.py:169
  17.4 0.5 concatenate.246
  17.9 0.2 fusion
  18.4 13.1 %all_to_all.15 = bf16[1,8,1,4,256]{4,3,2,0,1:T(4,128)(2,1)S(1)} all-to-all(bf16[1,8,1,4,256]{4,3,2,0,1:T(4,128)(2,1)S(1)} %bitcast.677), channel_id=1, replica_groups=mesh['space'=8,'section'=2,'dp'=2] {'space'}, dimensions={1} | all-to-all | bytes 32768 | tf_op jit(solution)/shard_map/all_to_all | solution.py:111
  31.5 1.2 collective-permute-done.1
  32.6 3.9 %conditional.5 = (bf16[1,8,1,4,256]{4,1,3,2,0:T(8,128)(2,1)S(1)}, f32[1728,128]{1,0:T(8,128)S(1)}) conditional(s32[]{:T(128)} %convert_element_type.78, (bf16[1,8,1,4,256]{4,3,2,0,1:T(4,128)(2,1)S(1)}, bf16[1728,128]{1,0:T(8,128)(2,1)S(1)}, bf16[2,4,1,2,256]{4,3,1,2,0:T(2,128)(2,1)S(1)}) %tuple.270, (bf16[1,1,8,8,256]{4,3,2,1,0:T(8,128)(2,1)S(1)}, ...), branch_computations={%region_2.3_spmd, %region_3.4_spmd} | conditional | flops 21309440 | bytes 3679274 | solution.py:169
  35.5 0.5 concatenate.408
  36.5 8.9 %all_to_all.16 = bf16[1,8,1,4,256]{4,3,2,0,1:T(4,128)(2,1)S(1)} all-to-all(bf16[1,8,1,4,256]{4,3,2,0,1:T(4,128)(2,1)S(1)} %copy.710), channel_id=1, replica_groups=mesh['space'=8,'section'=2,'dp'=2] {'space'}, dimensions={1} | all-to-all | bytes 32768 | tf_op jit(solution)/shard_map/all_to_all | solution.py:111
  45.5 1.2 collective-permute-done.2
  46.6 3.4 %conditional.6 = (bf16[1,8,1,4,256]{4,1,3,2,0:T(8,128)(2,1)S(1)}, f32[864,64]{1,0:T(8,128)S(1)}, f32[1728,128]{1,0:T(8,128)S(1)}) conditional(s32[]{:T(128)} %convert_element_type.78, (bf16[1,8,1,4,256]{4,3,2,0,1:T(4,128)(2,1)S(1)}, bf16[1728,128]{1,0:T(8,128)(2,1)S(1)}, bf16[2,4,1,2,256]{4,3,1,2,0:T(2,128)(2,1)S(1)}, ...), branch_computations={%region_4.5_spmd, %region_5.6_spmd} | conditional | flops 21530624 | bytes 4835378 | solution.py:169
  49.0 0.5 concatenate.529
  49.7 0.2 fusion.23
  50.1 8.9 %all_to_all.17 = bf16[1,8,1,4,256]{4,3,2,0,1:T(4,128)(2,1)S(1)} all-to-all(bf16[1,8,1,4,256]{4,3,2,0,1:T(4,128)(2,1)S(1)} %copy.714), channel_id=1, replica_groups=mesh['space'=8,'section'=2,'dp'=2] {'space'}, dimensions={1} | all-to-all | bytes 32768 | tf_op jit(solution)/shard_map/all_to_all | solution.py:111
  59.0 1.2 collective-permute-done.3
  60.2 3.7 %conditional.7 = (f32[864,64]{0,1:T(8,128)S(1)}) conditional(s32[]{:T(128)} %convert_element_type.78, (f32[864,64]{1,0:T(8,128)S(1)}) %tuple.78, (bf16[1,1,8,8,256]{4,3,2,1,0:T(8,128)(2,1)S(1)}, bf16[1,2,8,8,256]{4,3,2,1,0:T(8,128)(2,1)S(1)}, bf16[1,8,1,4,256]{4,1,3,2,0:T(8,128)(2,1)S(1)}, bf16[1,8,1,4,256]{4,3,2,0,1:T(4,128)(2,1)S(1)}, ...), branch_computations={%region_6.7_spmd, %region_7.8_spmd} | conditional | flops 14252032 | bytes 3606560 | solution.py:169
  62.8 0.5 concatenate.569
  63.7 0.2 convolution_add_fusion.1
  63.9 0.7 copy-done.1
  64.7 1.3 copy.719
  66.0 3.7 %reduce-scatter.5.cloned.1.call-done = f32[864,32]{0,1:T(8,128)} async-done(((f32[864,64]{0,1:T(8,128)}), f32[864,32]{0,1:T(8,128)}) %reduce-scatter.5.cloned.1.call-update) | async-done | bytes 110608 | tf_op jit(solution)/shard_map/reduce_scatter | solution.py:175
  69.7 11.8 %reduce-scatter.7.cloned.1.call-done = f32[1728,64]{0,1:T(8,128)} async-done(((f32[1728,128]{0,1:T(8,128)}), f32[1728,64]{0,1:T(8,128)}) %reduce-scatter.7.cloned.1.call-update) | async-done | bytes 442384 | tf_op jit(solution)/shard_map/reduce_scatter | solution.py:176
  81.6 0.6 copy-done.5
  82.3 0.6 dynamic-slice
  84.2 75.3 %all-reduce.159.cloned.1.call-done = (f32[864,32]{0,1:T(8,128)}, f32[1728,64]{0,1:T(8,128)}) async-done(((f32[864,32]{0,1:T(8,128)}, f32[1728,64]{0,1:T(8,128)}), (f32[864,32]{0,1:T(8,128)}, f32[1728,64]{0,1:T(8,128)})) %all-reduce.159.cloned.1.call-update) | async-done | bytes 552976
  159.5 1.6 constant_dynamic-slice_fusion
  161.1 1.4 constant_dynamic-slice_fusion.1
  162.6 20.4 %all-reduce.161.cloned.1.call-done = (f32[108,32]{0,1:T(8,128)}, f32[216,64]{0,1:T(8,128)}) async-done(((f32[108,32]{0,1:T(8,128)}, f32[216,64]{0,1:T(8,128)}), (f32[108,32]{0,1:T(8,128)}, f32[216,64]{0,1:T(8,128)})) %all-reduce.161.cloned.1.call-update) | async-done | bytes 69136 | tf_op jit(solution)/shard_map/psum | solution.py:182
  182.9 1.3 copy.1016
  184.2 1.5 copy.1017
  (343 shorter events, 9.6 us)
Async XLA Ops:
  7.2 5.8 %copy-start.3 = (bf16[2,1,2,8,8,256]{5,4,3,2,1,0:T(8,128)(2,1)S(1)}, bf16[2,1,2,8,8,256]{5,4,3,2,1,0:T(8,128)(2,1)}, u32[]{:S(2)}) copy-start(bf16[2,1,2,8,8,256]{5,4,3,2,1,0:T(8,128)(2,1)} %param.12) | copy-start | bytes 393220
  7.2 62.6 %reduce-scatter.5.cloned.1.call-start = ((), (), s32[]{:S(2)}) async-start(), calls=%async_computation.5 | async-start | bytes 344064 | tf_op jit(solution)/shard_map/reduce_scatter | solution.py:175
  8.1 6.7 %collective-permute-start = (bf16[2,1,8,8,256]{4,3,2,1,0:T(8,128)(2,1)S(1)}, bf16[2,1,8,8,256]{4,3,2,1,0:T(8,128)(2,1)S(1)}, u32[]{:S(2)}, u32[]{:S(2)}) collective-permute-start(bf16[2,1,8,8,256]{4,3,2,1,0:T(8,128)(2,1)S(1)} %slice.982), channel_id=1, source_target_pairs={{0,4},{4,8},{8,12},{12,16},{16,20},{20,24},{24,28},{1,5},{5,9},{9,... | collective-permute-start | bytes 196616 | tf_op jit(solution)/shard_map/ppermute | solution.py:18
  13.0 1.9 copy-start.2
  14.8 17.8 %copy-start = (bf16[1728,128]{1,0:T(8,128)(2,1)S(1)}, bf16[1728,128]{1,0:T(8,128)(2,1)}, u32[]{:S(2)}) copy-start(bf16[1728,128]{1,0:T(8,128)(2,1)} %param.14) | copy-start | bytes 1327108
  18.4 14.3 %copy-start.4 = (bf16[2,1,4,1,2,256]{5,4,3,2,1,0:T(2,128)(2,1)S(1)}, bf16[2,1,4,1,2,256]{5,4,3,2,1,0:T(2,128)(2,1)}, u32[]{:S(2)}) copy-start(bf16[2,1,4,1,2,256]{5,4,3,2,1,0:T(2,128)(2,1)} %param.15) | copy-start | bytes 24580
  31.5 1.2 collective-permute-start.1
  45.5 1.2 collective-permute-start.2
  59.0 1.2 collective-permute-start.3
  63.9 0.7 copy-start.1
  64.7 16.9 %reduce-scatter.7.cloned.1.call-start = ((), (), s32[]{:S(2)}) async-start(), calls=%async_computation.6 | async-start | bytes 1376256 | tf_op jit(solution)/shard_map/reduce_scatter | solution.py:176
  66.0 93.5 %all-reduce.159.cloned.1.call-start = ((), (), s32[]{:S(2)}) async-start(), calls=%async_computation.7 | async-start | bytes 1146880
  81.6 101.3 %all-reduce.161.cloned.1.call-start = ((), (), s32[]{:S(2)}) async-start(), calls=%async_computation.8 | async-start | bytes 163840 | tf_op jit(solution)/shard_map/psum | solution.py:182
  81.6 0.7 copy-start.5
Sparse Core Ops, SparseCore 0:
  64.8 4.9 reduce-scatter.4
  72.0 9.5 reduce-scatter.6
  85.5 73.9 all-reduce.158
  162.7 20.1 all-reduce.160
where the time goes:
time: 193 us; the launch traced here: 192 us
  waiting for transfers between devices  117 us (61%)
  blocking collectives  30.9 us (16%)
  local copies, waits for them, and re-layouts  21.1 us (11%)
  between operations  15.2 us (8%)
  starting transfers between devices  5 us (3%)
  loops' own time  2.46 us (1%)
    unnamed x5, waiting for transfers between devices  75.4 us
    all_to_all x3, blocking collectives, regroup(): lax.all_to_all(outgoing, 'space', split_axis=1, concat_axis=1, tiled=True)  30.9 us
    psum x1, waiting for transfers between devices, shards(): totals = lax.psum((blocks[0], blocks[1]), 'dp')  20.4 us
    reduce_scatter x1, waiting for transfers between devices, shards(): lax.psum_scatter(second_sum, 'section', scatter_dimension=1, tiled=True)  11.8 us
    unnamed x17, local copies, waits for them, and re-layouts  7.78 us
    ppermute x1, starting transfers between devices, passed_along(): return lax.ppermute(block, axis, route)  4.83 us
  transfers between devices with their start and end apart: 8, of which 8 were waited for; matrix products, arithmetic and copies ran while one was open for 1% of the time, Pallas kernels for 0%

commit v1 on v0

v1 whole, which is shorter than its diff:
```python
import jax
import jax.numpy as jnp
from jax import lax
from jax.experimental import pallas as pl
from jax.experimental.pallas import tpu as pltpu
from jax.sharding import PartitionSpec as P

CA = 32
CB = 64
CC = 128
TAPS = 27
SLOPE = 0.3
BF16 = jnp.bfloat16
F32 = jnp.float32


def round_up(value, step):
    return -(-value // step) * step


def leaky(condition, value):
    return jnp.where(condition > 0, value, SLOPE * value)


def contract(a, b, dim_a, dim_b):
    return lax.dot_general(a, b, (((dim_a,), (dim_b,)), ((), ())), preferred_element_type=F32)


def call(body, out_shape, scratch, args):
    vmem = pl.BlockSpec(memory_space=pltpu.VMEM)
    many = isinstance(out_shape, (list, tuple))
    return pl.pallas_call(
        body,
        out_shape=out_shape,
        in_specs=[vmem] * len(args),
        out_specs=[vmem] * len(out_shape) if many else vmem,
        scratch_shapes=scratch,
        compiler_params=pltpu.CompilerParams(vmem_limit_bytes=48 << 20),
    )(*args)


def banded_body(weight, banded):
    lane = lax.broadcasted_iota(jnp.int32, (CA, 2 * CB), 1)
    zero = jnp.zeros((CA, 2 * CB), F32)
    for tap in range(9):
        left, right = [], []
        for kz in range(3):
            part = weight[pl.ds((3 * tap + kz) * CA, CA), :].astype(F32)
            both = jnp.concatenate([part, part], axis=1)
            left.append(jnp.where(lane < CB, both, 0.0))
            right.append(jnp.where(lane < CB, 0.0, both))
        for half in range(2):
            rows = []
            for z in range(8):
                block = zero
                for odd, side in ((0, left), (1, right)):
                    kz = z - 2 * (2 * half + odd) + 1
                    if 0 <= kz <= 2:
                        block = block + side[kz]
                rows.append(block)
            banded[pl.ds(tap * 256, 256), half * 128 : half * 128 + 128] = jnp.concatenate(
                rows, axis=0
            ).astype(BF16)


def main_body(count, spread, mine, got, before, upstream, banded, second, keep, send, xf, hid, hgs, t2, t1):
    side = lax.axis_index("space") % 2
    section = lax.axis_index("section")
    rows = count * 4
    planes = [before[i] for i in range(3)]
    own, other = [mine[0], mine[1]], [got[0], got[1]]
    first = side == 0
    planes += [jnp.where(first, own[i], other[i]) for i in range(2)]
    planes += [jnp.where(first, other[i], own[i]) for i in range(2)]
    row = lax.broadcasted_iota(jnp.int32, (rows, 256), 0)
    tiles = []
    for i, plane in enumerate(planes):
        flat = plane.reshape(count * 8, 256).astype(F32)
        for h in range(2):
            xf[i, h, 0:8, :] = jnp.zeros((8, 128), F32)
            xf[i, h, pl.ds(8, count * 8), :] = flat[:, h * 128 : h * 128 + 128]
        triple = []
        for ky in range(3):
            part = jnp.concatenate(
                [xf[i, h, pl.ds(7 + ky, rows, stride=2), :] for h in range(2)], axis=1
            )
            if ky == 0:
                part = jnp.where(row % 4 == 0, 0.0, part)
            triple.append(part.astype(BF16))
        tiles.append(triple)
    columns = [
        jnp.concatenate([tiles[2 * i + kx][ky] for i in range(3)], axis=0)
        for kx in range(3)
        for ky in range(3)
    ]
    preact = jnp.dot(jnp.concatenate(columns, axis=1), banded[...], preferred_element_type=F32)
    hidden = leaky(preact, preact).astype(BF16).astype(F32)
    half = count * 2
    lane = lax.broadcasted_iota(jnp.int32, (half, 128), 1)
    low = lane < CB
    row2 = lax.broadcasted_iota(jnp.int32, (half, 128), 0)
    cols = []
    for kx in range(3):
        for h in range(2):
            hid[kx, h, 0:8, :] = jnp.zeros((8, 128), F32)
            hid[kx, h, pl.ds(8, rows), :] = hidden[
                kx * rows : kx * rows + rows, h * 128 : h * 128 + 128
            ]
        for ky in range(3):
            a = hid[kx, 0, pl.ds(7 + ky, half, stride=2), :]
            b = hid[kx, 1, pl.ds(7 + ky, half, stride=2), :]
            if ky == 0:
                a = jnp.where(row2 % 2 == 0, 0.0, a)
                b = jnp.where(row2 % 2 == 0, 0.0, b)
            ra = pltpu.roll(a, 64, 1)
            rb = pltpu.roll(b, 64, 1)
            zero_k = jnp.concatenate([jnp.where(low, 0.0, ra), ra[:, :CB]], axis=1)
            one_k = jnp.concatenate([jnp.where(low, ra, rb), rb[:, :CB]], axis=1)
            cols.append(jnp.concatenate([zero_k, one_k], axis=0).astype(BF16))
    out = jnp.zeros((2 * half, CC), F32)
    for tap in range(9):
        out = out + jnp.dot(
            cols[tap], second[pl.ds(tap * 192, 192), :], preferred_element_type=F32
        )
    up = upstream[...].reshape(half, 256).astype(F32)
    up = jnp.concatenate([up[:, :128], up[:, 128:]], axis=0)
    delta = leaky(out, up)
    delta_b = delta.astype(BF16)
    turned = jnp.where(section == 0, delta, pltpu.roll(delta, 64, 1)).astype(BF16)
    for tap in range(9):
        t2[pl.ds(tap * 192, 192), :] = contract(cols[tap], turned, 0, 0)
    row3 = lax.broadcasted_iota(jnp.int32, (2 * half, 128), 0)
    for kx in range(3):
        parts = []
        for ky in range(3):
            base = (3 * kx + ky) * 192
            c0 = contract(delta_b, second[pl.ds(base, 128), :], 1, 1)
            c1 = contract(delta_b, second[pl.ds(base + 128, 64), :], 1, 1)
            parts.append((c0, jnp.concatenate([c1, c1], axis=1)))
        odd = []
        for late, early in zip(parts[2], parts[0]):
            shifted = pltpu.roll(early, 2 * half - 1, 0)
            odd.append(late + jnp.where(row3 % 2 == 0, shifted, 0.0))
        for parity, (c0, c1) in enumerate((parts[1], odd)):
            turn = pltpu.roll(c0, 64, 1)
            k0, k1 = turn[:half], turn[half:]
            a = jnp.where(low, k0, c1[:half] + k1)
            b = jnp.where(low, k1, c1[half:])
            hgs[kx, 0, pl.ds(parity, half, stride=2), :] = a
            hgs[kx, 1, pl.ds(parity, half, stride=2), :] = b
    hidden_grad = jnp.concatenate(
        [jnp.concatenate([hgs[kx, h] for kx in range(3)], axis=0) for h in range(2)], axis=1
    )
    hidden_grad = hidden_grad.astype(BF16).astype(F32)
    delta_a = leaky(hidden, hidden_grad).astype(BF16)
    wide = lax.broadcasted_iota(jnp.int32, (96, 128), 1) < CB
    for tap in range(9):
        grid = contract(columns[tap], delta_a, 0, 0)
        g0, g1 = grid[:, :128], grid[:, 128:]
        left = jnp.concatenate([g1[96:128], g0[0:64] + g1[128:192]], axis=0)
        right = g0[32:128] + g1[160:256]
        fold = jnp.where(wide, left, right)
        fold = fold + pltpu.roll(fold, 64, 1)
        t1[pl.ds(tap * 96, 96), :] = jnp.where(section == 0, fold, pltpu.roll(fold, 32, 1))
    r2, r1 = TAPS * CB // spread, TAPS * CA // spread
    h2, h1 = packed_rows(spread)
    t2[pl.ds(TAPS * CB, t2.shape[0] - TAPS * CB), :] = jnp.zeros((t2.shape[0] - TAPS * CB, 128), F32)
    t1[pl.ds(TAPS * CA, t1.shape[0] - TAPS * CA), :] = jnp.zeros((t1.shape[0] - TAPS * CA, 128), F32)
    low2 = lax.broadcasted_iota(jnp.int32, (h2, 128), 1) < CB
    quarter = lax.broadcasted_iota(jnp.int32, (h1, 128), 1) // 32
    for d in range(spread):
        a = t2[pl.ds(d * r2, h2), :]
        b = t2[pl.ds(d * r2 + h2, h2), :]
        keep[d, 0:h2, :] = jnp.where(low2, a, pltpu.roll(b, 64, 1)).astype(BF16)
        send[d, 0:h2, :] = jnp.where(low2, pltpu.roll(a, 64, 1), b).astype(BF16)
        kept, sent = None, None
        for g in range(4):
            straight = t1[pl.ds(d * r1 + g * h1, h1), :]
            turn = pltpu.roll(straight, 32, 1)
            k, o = (straight, turn) if g % 2 == 0 else (turn, straight)
            kept = k if g == 0 else jnp.where(quarter == g, k, kept)
            sent = o if g == 0 else jnp.where(quarter == g, o, sent)
        keep[d, h2 : h2 + h1, :] = kept.astype(BF16)
        send[d, h2 : h2 + h1, :] = sent.astype(BF16)


def packed_rows(spread):
    r2, r1 = TAPS * CB // spread, TAPS * CA // spread
    return round_up(-(-r2 // 2), 16), round_up(-(-r1 // 4), 16)


def unpack_body(spread, mine, got, first_out, second_out):
    r2, r1 = TAPS * CB // spread, TAPS * CA // spread
    h2, h1 = packed_rows(spread)
    total = mine[...].astype(F32) + got[...].astype(F32)
    top, rest = total[:h2], total[h2:]
    second_out[0:h2, :] = top[:, :CB]
    second_out[pl.ds(h2, r2 - h2), :] = pltpu.roll(top, 64, 1)[: r2 - h2, :CB]
    for g in range(4):
        size = min(h1, r1 - g * h1)
        if size > 0:
            part = rest if g == 0 else pltpu.roll(rest, 128 - 32 * g, 1)
            first_out[pl.ds(g * h1, size), :] = part[:size, : CB // 2]


def swap_bit(count, bit):
    return [(i, i ^ (1 << bit)) for i in range(count)]


def pick(array, index, axis):
    return lax.dynamic_index_in_dim(array, index, axis, keepdims=False)


def shards(input_field, first_weight, second_weight, upstream_grad):
    micro_count, _, planes, volumes, rows_y, packed = input_field.shape
    spread = lax.axis_size("space")
    count = volumes // 2
    pairs = spread // 2
    space = lax.axis_index("space")
    section = lax.axis_index("section")
    side, pair = space % 2, space // 2

    own = pick(input_field[:, 0], section, 0).reshape(planes, count, 2, rows_y, packed)
    mine = pick(own, side, 2)
    got = lax.ppermute(pick(own, 1 - side, 2), "space", swap_bit(spread, 0))
    onward = jnp.where(
        side == 0,
        jnp.stack([mine[1], got[0], got[1]]),
        jnp.stack([got[1], mine[0], mine[1]]),
    )
    before = lax.ppermute(onward, "space", [(i, i + 2) for i in range(spread - 2)])

    up = pick(upstream_grad[:, 0], section, 0)
    bit = 0
    while 1 << bit < pairs:
        up = up.reshape(up.shape[0] // 2, 2, -1, *up.shape[-2:])
        here = (pair >> bit) & 1
        kept = pick(up, here, 1)
        came = lax.ppermute(pick(up, 1 - here, 1), "space", swap_bit(spread, bit + 1))
        up = jnp.where(here == 0, jnp.stack([kept, came], 1), jnp.stack([came, kept], 1))
        up = up.reshape(up.shape[0], -1, *up.shape[-2:])
        bit += 1
    up = up.reshape(count, *up.shape[-2:])

    banded = call(banded_body, jax.ShapeDtypeStruct((9 * 256, 256), BF16), [], (first_weight,))
    h2, h1 = packed_rows(spread)
    block = jax.ShapeDtypeStruct((spread, h2 + h1, 128), BF16)
    kept, outgoing = call(
        lambda *refs: main_body(count, spread, *refs),
        [block, block],
        [
            pltpu.VMEM((7, 2, count * 8 + 16, 128), F32),
            pltpu.VMEM((3, 2, count * 4 + 16, 128), F32),
            pltpu.VMEM((3, 2, count * 4, 128), F32),
            pltpu.VMEM((TAPS * CB + 2 * h2, 128), F32),
            pltpu.VMEM((TAPS * CA + 4 * h1, 128), F32),
        ],
        (mine, got, before, up, banded, second_weight),
    )

    def added(a, b):
        return (a.astype(F32) + b.astype(F32)).astype(BF16)

    total = added(kept, lax.ppermute(outgoing, "section", swap_bit(2, 0)))
    bits = spread.bit_length() - 1
    for bit in range(bits):
        paired = total.reshape(total.shape[0] // 2, 2, *total.shape[1:])
        here = (space >> bit) & 1
        kept = pick(paired, here, 1)
        total = added(kept, lax.ppermute(pick(paired, 1 - here, 1), "space", swap_bit(spread, bit)))
    total = total[0]
    replicas = lax.axis_size("dp")
    bit = 0
    while 1 << (bit + 1) < replicas:
        total = added(total, lax.ppermute(total, "dp", swap_bit(replicas, bit)))
        bit += 1
    came = lax.ppermute(total, "dp", swap_bit(replicas, bit))
    return tuple(
        call(
            lambda *refs: unpack_body(spread, *refs),
            [
                jax.ShapeDtypeStruct((TAPS * CA // spread, CB // 2), F32),
                jax.ShapeDtypeStruct((TAPS * CB // spread, CC // 2), F32),
            ],
            [],
            (total, came),
        )
    )


def solution(mesh):
    return jax.shard_map(
        shards,
        mesh=mesh,
        in_specs=(
            P(None, "dp", "space", None, None, None),
            P(),
            P(),
            P(None, "dp", None, "space", None, None),
        ),
        out_specs=(P("space", "section"), P("space", "section")),
        check_vma=False,
    )
```

time: 193 us -> 39.9 us (0.21)
  waiting for transfers between devices: 117 us -> 14.9 us
  blocking collectives: 30.9 us -> 0 us
  local copies, waits for them, and re-layouts: 21.1 us -> 3.3 us
  between operations: 15.2 us -> 0.82 us
  starting transfers between devices: 5 us -> 17.9 us
  Pallas kernels: 0 us -> 2.54 us
  loops' own time: 2.46 us -> 0 us
    unnamed x5 -> x0, waiting for transfers between devices: 75.4 us -> none
    all_to_all x3 -> x0, blocking collectives: 30.9 us -> none  [regroup(): lax.all_to_all(outgoing, 'space', split_axis=1, concat_axis=1, tiled=True)]
    psum x1 -> x0, waiting for transfers between devices: 20.4 us -> none  [shards(): totals = lax.psum((blocks[0], blocks[1]), 'dp')]
    reduce_scatter x2 -> x0, waiting for transfers between devices: 15.5 us -> none  [the longest x1 11.8 us: shards(): lax.psum_scatter(second_sum, 'section', scatter_dimension=1, tiled=True)]
    ppermute x4 -> x9, starting transfers between devices: 4.84 us -> 17.9 us  [the longest x3 6.38 us: shards(): lax.ppermute(pick(paired, 1 - here, 1), 'space', swap_bit(spread, bit))]
    ppermute x4 -> x9, waiting for transfers between devices: 5.38 us -> 14.9 us  [the longest x3 9.23 us: shards(): lax.ppermute(pick(paired, 1 - here, 1), 'space', swap_bit(spread, bit))]
    unnamed x17 -> x6, local copies, waits for them, and re-layouts: 7.78 us -> 1.09 us
    slice x155 -> x2, local copies, waits for them, and re-layouts: 4.83 us -> 0.01 us  [the longest x1 0.01 us: shards(): mine[0]]
  transfers between devices with their start and end apart: 8 -> 9, of which waited for: 8 -> 6; matrix products, arithmetic and copies ran while one was open for 1% -> 3% of each run, Pallas kernels for 0% -> 1%
where the time goes in v1:
time: 39.9 us; the launch traced here: 39.7 us
  starting transfers between devices  17.9 us (45%)
  waiting for transfers between devices  14.9 us (37%)
  local copies, waits for them, and re-layouts  3.3 us (8%)
  Pallas kernels  2.54 us (6%)
  between operations  0.82 us (2%)
    ppermute x3, waiting for transfers between devices, shards(): lax.ppermute(pick(paired, 1 - here, 1), 'space', swap_bit(spread, bit))  9.23 us
    ppermute x3, starting transfers between devices, shards(): lax.ppermute(pick(paired, 1 - here, 1), 'space', swap_bit(spread, bit))  6.38 us
    ppermute x2, starting transfers between devices, shards(): lax.ppermute(pick(up, 1 - here, 1), 'space', swap_bit(spread, bit + 1))  5.74 us
    ppermute x1, starting transfers between devices, shards(): lax.ppermute(onward, 'space', [(i, i + 2) for i in range(spread - 2)])  2.55 us
    pallas_call x3, Pallas kernels, call(): pl.pallas_call(body, out_shape=out_shape, in_specs=[vmem] * len(args), ou...  2.54 us
    ppermute x1, waiting for transfers between devices, shards(): came = lax.ppermute(total, 'dp', swap_bit(replicas, bit))  2.44 us
    ppermute x1, waiting for transfers between devices, shards(): lax.ppermute(onward, 'space', [(i, i + 2) for i in range(spread - 2)])  1.7 us
    ppermute x1, starting transfers between devices, shards(): came = lax.ppermute(total, 'dp', swap_bit(replicas, bit))  1.58 us
  transfers between devices with their start and end apart: 9, of which 6 were waited for; matrix products, arithmetic and copies ran while one was open for 3% of the time, Pallas kernels for 1%

profile of v1, /device:TPU:0, one launch (start us, length us, event | category | flops | bytes accessed | tf_op | source)
XLA Modules:
  0.0 39.7 jit_solution(4594164412938264549)
XLA Ops:
  0.6 0.0 copy-start
  0.7 0.7 %constant_dynamic-slice_fusion.5 = bf16[1,1,4,1,2,256]{5,4,3,2,1,0:T(2,128)(2,1)S(1)} fusion(bf16[2,1,4,1,2,256]{5,4,3,2,1,0:T(2,128)(2,1)} %param.7, s32[]{:T(128)S(6)} %select_n.97), kind=kLoop, calls=%fused_computation.22 | loop fusion | bytes 8196 | tf_op jit(solution)/shard_map/jit(dynamic_index_in_dim)/dynamic_slice | solution.py:211
  1.4 0.0 copy-start.1
  1.4 3.1 %collective-permute-start.2 = (bf16[2,1,2,256]{3,2,0,1:T(2,128)(2,1)S(1)}, bf16[2,1,2,256]{3,2,0,1:T(2,128)(2,1)S(1)}, u32[]{:S(2)}, u32[]{:S(2)}) collective-permute-start(bf16[2,1,2,256]{3,2,0,1:T(2,128)(2,1)S(1)} %get-tuple-element.18), channel_id=1, source_target_pairs={{0,8},{4,12},{8,0},{12,4},{16,24},{20,28},{24,16},{28,20},{1,9},{5... | collective-permute-start | bytes 6152 | tf_op jit(solution)/shard_map/ppermute | solution.py:239
  4.5 0.0 copy-done
  4.5 1.6 %collective-permute-start = (bf16[2,4,8,256]{3,2,1,0:T(8,128)(2,1)S(1)}, bf16[2,4,8,256]{3,2,1,0:T(8,128)(2,1)S(1)}, u32[]{:S(2)}, u32[]{:S(2)}) collective-permute-start(bf16[2,4,8,256]{3,2,1,0:T(8,128)(2,1)S(1)} %get-tuple-element.12), channel_id=1, source_target_pairs={{0,4},{4,0},{8,12},{12,8},{16,20},{20,16},{24,28},{28,24},{1,5},{5... | collective-permute-start | bytes 98312 | tf_op jit(solution)/shard_map/ppermute | solution.py:225
  6.1 1.1 %copy.10.weight = bf16[864,64]{1,0:T(8,128)(2,1)S(1)} copy(bf16[864,64]{0,1:T(8,128)(2,1)} %param.5) | data formatting | bytes 221184 | tf_op args[1]
  7.2 0.2 shard_map.59.refs_4_
  7.4 0.0 collective-permute-done.2
  7.5 2.7 %collective-permute-start.3 = (bf16[1,2,2,256]{3,2,1,0:T(2,128)(2,1)S(1)}, bf16[1,2,2,256]{3,2,1,0:T(2,128)(2,1)S(1)}, u32[]{:S(2)}, u32[]{:S(2)}) collective-permute-start(bf16[1,2,2,256]{3,2,1,0:T(2,128)(2,1)S(1)} %get-tuple-element.16), channel_id=1, source_target_pairs={{0,16},{4,20},{8,24},{12,28},{16,0},{20,4},{24,8},{28,12},{1,17},{... | collective-permute-start | bytes 6152 | tf_op jit(solution)/shard_map/ppermute | solution.py:239
  10.1 0.0 collective-permute-done.refs_1_
  10.2 2.6 %collective-permute-start.1 = (bf16[3,4,8,256]{3,2,1,0:T(8,128)(2,1)S(1)}, bf16[3,4,8,256]{3,2,1,0:T(8,128)(2,1)S(1)}, u32[]{:S(2)}, u32[]{:S(2)}) collective-permute-start(bf16[3,4,8,256]{3,2,1,0:T(8,128)(2,1)S(1)} %maximum_select_fusion), channel_id=1, source_target_pairs={{0,8},{4,12},{8,16},{12,20},{16,24},{20,28},{1,9},{5,13},{9,17},{1... | collective-permute-start | bytes 147464 | tf_op jit(solution)/shard_map/ppermute | solution.py:231
  12.7 0.0 collective-permute-done.3
  12.7 1.7 %collective-permute-done.1.refs_2_ = bf16[3,4,8,256]{3,2,1,0:T(8,128)(2,1)S(1)} collective-permute-done((bf16[3,4,8,256]{3,2,1,0:T(8,128)(2,1)S(1)}, bf16[3,4,8,256]{3,2,1,0:T(8,128)(2,1)S(1)}, u32[]{:S(2)}, u32[]{:S(2)}) %collective-permute-start.1) | collective-permute-done | bytes 49184 | tf_op jit(solution)/shard_map/ppermute | solution.py:231
  14.4 0.0 copy-done.1
  14.4 2.2 %shard_map.60 = (bf16[8,144,128]{2,1,0:T(8,128)(2,1)S(1)}, bf16[8,144,128]{2,1,0:T(8,128)(2,1)S(1)}) custom-call(bf16[2,4,8,256]{3,2,1,0:T(8,128)(2,1)S(1)} %get-tuple-element.11.refs_0_, bf16[2,4,8,256]{3,2,1,0:T(8,128)(2,1)S(1)} %collective-permute-done.refs_1_, bf16[3,4,8,256]{3,2,1,0:T(8,128)(2,1)S(1)} %collective-permute-done.1.refs_2_, ...), custom_call_target="tpu_custom_call" | custom-call | tf_op jit(solution)/shard_map/pallas_call | solution.py:32
  16.7 0.1 collective-permute-start.4
  16.7 1.6 %collective-permute-done.4 = bf16[8,144,128]{2,1,0:T(8,128)(2,1)S(1)} collective-permute-done((bf16[8,144,128]{2,1,0:T(8,128)(2,1)S(1)}, bf16[8,144,128]{2,1,0:T(8,128)(2,1)S(1)}, u32[]{:S(2)}, u32[]{:S(2)}) %collective-permute-start.4) | collective-permute-done | bytes 294944 | tf_op jit(solution)/shard_map/ppermute | solution.py:264
  18.3 0.1 add_convert_fusion
  18.4 1.6 %collective-permute-start.5 = (bf16[4,144,128]{2,1,0:T(8,128)(2,1)S(1)}, bf16[4,144,128]{2,1,0:T(8,128)(2,1)S(1)}, u32[]{:S(2)}, u32[]{:S(2)}) collective-permute-start(bf16[4,144,128]{2,1,0:T(8,128)(2,1)S(1)} %dynamic-slice_bitcast_fusion), channel_id=1, source_target_pairs={{0,4},{4,0},{8,12},{12,8},{16,20},{20,16},{24,28},{28,24},{1,5},{5... | collective-permute-start | bytes 442376 | tf_op jit(solution)/shard_map/ppermute | solution.py:270
  20.0 4.4 %collective-permute-done.5 = bf16[4,144,128]{2,1,0:T(8,128)(2,1)S(1)} collective-permute-done((bf16[4,144,128]{2,1,0:T(8,128)(2,1)S(1)}, bf16[4,144,128]{2,1,0:T(8,128)(2,1)S(1)}, u32[]{:S(2)}, u32[]{:S(2)}) %collective-permute-start.5) | collective-permute-done | bytes 147488 | tf_op jit(solution)/shard_map/ppermute | solution.py:270
  24.4 2.4 %collective-permute-start.6 = (bf16[2,144,128]{2,1,0:T(8,128)(2,1)S(1)}, bf16[2,144,128]{2,1,0:T(8,128)(2,1)S(1)}, u32[]{:S(2)}, u32[]{:S(2)}) collective-permute-start(bf16[2,144,128]{2,1,0:T(8,128)(2,1)S(1)} %dynamic-slice_bitcast_fusion.1), channel_id=1, source_target_pairs={{0,8},{4,12},{8,0},{12,4},{16,24},{20,28},{24,16},{28,20},{1,9},{5... | collective-permute-start | bytes 221192 | tf_op jit(solution)/shard_map/ppermute | solution.py:270
  26.8 2.3 %collective-permute-done.6 = bf16[2,144,128]{2,1,0:T(8,128)(2,1)S(1)} collective-permute-done((bf16[2,144,128]{2,1,0:T(8,128)(2,1)S(1)}, bf16[2,144,128]{2,1,0:T(8,128)(2,1)S(1)}, u32[]{:S(2)}, u32[]{:S(2)}) %collective-permute-start.6) | collective-permute-done | bytes 73760 | tf_op jit(solution)/shard_map/ppermute | solution.py:270
  29.2 2.4 %collective-permute-start.7 = (bf16[1,144,128]{2,1,0:T(8,128)(2,1)S(1)}, bf16[1,144,128]{2,1,0:T(8,128)(2,1)S(1)}, u32[]{:S(2)}, u32[]{:S(2)}) collective-permute-start(bf16[1,144,128]{2,1,0:T(8,128)(2,1)S(1)} %constant_dynamic-slice_fusion), channel_id=1, source_target_pairs={{0,16},{4,20},{8,24},{12,28},{16,0},{20,4},{24,8},{28,12},{1,17},{... | collective-permute-start | bytes 110600 | tf_op jit(solution)/shard_map/ppermute | solution.py:270
  31.6 2.5 %collective-permute-done.7 = bf16[1,144,128]{2,1,0:T(8,128)(2,1)S(1)} collective-permute-done((bf16[1,144,128]{2,1,0:T(8,128)(2,1)S(1)}, bf16[1,144,128]{2,1,0:T(8,128)(2,1)S(1)}, u32[]{:S(2)}, u32[]{:S(2)}) %collective-permute-start.7) | collective-permute-done | bytes 36896 | tf_op jit(solution)/shard_map/ppermute | solution.py:270
  34.2 1.6 %collective-permute-start.8 = (bf16[144,128]{1,0:T(8,128)(2,1)S(1)}, bf16[144,128]{1,0:T(8,128)(2,1)S(1)}, u32[]{:S(2)}, u32[]{:S(2)}) collective-permute-start(bf16[144,128]{1,0:T(8,128)(2,1)S(1)} %fusion.2.refs_0_), channel_id=1, source_target_pairs={{0,1},{1,0},{2,3},{3,2},{4,5},{5,4},{6,7},{7,6},{8,9},{9,8},{10,11... | collective-permute-start | bytes 110600 | tf_op jit(solution)/shard_map/ppermute | solution.py:277
  35.8 2.4 %collective-permute-done.8.refs_1_ = bf16[144,128]{1,0:T(8,128)(2,1)S(1)} collective-permute-done((bf16[144,128]{1,0:T(8,128)(2,1)S(1)}, bf16[144,128]{1,0:T(8,128)(2,1)S(1)}, u32[]{:S(2)}, u32[]{:S(2)}) %collective-permute-start.8) | collective-permute-done | bytes 36896 | tf_op jit(solution)/shard_map/ppermute | solution.py:277
  38.2 0.1 shard_map.61
  38.3 0.7 %copy.14 = f32[216,64]{0,1:T(8,128)} copy(f32[216,64]{1,0:T(8,128)S(1)} %get-tuple-element.9) | data formatting | bytes 110592 | tf_op jit(solution)/shard_map/pallas_call | solution.py:32
  39.0 0.7 %copy.13 = f32[108,32]{0,1:T(8,128)} copy(f32[108,32]{1,0:T(8,128)S(1)} %get-tuple-element.8) | data formatting | bytes 27648 | tf_op jit(solution)/shard_map/pallas_call | solution.py:32
  (15 shorter events, 0.2 us)
Async XLA Ops:
  0.6 3.9 %copy-start = (bf16[2,1,2,8,8,256]{5,4,3,2,1,0:T(8,128)(2,1)S(1)}, bf16[2,1,2,8,8,256]{5,4,3,2,1,0:T(8,128)(2,1)}, u32[]{:S(2)}) copy-start(bf16[2,1,2,8,8,256]{5,4,3,2,1,0:T(8,128)(2,1)} %param.4) | copy-start | bytes 393220
  1.4 13.0 %copy-start.1 = (bf16[1728,128]{1,0:T(8,128)(2,1)S(1)}, bf16[1728,128]{1,0:T(8,128)(2,1)}, u32[]{:S(2)}) copy-start(bf16[1728,128]{1,0:T(8,128)(2,1)} %refs_5_.1) | copy-start | bytes 1327108
  1.4 6.0 %collective-permute-start.2 = (bf16[2,1,2,256]{3,2,0,1:T(2,128)(2,1)S(1)}, bf16[2,1,2,256]{3,2,0,1:T(2,128)(2,1)S(1)}, u32[]{:S(2)}, u32[]{:S(2)}) collective-permute-start(bf16[2,1,2,256]{3,2,0,1:T(2,128)(2,1)S(1)} %get-tuple-element.18), channel_id=1, source_target_pairs={{0,8},{4,12},{8,0},{12,4},{16,24},{20,28},{24,16},{28,20},{1,9},{5... | collective-permute-start | bytes 6152 | tf_op jit(solution)/shard_map/ppermute | solution.py:239
  4.5 5.6 %collective-permute-start = (bf16[2,4,8,256]{3,2,1,0:T(8,128)(2,1)S(1)}, bf16[2,4,8,256]{3,2,1,0:T(8,128)(2,1)S(1)}, u32[]{:S(2)}, u32[]{:S(2)}) collective-permute-start(bf16[2,4,8,256]{3,2,1,0:T(8,128)(2,1)S(1)} %get-tuple-element.12), channel_id=1, source_target_pairs={{0,4},{4,0},{8,12},{12,8},{16,20},{20,16},{24,28},{28,24},{1,5},{5... | collective-permute-start | bytes 98312 | tf_op jit(solution)/shard_map/ppermute | solution.py:225
  7.5 5.2 %collective-permute-start.3 = (bf16[1,2,2,256]{3,2,1,0:T(2,128)(2,1)S(1)}, bf16[1,2,2,256]{3,2,1,0:T(2,128)(2,1)S(1)}, u32[]{:S(2)}, u32[]{:S(2)}) collective-permute-start(bf16[1,2,2,256]{3,2,1,0:T(2,128)(2,1)S(1)} %get-tuple-element.16), channel_id=1, source_target_pairs={{0,16},{4,20},{8,24},{12,28},{16,0},{20,4},{24,8},{28,12},{1,17},{... | collective-permute-start | bytes 6152 | tf_op jit(solution)/shard_map/ppermute | solution.py:239
  10.2 4.3 %collective-permute-start.1 = (bf16[3,4,8,256]{3,2,1,0:T(8,128)(2,1)S(1)}, bf16[3,4,8,256]{3,2,1,0:T(8,128)(2,1)S(1)}, u32[]{:S(2)}, u32[]{:S(2)}) collective-permute-start(bf16[3,4,8,256]{3,2,1,0:T(8,128)(2,1)S(1)} %maximum_select_fusion), channel_id=1, source_target_pairs={{0,8},{4,12},{8,16},{12,20},{16,24},{20,28},{1,9},{5,13},{9,17},{1... | collective-permute-start | bytes 147464 | tf_op jit(solution)/shard_map/ppermute | solution.py:231
  16.7 1.6 %collective-permute-start.4 = (bf16[8,144,128]{2,1,0:T(8,128)(2,1)S(1)}, bf16[8,144,128]{2,1,0:T(8,128)(2,1)S(1)}, u32[]{:S(2)}, u32[]{:S(2)}) collective-permute-start(bf16[8,144,128]{2,1,0:T(8,128)(2,1)S(1)} %get-tuple-element.5), channel_id=1, source_target_pairs={{0,2},{2,0},{1,3},{3,1},{4,6},{6,4},{5,7},{7,5},{8,10},{10,8},{9,1... | collective-permute-start | bytes 884744 | tf_op jit(solution)/shard_map/ppermute | solution.py:264
  18.4 6.0 %collective-permute-start.5 = (bf16[4,144,128]{2,1,0:T(8,128)(2,1)S(1)}, bf16[4,144,128]{2,1,0:T(8,128)(2,1)S(1)}, u32[]{:S(2)}, u32[]{:S(2)}) collective-permute-start(bf16[4,144,128]{2,1,0:T(8,128)(2,1)S(1)} %dynamic-slice_bitcast_fusion), channel_id=1, source_target_pairs={{0,4},{4,0},{8,12},{12,8},{16,20},{20,16},{24,28},{28,24},{1,5},{5... | collective-permute-start | bytes 442376 | tf_op jit(solution)/shard_map/ppermute | solution.py:270
  24.4 4.7 %collective-permute-start.6 = (bf16[2,144,128]{2,1,0:T(8,128)(2,1)S(1)}, bf16[2,144,128]{2,1,0:T(8,128)(2,1)S(1)}, u32[]{:S(2)}, u32[]{:S(2)}) collective-permute-start(bf16[2,144,128]{2,1,0:T(8,128)(2,1)S(1)} %dynamic-slice_bitcast_fusion.1), channel_id=1, source_target_pairs={{0,8},{4,12},{8,0},{12,4},{16,24},{20,28},{24,16},{28,20},{1,9},{5... | collective-permute-start | bytes 221192 | tf_op jit(solution)/shard_map/ppermute | solution.py:270
  29.2 4.9 %collective-permute-start.7 = (bf16[1,144,128]{2,1,0:T(8,128)(2,1)S(1)}, bf16[1,144,128]{2,1,0:T(8,128)(2,1)S(1)}, u32[]{:S(2)}, u32[]{:S(2)}) collective-permute-start(bf16[1,144,128]{2,1,0:T(8,128)(2,1)S(1)} %constant_dynamic-slice_fusion), channel_id=1, source_target_pairs={{0,16},{4,20},{8,24},{12,28},{16,0},{20,4},{24,8},{28,12},{1,17},{... | collective-permute-start | bytes 110600 | tf_op jit(solution)/shard_map/ppermute | solution.py:270
  34.2 4.0 %collective-permute-start.8 = (bf16[144,128]{1,0:T(8,128)(2,1)S(1)}, bf16[144,128]{1,0:T(8,128)(2,1)S(1)}, u32[]{:S(2)}, u32[]{:S(2)}) collective-permute-start(bf16[144,128]{1,0:T(8,128)(2,1)S(1)} %fusion.2.refs_0_), channel_id=1, source_target_pairs={{0,1},{1,0},{2,3},{3,2},{4,5},{5,4},{6,7},{7,6},{8,9},{9,8},{10,11... | collective-permute-start | bytes 110600 | tf_op jit(solution)/shard_map/ppermute | solution.py:277

commit v2 on v1

--- a/solution.py
+++ b/solution.py
@@ -35,18 +35,20 @@
         in_specs=[vmem] * len(args),
         out_specs=[vmem] * len(out_shape) if many else vmem,
         scratch_shapes=scratch,
-        compiler_params=pltpu.CompilerParams(vmem_limit_bytes=48 << 20),
+        compiler_params=pltpu.CompilerParams(vmem_limit_bytes=32 << 20),
     )(*args)
 
 
 def banded_body(weight, banded):
     lane = lax.broadcasted_iota(jnp.int32, (CA, 2 * CB), 1)
     zero = jnp.zeros((CA, 2 * CB), F32)
+    turned = weight[...].astype(F32).T
+    turned = jnp.concatenate([turned, turned], axis=1)
     for tap in range(9):
         left, right = [], []
         for kz in range(3):
-            part = weight[pl.ds((3 * tap + kz) * CA, CA), :].astype(F32)
-            both = jnp.concatenate([part, part], axis=1)
+            start = (3 * tap + kz) * CA
+            both = turned[start : start + CA]
             left.append(jnp.where(lane < CB, both, 0.0))
             right.append(jnp.where(lane < CB, 0.0, both))
         for half in range(2):
@@ -168,14 +170,20 @@
     t1[pl.ds(TAPS * CA, t1.shape[0] - TAPS * CA), :] = jnp.zeros((t1.shape[0] - TAPS * CA, 128), F32)
     low2 = lax.broadcasted_iota(jnp.int32, (h2, 128), 1) < CB
     quarter = lax.broadcasted_iota(jnp.int32, (h1, 128), 1) // 32
-    for d in range(spread):
-        a = t2[pl.ds(d * r2, h2), :]
-        b = t2[pl.ds(d * r2 + h2, h2), :]
+
+    def block(ref, d, start, size):
+        even = ref[pl.ds(2 * d * size[0] + start, size[1]), :]
+        odd = ref[pl.ds((2 * d + 1) * size[0] + start, size[1]), :]
+        return jnp.where(first, even, odd)
+
+    for d in range(spread // 2):
+        a = block(t2, d, 0, (r2, h2))
+        b = block(t2, d, h2, (r2, h2))
         keep[d, 0:h2, :] = jnp.where(low2, a, pltpu.roll(b, 64, 1)).astype(BF16)
         send[d, 0:h2, :] = jnp.where(low2, pltpu.roll(a, 64, 1), b).astype(BF16)
         kept, sent = None, None
         for g in range(4):
-            straight = t1[pl.ds(d * r1 + g * h1, h1), :]
+            straight = block(t1, d, g * h1, (r1, h1))
             turn = pltpu.roll(straight, 32, 1)
             k, o = (straight, turn) if g % 2 == 0 else (turn, straight)
             kept = k if g == 0 else jnp.where(quarter == g, k, kept)
@@ -189,18 +197,21 @@
     return round_up(-(-r2 // 2), 16), round_up(-(-r1 // 4), 16)
 
 
-def unpack_body(spread, mine, got, first_out, second_out):
+def unpack_body(spread, mine, got, first_out, second_out, first_buf, second_buf, sems):
     r2, r1 = TAPS * CB // spread, TAPS * CA // spread
     h2, h1 = packed_rows(spread)
     total = mine[...].astype(F32) + got[...].astype(F32)
-    top, rest = total[:h2], total[h2:]
-    second_out[0:h2, :] = top[:, :CB]
-    second_out[pl.ds(h2, r2 - h2), :] = pltpu.roll(top, 64, 1)[: r2 - h2, :CB]
-    for g in range(4):
-        size = min(h1, r1 - g * h1)
-        if size > 0:
-            part = rest if g == 0 else pltpu.roll(rest, 128 - 32 * g, 1)
-            first_out[pl.ds(g * h1, size), :] = part[:size, : CB // 2]
+    top = total[:h2].T
+    second_buf[...] = jnp.concatenate([top[:CB], top[CB:]], axis=1)[:, :r2]
+    second_copy = pltpu.make_async_copy(second_buf, second_out, sems.at[0])
+    second_copy.start()
+    rest = total[h2:].T
+    rest = jnp.concatenate([rest[32 * g : 32 * g + 32] for g in range(4)], axis=1)
+    first_buf[...] = rest[:, :r1]
+    first_copy = pltpu.make_async_copy(first_buf, first_out, sems.at[1])
+    first_copy.start()
+    second_copy.wait()
+    first_copy.wait()
 
 
 def swap_bit(count, bit):
@@ -214,15 +225,28 @@
 def shards(input_field, first_weight, second_weight, upstream_grad):
     micro_count, _, planes, volumes, rows_y, packed = input_field.shape
     spread = lax.axis_size("space")
-    count = volumes // 2
     pairs = spread // 2
     space = lax.axis_index("space")
     section = lax.axis_index("section")
     side, pair = space % 2, space // 2
 
-    own = pick(input_field[:, 0], section, 0).reshape(planes, count, 2, rows_y, packed)
-    mine = pick(own, side, 2)
-    got = lax.ppermute(pick(own, 1 - side, 2), "space", swap_bit(spread, 0))
+    partner = lax.ppermute(upstream_grad, "space", swap_bit(spread, 0))
+    both = jnp.where(
+        side == 0, jnp.stack([upstream_grad, partner], 4), jnp.stack([partner, upstream_grad], 4)
+    )
+    up = pick(both[:, 0, :, 0], section, 0)[:, None]
+    bits = pairs.bit_length() - 1
+    for bit in reversed(range(bits)):
+        up = up.reshape(2, up.shape[0] // 2, *up.shape[1:])
+        here = (pair >> bit) & 1
+        kept = pick(up, here, 0)
+        came = lax.ppermute(pick(up, 1 - here, 0), "space", swap_bit(spread, bit + 1))
+        up = jnp.where(here == 0, jnp.stack([kept, came], 2), jnp.stack([came, kept], 2))
+        up = up.reshape(up.shape[0], -1, *up.shape[3:])
+    up = up.reshape(volumes, *up.shape[-2:])
+
+    mine = pick(input_field[:, 0], section, 0)
+    got = lax.ppermute(mine, "space", swap_bit(spread, 0))
     onward = jnp.where(
         side == 0,
         jnp.stack([mine[1], got[0], got[1]]),
@@ -230,28 +254,16 @@
     )
     before = lax.ppermute(onward, "space", [(i, i + 2) for i in range(spread - 2)])
 
-    up = pick(upstream_grad[:, 0], section, 0)
-    bit = 0
-    while 1 << bit < pairs:
-        up = up.reshape(up.shape[0] // 2, 2, -1, *up.shape[-2:])
-        here = (pair >> bit) & 1
-        kept = pick(up, here, 1)
-        came = lax.ppermute(pick(up, 1 - here, 1), "space", swap_bit(spread, bit + 1))
-        up = jnp.where(here == 0, jnp.stack([kept, came], 1), jnp.stack([came, kept], 1))
-        up = up.reshape(up.shape[0], -1, *up.shape[-2:])
-        bit += 1
-    up = up.reshape(count, *up.shape[-2:])
-
-    banded = call(banded_body, jax.ShapeDtypeStruct((9 * 256, 256), BF16), [], (first_weight,))
+    banded = call(banded_body, jax.ShapeDtypeStruct((9 * 256, 256), BF16), [], (first_weight.T,))
     h2, h1 = packed_rows(spread)
-    block = jax.ShapeDtypeStruct((spread, h2 + h1, 128), BF16)
+    block = jax.ShapeDtypeStruct((pairs, h2 + h1, 128), BF16)
     kept, outgoing = call(
-        lambda *refs: main_body(count, spread, *refs),
+        lambda *refs: main_body(volumes, spread, *refs),
         [block, block],
         [
-            pltpu.VMEM((7, 2, count * 8 + 16, 128), F32),
-            pltpu.VMEM((3, 2, count * 4 + 16, 128), F32),
-            pltpu.VMEM((3, 2, count * 4, 128), F32),
+            pltpu.VMEM((7, 2, volumes * 8 + 16, 128), F32),
+            pltpu.VMEM((3, 2, volumes * 4 + 16, 128), F32),
+            pltpu.VMEM((3, 2, volumes * 4, 128), F32),
             pltpu.VMEM((TAPS * CB + 2 * h2, 128), F32),
             pltpu.VMEM((TAPS * CA + 4 * h1, 128), F32),
         ],
@@ -262,12 +274,12 @@
         return (a.astype(F32) + b.astype(F32)).astype(BF16)
 
     total = added(kept, lax.ppermute(outgoing, "section", swap_bit(2, 0)))
-    bits = spread.bit_length() - 1
     for bit in range(bits):
         paired = total.reshape(total.shape[0] // 2, 2, *total.shape[1:])
-        here = (space >> bit) & 1
+        here = (pair >> bit) & 1
         kept = pick(paired, here, 1)
-        total = added(kept, lax.ppermute(pick(paired, 1 - here, 1), "space", swap_bit(spread, bit)))
+        came = lax.ppermute(pick(paired, 1 - here, 1), "space", swap_bit(spread, bit + 1))
+        total = added(kept, came)
     total = total[0]
     replicas = lax.axis_size("dp")
     bit = 0
@@ -275,17 +287,22 @@
         total = added(total, lax.ppermute(total, "dp", swap_bit(replicas, bit)))
         bit += 1
     came = lax.ppermute(total, "dp", swap_bit(replicas, bit))
-    return tuple(
-        call(
-            lambda *refs: unpack_body(spread, *refs),
-            [
-                jax.ShapeDtypeStruct((TAPS * CA // spread, CB // 2), F32),
-                jax.ShapeDtypeStruct((TAPS * CB // spread, CC // 2), F32),
-            ],
-            [],
-            (total, came),
-        )
-    )
+    first_out = (CB // 2, TAPS * CA // spread)
+    second_out = (CC // 2, TAPS * CB // spread)
+    vmem, hbm = pl.BlockSpec(memory_space=pltpu.VMEM), pl.BlockSpec(memory_space=pl.ANY)
+    first_grad, second_grad = pl.pallas_call(
+        lambda *refs: unpack_body(spread, *refs),
+        out_shape=[jax.ShapeDtypeStruct(first_out, F32), jax.ShapeDtypeStruct(second_out, F32)],
+        in_specs=[vmem, vmem],
+        out_specs=[hbm, hbm],
+        scratch_shapes=[
+            pltpu.VMEM(first_out, F32),
+            pltpu.VMEM(second_out, F32),
+            pltpu.SemaphoreType.DMA((2,)),
+        ],
+        compiler_params=pltpu.CompilerParams(vmem_limit_bytes=16 << 20),
+    )(total, came)
+    return (first_grad.T, second_grad.T)
 
 
 def solution(mesh):

time: 39.9 us -> 37.7 us (0.945)
  waiting for transfers between devices: 14.9 us -> 11.4 us
  Pallas kernels: 2.54 us -> 3.44 us
  other arithmetic: 0.2 us -> 0.92 us
  local copies, waits for them, and re-layouts: 3.3 us -> 2.6 us
    ppermute x6, waiting for transfers between devices: 9.24 us -> 5.46 us  [the longest x2 4.52 us: shards(): lax.ppermute(pick(paired, 1 - here, 1), 'space', swap_bit(spread, bit + 1))]
    pallas_call x2 -> x0, local copies, waits for them, and re-layouts: 1.4 us -> none  [call(): pl.pallas_call(body, out_shape=out_shape, in_specs=[vmem] * len(args), ou...]
    squeeze x3, local copies, waits for them, and re-layouts: 0.05 us -> 0.87 us  [pick(): return lax.dynamic_index_in_dim(array, index, axis, keepdims=False)]
    pallas_call x0 -> x1, Pallas kernels: none -> 0.82 us  [shards(): pl.pallas_call(lambda *refs: unpack_body(spread, *refs), out_shape=[jax.S...]
    select_n x2 -> x3, other arithmetic: 0.03 us -> 0.82 us  [the longest x1 0.78 us: shards(): jnp.where(side == 0, jnp.stack([upstream_grad, partner], 4), jnp.stack([p...]
    slice x1, local copies, waits for them, and re-layouts: 0.01 us -> 0.78 us  [shards(): mine[0]]
    dynamic_slice x3, local copies, waits for them, and re-layouts: 0.74 us -> 0.03 us  [pick(): return lax.dynamic_index_in_dim(array, index, axis, keepdims=False)]
    ppermute x6, starting transfers between devices: 13.7 us -> 14.2 us  [the longest x2 6.32 us: shards(): lax.ppermute(pick(paired, 1 - here, 1), 'space', swap_bit(spread, bit + 1))]
  transfers between devices with their start and end apart: 9 -> 9, of which waited for: 6 -> 6; matrix products, arithmetic and copies ran while one was open for 3% -> 7% of each run, Pallas kernels for 1% -> 1%
where the time goes in v2:
time: 37.7 us; the launch traced here: 37.4 us
  starting transfers between devices  18.2 us (48%)
  waiting for transfers between devices  11.4 us (30%)
  Pallas kernels  3.44 us (9%)
  local copies, waits for them, and re-layouts  2.6 us (7%)
  other arithmetic  0.92 us (2%)
  between operations  0.77 us (2%)
    ppermute x2, starting transfers between devices, shards(): lax.ppermute(pick(paired, 1 - here, 1), 'space', swap_bit(spread, bit + 1))  6.32 us
    ppermute x2, starting transfers between devices, shards(): lax.ppermute(pick(up, 1 - here, 0), 'space', swap_bit(spread, bit + 1))  4.82 us
    ppermute x2, waiting for transfers between devices, shards(): lax.ppermute(pick(paired, 1 - here, 1), 'space', swap_bit(spread, bit + 1))  4.52 us
    ppermute x1, starting transfers between devices, shards(): partner = lax.ppermute(upstream_grad, 'space', swap_bit(spread, 0))  3 us
    pallas_call x2, Pallas kernels, call(): pl.pallas_call(body, out_shape=out_shape, in_specs=[vmem] * len(args), ou...  2.62 us
    ppermute x1, waiting for transfers between devices, shards(): came = lax.ppermute(total, 'dp', swap_bit(replicas, bit))  2.44 us
    ppermute x1, starting transfers between devices, shards(): lax.ppermute(onward, 'space', [(i, i + 2) for i in range(spread - 2)])  2.36 us
    ppermute x1, waiting for transfers between devices, shards(): lax.ppermute(onward, 'space', [(i, i + 2) for i in range(spread - 2)])  2.15 us
  transfers between devices with their start and end apart: 9, of which 6 were waited for; matrix products, arithmetic and copies ran while one was open for 7% of the time, Pallas kernels for 1%

profile of v2, /device:TPU:0, one launch (start us, length us, event | category | flops | bytes accessed | tf_op | source)
XLA Modules:
  0.0 37.4 jit_solution(17547481887269160630)
XLA Ops:
  0.6 0.0 copy-start
  0.6 3.0 %collective-permute-start.2 = (bf16[2,1,4,1,2,256]{5,4,3,2,1,0:T(2,128)(2,1)}, bf16[2,1,4,1,2,256]{5,4,3,2,1,0:T(2,128)(2,1)S(1)}, u32[]{:S(2)}, u32[]{:S(2)}) collective-permute-start(bf16[2,1,4,1,2,256]{5,4,3,2,1,0:T(2,128)(2,1)} %param.7), channel_id=1, source_target_pairs={{0,4},{4,0},{8,12},{12,8},{16,20},{20,16},{24,28},{28,24},{1,5},{5... | collective-permute-start | bytes 24584 | tf_op jit(solution)/shard_map/ppermute | solution.py:233
  3.6 0.8 %dynamic-slice_bitcast_fusion.1.refs_0_ = bf16[2,8,8,256]{3,2,1,0:T(8,128)(2,1)S(1)} fusion(bf16[2,1,2,8,8,256]{5,4,3,2,1,0:T(8,128)(2,1)} %param.4, s32[]{:T(128)S(6)} %select_n.91), kind=kLoop, calls=%fused_computation.6 | loop fusion | bytes 131076 | tf_op jit(solution)/shard_map/jit(dynamic_index_in_dim)/squeeze | solution.py:222
  4.5 0.1 collective-permute-start
  4.5 0.9 %collective-permute-done.2 = bf16[2,1,4,1,2,256]{5,4,3,2,1,0:T(2,128)(2,1)S(1)} collective-permute-done((bf16[2,1,4,1,2,256]{5,4,3,2,1,0:T(2,128)(2,1)}, bf16[2,1,4,1,2,256]{5,4,3,2,1,0:T(2,128)(2,1)S(1)}, u32[]{:S(2)}, u32[]{:S(2)}) %collective-permute-start.2) | collective-permute-done | bytes 8224 | tf_op jit(solution)/shard_map/ppermute | solution.py:233
  5.5 0.8 %broadcast_select_fusion = bf16[1,1,4,1,2,2,256]{6,5,2,0,4,3,1:T(2,128)(2,1)S(1)} fusion(pred[]{:T(512)S(6)} %eq.12, s32[]{:T(128)S(6)} %select_n.91, bf16[2,1,4,1,1,2,256]{6,5,2,0,4,3,1:T(2,128)(2,1)S(1)} %bitcast.42, bf16[2,1,4,1,1,2,256]{6,5,2,0,4,3,1:T(2,128)(2,1)} %bitcast.41), kind=kLoop, calls=%fused_computation.14 | loop fusion | flops 12288 | bytes 24581 | tf_op jit(solution)/shard_map/jit(_where)/select_n | solution.py:234
  6.3 3.2 %collective-permute-start.3 = (bf16[2,1,2,2,256]{4,3,2,0,1:T(2,128)(2,1)S(1)}, bf16[2,1,2,2,256]{4,3,2,0,1:T(2,128)(2,1)S(1)}, u32[]{:S(2)}, u32[]{:S(2)}) collective-permute-start(bf16[2,1,2,2,256]{4,3,2,0,1:T(2,128)(2,1)S(1)} %bitcast.43), channel_id=1, source_target_pairs={{0,16},{4,20},{8,24},{12,28},{16,0},{20,4},{24,8},{28,12},{1,17},{... | collective-permute-start | bytes 12296 | tf_op jit(solution)/shard_map/ppermute | solution.py:243
  9.5 0.8 %dynamic-slice_bitcast_fusion.2 = (bf16[1,8,8,256]{3,2,1,0:T(8,128)(2,1)S(1)}, bf16[1,8,8,256]{3,2,1,0:T(8,128)(2,1)S(1)}) fusion(bf16[2,1,2,8,8,256]{5,4,3,2,1,0:T(8,128)(2,1)} %param.4, s32[]{:T(128)S(6)} %select_n.91, s32[]{:T(128)S(6)} %add.51), kind=kLoop, calls=%fused_computation.8 | loop fusion | bytes 131080 | tf_op jit(solution)/shard_map/slice | solution.py:253
  10.3 0.0 copy-start.1
  10.3 0.9 %copy-done.1 = bf16[864,64]{0,1:T(8,128)(2,1)S(1)} copy-done((bf16[864,64]{0,1:T(8,128)(2,1)S(1)}, bf16[864,64]{0,1:T(8,128)(2,1)}, u32[]{:S(2)}) %copy-start.1) | copy-done | bytes 110616
  11.2 0.3 shard_map.59.refs_4_
  11.5 0.0 collective-permute-done.3
  11.6 1.6 %collective-permute-start.4 = (bf16[1,2,2,2,256]{4,3,2,1,0:T(2,128)(2,1)S(1)}, bf16[1,2,2,2,256]{4,3,2,1,0:T(2,128)(2,1)S(1)}, u32[]{:S(2)}, u32[]{:S(2)}) collective-permute-start(bf16[1,2,2,2,256]{4,3,2,1,0:T(2,128)(2,1)S(1)} %get-tuple-element.13), channel_id=1, source_target_pairs={{0,8},{4,12},{8,0},{12,4},{16,24},{20,28},{24,16},{28,20},{1,9},{5... | collective-permute-start | bytes 12296 | tf_op jit(solution)/shard_map/ppermute | solution.py:243
  13.2 0.0 collective-permute-done.refs_1_
  13.3 2.4 %collective-permute-start.1 = (bf16[3,8,8,256]{3,2,1,0:T(8,128)(2,1)S(1)}, bf16[3,8,8,256]{3,2,1,0:T(8,128)(2,1)S(1)}, u32[]{:S(2)}, u32[]{:S(2)}) collective-permute-start(bf16[3,8,8,256]{3,2,1,0:T(8,128)(2,1)S(1)} %maximum_select_fusion), channel_id=1, source_target_pairs={{0,8},{4,12},{8,16},{12,20},{16,24},{20,28},{1,9},{5,13},{9,17},{1... | collective-permute-start | bytes 294920 | tf_op jit(solution)/shard_map/ppermute | solution.py:255
  15.6 0.0 collective-permute-done.4
  15.7 2.2 %collective-permute-done.1.refs_2_ = bf16[3,8,8,256]{3,2,1,0:T(8,128)(2,1)S(1)} collective-permute-done((bf16[3,8,8,256]{3,2,1,0:T(8,128)(2,1)S(1)}, bf16[3,8,8,256]{3,2,1,0:T(8,128)(2,1)S(1)}, u32[]{:S(2)}, u32[]{:S(2)}) %collective-permute-start.1) | collective-permute-done | bytes 98336 | tf_op jit(solution)/shard_map/ppermute | solution.py:255
  17.8 0.0 copy-done
  17.8 2.3 %shard_map.60 = (bf16[4,144,128]{2,1,0:T(8,128)(2,1)S(1)}, bf16[4,144,128]{2,1,0:T(8,128)(2,1)S(1)}) custom-call(bf16[2,8,8,256]{3,2,1,0:T(8,128)(2,1)S(1)} %dynamic-slice_bitcast_fusion.1.refs_0_, bf16[2,8,8,256]{3,2,1,0:T(8,128)(2,1)S(1)} %collective-permute-done.refs_1_, bf16[3,8,8,256]{3,2,1,0:T(8,128)(2,1)S(1)} %collective-permute-done.1.refs_2_, ...), custom_call_target="tpu_custom_call" | custom-call | tf_op jit(solution)/shard_map/pallas_call | solution.py:32
  20.1 0.1 collective-permute-start.5
  20.2 1.4 %collective-permute-done.5 = bf16[4,144,128]{2,1,0:T(8,128)(2,1)S(1)} collective-permute-done((bf16[4,144,128]{2,1,0:T(8,128)(2,1)S(1)}, bf16[4,144,128]{2,1,0:T(8,128)(2,1)S(1)}, u32[]{:S(2)}, u32[]{:S(2)}) %collective-permute-start.5) | collective-permute-done | bytes 147488 | tf_op jit(solution)/shard_map/ppermute | solution.py:276
  21.6 2.6 %collective-permute-start.6 = (bf16[2,144,128]{2,1,0:T(8,128)(2,1)S(1)}, bf16[2,144,128]{2,1,0:T(8,128)(2,1)S(1)}, u32[]{:S(2)}, u32[]{:S(2)}) collective-permute-start(bf16[2,144,128]{2,1,0:T(8,128)(2,1)S(1)} %dynamic-slice_bitcast_fusion), channel_id=1, source_target_pairs={{0,8},{4,12},{8,0},{12,4},{16,24},{20,28},{24,16},{28,20},{1,9},{5... | collective-permute-start | bytes 221192 | tf_op jit(solution)/shard_map/ppermute | solution.py:281
  24.3 2.6 %collective-permute-done.6 = bf16[2,144,128]{2,1,0:T(8,128)(2,1)S(1)} collective-permute-done((bf16[2,144,128]{2,1,0:T(8,128)(2,1)S(1)}, bf16[2,144,128]{2,1,0:T(8,128)(2,1)S(1)}, u32[]{:S(2)}, u32[]{:S(2)}) %collective-permute-start.6) | collective-permute-done | bytes 73760 | tf_op jit(solution)/shard_map/ppermute | solution.py:281
  26.9 3.7 %collective-permute-start.7 = (bf16[1,144,128]{2,1,0:T(8,128)(2,1)S(1)}, bf16[1,144,128]{2,1,0:T(8,128)(2,1)S(1)}, u32[]{:S(2)}, u32[]{:S(2)}) collective-permute-start(bf16[1,144,128]{2,1,0:T(8,128)(2,1)S(1)} %constant_dynamic-slice_fusion), channel_id=1, source_target_pairs={{0,16},{4,20},{8,24},{12,28},{16,0},{20,4},{24,8},{28,12},{1,17},{... | collective-permute-start | bytes 110600 | tf_op jit(solution)/shard_map/ppermute | solution.py:281
  30.6 1.9 %collective-permute-done.7 = bf16[1,144,128]{2,1,0:T(8,128)(2,1)S(1)} collective-permute-done((bf16[1,144,128]{2,1,0:T(8,128)(2,1)S(1)}, bf16[1,144,128]{2,1,0:T(8,128)(2,1)S(1)}, u32[]{:S(2)}, u32[]{:S(2)}) %collective-permute-start.7) | collective-permute-done | bytes 36896 | tf_op jit(solution)/shard_map/ppermute | solution.py:281
  32.5 1.6 %collective-permute-start.8 = (bf16[144,128]{1,0:T(8,128)(2,1)S(1)}, bf16[144,128]{1,0:T(8,128)(2,1)S(1)}, u32[]{:S(2)}, u32[]{:S(2)}) collective-permute-start(bf16[144,128]{1,0:T(8,128)(2,1)S(1)} %fusion.1.refs_0_), channel_id=1, source_target_pairs={{0,1},{1,0},{2,3},{3,2},{4,5},{5,4},{6,7},{7,6},{8,9},{9,8},{10,11... | collective-permute-start | bytes 110600 | tf_op jit(solution)/shard_map/ppermute | solution.py:289
  34.1 2.4 %collective-permute-done.8.refs_1_ = bf16[144,128]{1,0:T(8,128)(2,1)S(1)} collective-permute-done((bf16[144,128]{1,0:T(8,128)(2,1)S(1)}, bf16[144,128]{1,0:T(8,128)(2,1)S(1)}, u32[]{:S(2)}, u32[]{:S(2)}) %collective-permute-start.8) | collective-permute-done | bytes 36896 | tf_op jit(solution)/shard_map/ppermute | solution.py:289
  36.5 0.8 %shard_map.61 = (f32[32,108]{1,0:T(8,128)}, f32[64,216]{1,0:T(8,128)}) custom-call(bf16[144,128]{1,0:T(8,128)(2,1)S(1)} %fusion.1.refs_0_, bf16[144,128]{1,0:T(8,128)(2,1)S(1)} %collective-permute-done.8.refs_1_), custom_call_target="tpu_custom_call" | custom-call | tf_op jit(solution)/shard_map/pallas_call | solution.py:293
  (13 shorter events, 0.2 us)
Async XLA Ops:
  0.6 17.2 %copy-start = (bf16[1728,128]{1,0:T(8,128)(2,1)S(1)}, bf16[1728,128]{1,0:T(8,128)(2,1)}, u32[]{:S(2)}) copy-start(bf16[1728,128]{1,0:T(8,128)(2,1)} %refs_5_.1) | copy-start | bytes 1327108
  0.6 4.8 %collective-permute-start.2 = (bf16[2,1,4,1,2,256]{5,4,3,2,1,0:T(2,128)(2,1)}, bf16[2,1,4,1,2,256]{5,4,3,2,1,0:T(2,128)(2,1)S(1)}, u32[]{:S(2)}, u32[]{:S(2)}) collective-permute-start(bf16[2,1,4,1,2,256]{5,4,3,2,1,0:T(2,128)(2,1)} %param.7), channel_id=1, source_target_pairs={{0,4},{4,0},{8,12},{12,8},{16,20},{20,16},{24,28},{28,24},{1,5},{5... | collective-permute-start | bytes 24584 | tf_op jit(solution)/shard_map/ppermute | solution.py:233
  4.5 8.7 %collective-permute-start = (bf16[2,8,8,256]{3,2,1,0:T(8,128)(2,1)S(1)}, bf16[2,8,8,256]{3,2,1,0:T(8,128)(2,1)S(1)}, u32[]{:S(2)}, u32[]{:S(2)}) collective-permute-start(bf16[2,8,8,256]{3,2,1,0:T(8,128)(2,1)S(1)} %dynamic-slice_bitcast_fusion.1.refs_0_), channel_id=1, source_target_pairs={{0,4},{4,0},{8,12},{12,8},{16,20},{20,16},{24,28},{28,24},{1,5},{5... | collective-permute-start | bytes 196616 | tf_op jit(solution)/shard_map/ppermute | solution.py:249
  6.3 5.2 %collective-permute-start.3 = (bf16[2,1,2,2,256]{4,3,2,0,1:T(2,128)(2,1)S(1)}, bf16[2,1,2,2,256]{4,3,2,0,1:T(2,128)(2,1)S(1)}, u32[]{:S(2)}, u32[]{:S(2)}) collective-permute-start(bf16[2,1,2,2,256]{4,3,2,0,1:T(2,128)(2,1)S(1)} %bitcast.43), channel_id=1, source_target_pairs={{0,16},{4,20},{8,24},{12,28},{16,0},{20,4},{24,8},{28,12},{1,17},{... | collective-permute-start | bytes 12296 | tf_op jit(solution)/shard_map/ppermute | solution.py:243
  10.3 0.9 %copy-start.1 = (bf16[864,64]{0,1:T(8,128)(2,1)S(1)}, bf16[864,64]{0,1:T(8,128)(2,1)}, u32[]{:S(2)}) copy-start(bf16[864,64]{0,1:T(8,128)(2,1)} %param.5) | copy-start | bytes 331780
  11.6 4.0 %collective-permute-start.4 = (bf16[1,2,2,2,256]{4,3,2,1,0:T(2,128)(2,1)S(1)}, bf16[1,2,2,2,256]{4,3,2,1,0:T(2,128)(2,1)S(1)}, u32[]{:S(2)}, u32[]{:S(2)}) collective-permute-start(bf16[1,2,2,2,256]{4,3,2,1,0:T(2,128)(2,1)S(1)} %get-tuple-element.13), channel_id=1, source_target_pairs={{0,8},{4,12},{8,0},{12,4},{16,24},{20,28},{24,16},{28,20},{1,9},{5... | collective-permute-start | bytes 12296 | tf_op jit(solution)/shard_map/ppermute | solution.py:243
  13.3 4.6 %collective-permute-start.1 = (bf16[3,8,8,256]{3,2,1,0:T(8,128)(2,1)S(1)}, bf16[3,8,8,256]{3,2,1,0:T(8,128)(2,1)S(1)}, u32[]{:S(2)}, u32[]{:S(2)}) collective-permute-start(bf16[3,8,8,256]{3,2,1,0:T(8,128)(2,1)S(1)} %maximum_select_fusion), channel_id=1, source_target_pairs={{0,8},{4,12},{8,16},{12,20},{16,24},{20,28},{1,9},{5,13},{9,17},{1... | collective-permute-start | bytes 294920 | tf_op jit(solution)/shard_map/ppermute | solution.py:255
  20.1 1.4 %collective-permute-start.5 = (bf16[4,144,128]{2,1,0:T(8,128)(2,1)S(1)}, bf16[4,144,128]{2,1,0:T(8,128)(2,1)S(1)}, u32[]{:S(2)}, u32[]{:S(2)}) collective-permute-start(bf16[4,144,128]{2,1,0:T(8,128)(2,1)S(1)} %get-tuple-element.7), channel_id=1, source_target_pairs={{0,2},{2,0},{1,3},{3,1},{4,6},{6,4},{5,7},{7,5},{8,10},{10,8},{9,1... | collective-permute-start | bytes 442376 | tf_op jit(solution)/shard_map/ppermute | solution.py:276
  21.6 5.2 %collective-permute-start.6 = (bf16[2,144,128]{2,1,0:T(8,128)(2,1)S(1)}, bf16[2,144,128]{2,1,0:T(8,128)(2,1)S(1)}, u32[]{:S(2)}, u32[]{:S(2)}) collective-permute-start(bf16[2,144,128]{2,1,0:T(8,128)(2,1)S(1)} %dynamic-slice_bitcast_fusion), channel_id=1, source_target_pairs={{0,8},{4,12},{8,0},{12,4},{16,24},{20,28},{24,16},{28,20},{1,9},{5... | collective-permute-start | bytes 221192 | tf_op jit(solution)/shard_map/ppermute | solution.py:281
  26.9 5.6 %collective-permute-start.7 = (bf16[1,144,128]{2,1,0:T(8,128)(2,1)S(1)}, bf16[1,144,128]{2,1,0:T(8,128)(2,1)S(1)}, u32[]{:S(2)}, u32[]{:S(2)}) collective-permute-start(bf16[1,144,128]{2,1,0:T(8,128)(2,1)S(1)} %constant_dynamic-slice_fusion), channel_id=1, source_target_pairs={{0,16},{4,20},{8,24},{12,28},{16,0},{20,4},{24,8},{28,12},{1,17},{... | collective-permute-start | bytes 110600 | tf_op jit(solution)/shard_map/ppermute | solution.py:281
  32.5 4.0 %collective-permute-start.8 = (bf16[144,128]{1,0:T(8,128)(2,1)S(1)}, bf16[144,128]{1,0:T(8,128)(2,1)S(1)}, u32[]{:S(2)}, u32[]{:S(2)}) collective-permute-start(bf16[144,128]{1,0:T(8,128)(2,1)S(1)} %fusion.1.refs_0_), channel_id=1, source_target_pairs={{0,1},{1,0},{2,3},{3,2},{4,5},{5,4},{6,7},{7,6},{8,9},{9,8},{10,11... | collective-permute-start | bytes 110600 | tf_op jit(solution)/shard_map/ppermute | solution.py:289

commit v3 on v2

--- a/solution.py
+++ b/solution.py
@@ -10,6 +10,7 @@
 CC = 128
 TAPS = 27
 SLOPE = 0.3
+SPAN = 2
 BF16 = jnp.bfloat16
 F32 = jnp.float32
 
@@ -65,52 +66,98 @@
             ).astype(BF16)
 
 
-def main_body(count, spread, mine, got, before, upstream, banded, second, keep, send, xf, hid, hgs, t2, t1):
-    side = lax.axis_index("space") % 2
+def cut_body(span, pairs, field, upstream, *outs):
+    pair = lax.axis_index("space") // 2
     section = lax.axis_index("section")
-    rows = count * 4
-    planes = [before[i] for i in range(3)]
-    own, other = [mine[0], mine[1]], [got[0], got[1]]
-    first = side == 0
-    planes += [jnp.where(first, own[i], other[i]) for i in range(2)]
-    planes += [jnp.where(first, other[i], own[i]) for i in range(2)]
+    width = 2 * span
+
+    def fill(out, k, micro):
+        first = ((pair ^ k) // span) * width
+        for i in range(2):
+            out[pl.ds(i * width, width)] = field[micro, 0, i, pl.ds(first, width)]
+        if k < span:
+            rows = [upstream[micro, 0, p, 0, pl.ds(j, 1), :] for j in range(2) for p in range(pairs)]
+            rows = jnp.concatenate([r.astype(F32) for r in rows], axis=0).astype(BF16)
+            out[pl.ds(2 * width, pairs // 4)] = rows.reshape(pairs // 4, 8, 256)
+
+    fill(outs[0], 0, section)
+    for k in range(1, pairs):
+        for micro in range(2):
+            fill(outs[k].at[micro], k, micro)
+
+
+def main_body(span, pairs, spread, mine, partner, *refs):
+    received = refs[: pairs - 1]
+    swapped, banded, second, keep, send, xf, hid, hgs, us, t2, t1 = refs[pairs - 1 :]
+    space = lax.axis_index("space")
+    side, pair = space % 2, space // 2
+    section = lax.axis_index("section")
+    width = 2 * span
+    tail = pairs // 4
+    base = width * 8 + 8
+    total = 2 * pairs * width * 8
+    for i in range(2):
+        for h in range(2):
+            xf[i, h, 0:base, :] = jnp.zeros((base, 128), F32)
+
+    def place(load, k, at_side):
+        there = pair ^ k
+        start = pl.multiple_of(base + (2 * there + at_side) * (width * 8), 8)
+        for i in range(2):
+            tiles = load(i * width, width).reshape(width * 8, 256).astype(F32)
+            for h in range(2):
+                xf[i, h, pl.ds(start, width * 8), :] = tiles[:, h * 128 : h * 128 + 128]
+        if k < span:
+            rows = load(2 * width, tail).reshape(2 * pairs, 256).astype(F32)
+            volume = 2 * (there % span) + at_side
+            for j in range(2):
+                for h in range(2):
+                    us[h, pl.ds(2 * volume + j, pairs, stride=2 * width), :] = rows[
+                        j * pairs : j * pairs + pairs, h * 128 : h * 128 + 128
+                    ]
+
+    place(lambda at, size: mine[pl.ds(at, size)], 0, side)
+    place(lambda at, size: partner[pl.ds(at, size)], 0, 1 - side)
+    offset = 0
+    for k in range(1, pairs):
+        ref = received[k - 1]
+        place(lambda at, size: ref[section, pl.ds(at, size)], k, side ^ section)
+        start = offset
+        place(lambda at, size: swapped[pl.ds(start + at, size)], k, 1 - (side ^ section))
+        offset += ref.shape[1]
+
+    rows = total // 2
     row = lax.broadcasted_iota(jnp.int32, (rows, 256), 0)
-    tiles = []
-    for i, plane in enumerate(planes):
-        flat = plane.reshape(count * 8, 256).astype(F32)
-        for h in range(2):
-            xf[i, h, 0:8, :] = jnp.zeros((8, 128), F32)
-            xf[i, h, pl.ds(8, count * 8), :] = flat[:, h * 128 : h * 128 + 128]
-        triple = []
+    columns = []
+    for kx in range(3):
         for ky in range(3):
+            start = base + ky - 1 - (width * 8 if kx == 0 else 0)
             part = jnp.concatenate(
-                [xf[i, h, pl.ds(7 + ky, rows, stride=2), :] for h in range(2)], axis=1
+                [xf[0 if kx == 1 else 1, h, pl.ds(start, rows, stride=2), :] for h in range(2)],
+                axis=1,
             )
             if ky == 0:
                 part = jnp.where(row % 4 == 0, 0.0, part)
-            triple.append(part.astype(BF16))
-        tiles.append(triple)
-    columns = [
-        jnp.concatenate([tiles[2 * i + kx][ky] for i in range(3)], axis=0)
-        for kx in range(3)
-        for ky in range(3)
-    ]
+            columns.append(part.astype(BF16))
     preact = jnp.dot(jnp.concatenate(columns, axis=1), banded[...], preferred_element_type=F32)
     hidden = leaky(preact, preact).astype(BF16).astype(F32)
-    half = count * 2
-    lane = lax.broadcasted_iota(jnp.int32, (half, 128), 1)
-    low = lane < CB
+    step = width * 4
+    base2 = step + 8
+    for i in range(2):
+        picked = jnp.concatenate(
+            [hidden[(2 * n + i) * step : (2 * n + i + 1) * step] for n in range(pairs)], axis=0
+        )
+        for h in range(2):
+            hid[i, h, 0:base2, :] = jnp.zeros((base2, 128), F32)
+            hid[i, h, pl.ds(base2, pairs * step), :] = picked[:, h * 128 : h * 128 + 128]
+    half = pairs * width * 2
+    low = lax.broadcasted_iota(jnp.int32, (half, 128), 1) < CB
     row2 = lax.broadcasted_iota(jnp.int32, (half, 128), 0)
     cols = []
     for kx in range(3):
-        for h in range(2):
-            hid[kx, h, 0:8, :] = jnp.zeros((8, 128), F32)
-            hid[kx, h, pl.ds(8, rows), :] = hidden[
-                kx * rows : kx * rows + rows, h * 128 : h * 128 + 128
-            ]
         for ky in range(3):
-            a = hid[kx, 0, pl.ds(7 + ky, half, stride=2), :]
-            b = hid[kx, 1, pl.ds(7 + ky, half, stride=2), :]
+            start = base2 + ky - 1 - (step if kx == 0 else 0)
+            a, b = [hid[0 if kx == 1 else 1, h, pl.ds(start, half, stride=2), :] for h in range(2)]
             if ky == 0:
                 a = jnp.where(row2 % 2 == 0, 0.0, a)
                 b = jnp.where(row2 % 2 == 0, 0.0, b)
@@ -124,34 +171,45 @@
         out = out + jnp.dot(
             cols[tap], second[pl.ds(tap * 192, 192), :], preferred_element_type=F32
         )
-    up = upstream[...].reshape(half, 256).astype(F32)
-    up = jnp.concatenate([up[:, :128], up[:, 128:]], axis=0)
+    up = jnp.concatenate([us[0], us[1]], axis=0)
     delta = leaky(out, up)
     delta_b = delta.astype(BF16)
     turned = jnp.where(section == 0, delta, pltpu.roll(delta, 64, 1)).astype(BF16)
     for tap in range(9):
         t2[pl.ds(tap * 192, 192), :] = contract(cols[tap], turned, 0, 0)
     row3 = lax.broadcasted_iota(jnp.int32, (2 * half, 128), 0)
-    for kx in range(3):
-        parts = []
-        for ky in range(3):
-            base = (3 * kx + ky) * 192
-            c0 = contract(delta_b, second[pl.ds(base, 128), :], 1, 1)
-            c1 = contract(delta_b, second[pl.ds(base + 128, 64), :], 1, 1)
-            parts.append((c0, jnp.concatenate([c1, c1], axis=1)))
-        odd = []
-        for late, early in zip(parts[2], parts[0]):
-            shifted = pltpu.roll(early, 2 * half - 1, 0)
-            odd.append(late + jnp.where(row3 % 2 == 0, shifted, 0.0))
-        for parity, (c0, c1) in enumerate((parts[1], odd)):
+    next_y = row3 % 2 == 0
+    next_x = row3 % half < half - 2 * width
+    grads = []
+    for tap in range(9):
+        c0 = contract(delta_b, second[pl.ds(tap * 192, 128), :], 1, 1)
+        c1 = contract(delta_b, second[pl.ds(tap * 192 + 128, 64), :], 1, 1)
+        grads.append([c0, jnp.concatenate([c1, c1], axis=1)])
+
+    def joined(late, early, distance, valid):
+        return [
+            l + jnp.where(valid, pltpu.roll(e, 2 * half - distance, 0), 0.0)
+            for l, e in zip(late, early)
+        ]
+
+    for i in range(2):
+        if i == 0:
+            over_y = grads[3:6]
+        else:
+            over_y = [joined(grads[6 + ky], grads[ky], 2 * width, next_x) for ky in range(3)]
+        for parity, (c0, c1) in enumerate((over_y[1], joined(over_y[2], over_y[0], 1, next_y))):
             turn = pltpu.roll(c0, 64, 1)
             k0, k1 = turn[:half], turn[half:]
-            a = jnp.where(low, k0, c1[:half] + k1)
-            b = jnp.where(low, k1, c1[half:])
-            hgs[kx, 0, pl.ds(parity, half, stride=2), :] = a
-            hgs[kx, 1, pl.ds(parity, half, stride=2), :] = b
+            hgs[i, 0, pl.ds(parity, half, stride=2), :] = jnp.where(low, k0, c1[:half] + k1)
+            hgs[i, 1, pl.ds(parity, half, stride=2), :] = jnp.where(low, k1, c1[half:])
     hidden_grad = jnp.concatenate(
-        [jnp.concatenate([hgs[kx, h] for kx in range(3)], axis=0) for h in range(2)], axis=1
+        [
+            jnp.concatenate(
+                [hgs[n % 2, h, pl.ds(n // 2 * step, step), :] for n in range(2 * pairs)], axis=0
+            )
+            for h in range(2)
+        ],
+        axis=1,
     )
     hidden_grad = hidden_grad.astype(BF16).astype(F32)
     delta_a = leaky(hidden, hidden_grad).astype(BF16)
@@ -170,26 +228,29 @@
     t1[pl.ds(TAPS * CA, t1.shape[0] - TAPS * CA), :] = jnp.zeros((t1.shape[0] - TAPS * CA, 128), F32)
     low2 = lax.broadcasted_iota(jnp.int32, (h2, 128), 1) < CB
     quarter = lax.broadcasted_iota(jnp.int32, (h1, 128), 1) // 32
-
-    def block(ref, d, start, size):
-        even = ref[pl.ds(2 * d * size[0] + start, size[1]), :]
-        odd = ref[pl.ds((2 * d + 1) * size[0] + start, size[1]), :]
-        return jnp.where(first, even, odd)
-
-    for d in range(spread // 2):
-        a = block(t2, d, 0, (r2, h2))
-        b = block(t2, d, h2, (r2, h2))
-        keep[d, 0:h2, :] = jnp.where(low2, a, pltpu.roll(b, 64, 1)).astype(BF16)
-        send[d, 0:h2, :] = jnp.where(low2, pltpu.roll(a, 64, 1), b).astype(BF16)
+    within = space % width
+
+    def block(ref, n, stride, start, size):
+        found = ref[pl.ds(n * width * stride + start, size), :]
+        for other in range(1, width):
+            more = ref[pl.ds((n * width + other) * stride + start, size), :]
+            found = jnp.where(within == other, more, found)
+        return found
+
+    for n in range(pairs // span):
+        a = block(t2, n, r2, 0, h2)
+        b = block(t2, n, r2, h2, h2)
+        keep[n, 0:h2, :] = jnp.where(low2, a, pltpu.roll(b, 64, 1)).astype(BF16)
+        send[n, 0:h2, :] = jnp.where(low2, pltpu.roll(a, 64, 1), b).astype(BF16)
         kept, sent = None, None
         for g in range(4):
-            straight = block(t1, d, g * h1, (r1, h1))
+            straight = block(t1, n, r1, g * h1, h1)
             turn = pltpu.roll(straight, 32, 1)
             k, o = (straight, turn) if g % 2 == 0 else (turn, straight)
             kept = k if g == 0 else jnp.where(quarter == g, k, kept)
             sent = o if g == 0 else jnp.where(quarter == g, o, sent)
-        keep[d, h2 : h2 + h1, :] = kept.astype(BF16)
-        send[d, h2 : h2 + h1, :] = sent.astype(BF16)
+        keep[n, h2 : h2 + h1, :] = kept.astype(BF16)
+        send[n, h2 : h2 + h1, :] = sent.astype(BF16)
 
 
 def packed_rows(spread):
@@ -223,63 +284,62 @@
 
 
 def shards(input_field, first_weight, second_weight, upstream_grad):
-    micro_count, _, planes, volumes, rows_y, packed = input_field.shape
     spread = lax.axis_size("space")
     pairs = spread // 2
-    space = lax.axis_index("space")
+    span = SPAN
+    width = 2 * span
+    tail = pairs // 4
+    pair = lax.axis_index("space") // 2
     section = lax.axis_index("section")
-    side, pair = space % 2, space // 2
-
-    partner = lax.ppermute(upstream_grad, "space", swap_bit(spread, 0))
-    both = jnp.where(
-        side == 0, jnp.stack([upstream_grad, partner], 4), jnp.stack([partner, upstream_grad], 4)
-    )
-    up = pick(both[:, 0, :, 0], section, 0)[:, None]
-    bits = pairs.bit_length() - 1
-    for bit in reversed(range(bits)):
-        up = up.reshape(2, up.shape[0] // 2, *up.shape[1:])
-        here = (pair >> bit) & 1
-        kept = pick(up, here, 0)
-        came = lax.ppermute(pick(up, 1 - here, 0), "space", swap_bit(spread, bit + 1))
-        up = jnp.where(here == 0, jnp.stack([kept, came], 2), jnp.stack([came, kept], 2))
-        up = up.reshape(up.shape[0], -1, *up.shape[3:])
-    up = up.reshape(volumes, *up.shape[-2:])
-
-    mine = pick(input_field[:, 0], section, 0)
-    got = lax.ppermute(mine, "space", swap_bit(spread, 0))
-    onward = jnp.where(
-        side == 0,
-        jnp.stack([mine[1], got[0], got[1]]),
-        jnp.stack([got[1], mine[0], mine[1]]),
-    )
-    before = lax.ppermute(onward, "space", [(i, i + 2) for i in range(spread - 2)])
+
+    piece = lambda k: 2 * width + (tail if k < span else 0)
+    mine, *outgoing = call(
+        lambda *refs: cut_body(span, pairs, *refs),
+        [jax.ShapeDtypeStruct((piece(0), 8, 256), BF16)]
+        + [jax.ShapeDtypeStruct((2, piece(k), 8, 256), BF16) for k in range(1, pairs)],
+        [],
+        (input_field, upstream_grad),
+    )
+    received = [None] * (pairs - 1)
+    for k in sorted(range(1, pairs), key=lambda k: (k != 2, -k)):
+        route = [(2 * d + c, 2 * (d ^ (2 * k) ^ c) + c) for d in range(spread) for c in range(2)]
+        received[k - 1] = lax.ppermute(outgoing[k - 1], ("space", "section"), route)
+    partner = lax.ppermute(mine, "space", swap_bit(spread, 0))
+    swapped = lax.ppermute(
+        jnp.concatenate([pick(block, 1 - section, 0) for block in received]),
+        "section",
+        swap_bit(2, 0),
+    )
 
     banded = call(banded_body, jax.ShapeDtypeStruct((9 * 256, 256), BF16), [], (first_weight.T,))
     h2, h1 = packed_rows(spread)
-    block = jax.ShapeDtypeStruct((pairs, h2 + h1, 128), BF16)
+    block = jax.ShapeDtypeStruct((pairs // span, h2 + h1, 128), BF16)
     kept, outgoing = call(
-        lambda *refs: main_body(volumes, spread, *refs),
+        lambda *refs: main_body(span, pairs, spread, *refs),
         [block, block],
         [
-            pltpu.VMEM((7, 2, volumes * 8 + 16, 128), F32),
-            pltpu.VMEM((3, 2, volumes * 4 + 16, 128), F32),
-            pltpu.VMEM((3, 2, volumes * 4, 128), F32),
+            pltpu.VMEM((2, 2, (2 * pairs + 1) * width * 8 + 16, 128), F32),
+            pltpu.VMEM((2, 2, (pairs + 1) * width * 4 + 16, 128), F32),
+            pltpu.VMEM((2, 2, pairs * width * 4, 128), F32),
+            pltpu.VMEM((2, pairs * width * 2, 128), F32),
             pltpu.VMEM((TAPS * CB + 2 * h2, 128), F32),
             pltpu.VMEM((TAPS * CA + 4 * h1, 128), F32),
         ],
-        (mine, got, before, up, banded, second_weight),
+        (mine, partner, *received, swapped, banded, second_weight),
     )
 
     def added(a, b):
         return (a.astype(F32) + b.astype(F32)).astype(BF16)
 
     total = added(kept, lax.ppermute(outgoing, "section", swap_bit(2, 0)))
-    for bit in range(bits):
+    bit = span.bit_length() - 1
+    while total.shape[0] > 1:
         paired = total.reshape(total.shape[0] // 2, 2, *total.shape[1:])
         here = (pair >> bit) & 1
         kept = pick(paired, here, 1)
         came = lax.ppermute(pick(paired, 1 - here, 1), "space", swap_bit(spread, bit + 1))
         total = added(kept, came)
+        bit += 1
     total = total[0]
     replicas = lax.axis_size("dp")
     bit = 0

time: 37.7 us -> 32 us (0.85)
  starting transfers between devices: 18.2 us -> 12.1 us
  waiting for transfers between devices: 11.4 us -> 12.9 us
  other arithmetic: 0.92 us -> 0.05 us
    ppermute x2 -> x1, starting transfers between devices: 6.32 us -> 2.3 us  [shards(): lax.ppermute(pick(paired, 1 - here, 1), 'space', swap_bit(spread, bit + 1))]
    ppermute x5, waiting for transfers between devices: 3.1 us -> 6.22 us  [the longest x3 5.38 us: shards(): received[k - 1] = lax.ppermute(outgoing[k - 1], ('space', 'section'), route)]
    ppermute x5, starting transfers between devices: 10.2 us -> 8.17 us  [the longest x3 5.75 us: shards(): received[k - 1] = lax.ppermute(outgoing[k - 1], ('space', 'section'), route)]
    unnamed x4 -> x8, local copies, waits for them, and re-layouts: 0.9 us -> 2.5 us
    ppermute x2 -> x1, waiting for transfers between devices: 4.52 us -> 2.99 us  [shards(): lax.ppermute(pick(paired, 1 - here, 1), 'space', swap_bit(spread, bit + 1))]
    squeeze x3 -> x4, local copies, waits for them, and re-layouts: 0.87 us -> 0.02 us  [pick(): return lax.dynamic_index_in_dim(array, index, axis, keepdims=False)]
    select_n x4 -> x0, other arithmetic: 0.84 us -> none  [the longest x1 0.78 us: shards(): jnp.where(side == 0, jnp.stack([upstream_grad, partner], 4), jnp.stack([p...]
    slice x2 -> x0, local copies, waits for them, and re-layouts: 0.78 us -> none  [the longest x1 0.78 us: shards(): mine[0]]
  transfers between devices with their start and end apart: 9 -> 8, of which waited for: 6 -> 7; matrix products, arithmetic and copies ran while one was open for 7% -> 0% of each run, Pallas kernels for 1% -> 1%
where the time goes in v3:
time: 32 us; the launch traced here: 31.8 us
  waiting for transfers between devices  12.9 us (40%)
  starting transfers between devices  12.1 us (38%)
  Pallas kernels  3.45 us (11%)
  local copies, waits for them, and re-layouts  2.52 us (8%)
  between operations  0.71 us (2%)
    ppermute x3, starting transfers between devices, shards(): received[k - 1] = lax.ppermute(outgoing[k - 1], ('space', 'section'), route)  5.75 us
    ppermute x3, waiting for transfers between devices, shards(): received[k - 1] = lax.ppermute(outgoing[k - 1], ('space', 'section'), route)  5.38 us
    ppermute x1, waiting for transfers between devices, shards(): lax.ppermute(pick(paired, 1 - here, 1), 'space', swap_bit(spread, bit + 1))  2.99 us
    pallas_call x3, Pallas kernels, call(): pl.pallas_call(body, out_shape=out_shape, in_specs=[vmem] * len(args), ou...  2.63 us
    unnamed x8, local copies, waits for them, and re-layouts  2.5 us
    ppermute x1, waiting for transfers between devices, shards(): came = lax.ppermute(total, 'dp', swap_bit(replicas, bit))  2.44 us
    ppermute x1, starting transfers between devices, shards(): lax.ppermute(pick(paired, 1 - here, 1), 'space', swap_bit(spread, bit + 1))  2.3 us
    ppermute x1, starting transfers between devices, shards(): partner = lax.ppermute(mine, 'space', swap_bit(spread, 0))  2.26 us
  transfers between devices with their start and end apart: 8, of which 7 were waited for; matrix products, arithmetic and copies ran while one was open for 0% of the time, Pallas kernels for 1%

profile of v3, /device:TPU:0, one launch (start us, length us, event | category | flops | bytes accessed | tf_op | source)
XLA Modules:
  0.0 31.8 jit_solution(16635286545772628385)
XLA Ops:
  0.6 0.0 copy-start.1
  0.6 0.9 %copy-done.1 = bf16[2,1,2,8,8,256]{5,4,3,2,1,0:T(8,128)(2,1)S(1)} copy-done((bf16[2,1,2,8,8,256]{5,4,3,2,1,0:T(8,128)(2,1)S(1)}, bf16[2,1,2,8,8,256]{5,4,3,2,1,0:T(8,128)(2,1)}, u32[]{:S(2)}) %copy-start.1) | copy-done | bytes 131096
  1.5 0.0 copy-start.3
  1.5 0.7 %copy-done.3 = bf16[2,1,4,1,2,256]{5,4,3,2,1,0:T(2,128)(2,1)S(1)} copy-done((bf16[2,1,4,1,2,256]{5,4,3,2,1,0:T(2,128)(2,1)S(1)}, bf16[2,1,4,1,2,256]{5,4,3,2,1,0:T(2,128)(2,1)}, u32[]{:S(2)}) %copy-start.3) | copy-done | bytes 8216
  2.2 0.0 copy-start
  2.3 5.1 %collective-permute-start.3 = (bf16[2,8,8,256]{3,2,1,0:T(8,128)(2,1)S(1)}, bf16[2,8,8,256]{3,2,1,0:T(8,128)(2,1)S(1)}, u32[]{:S(2)}, u32[]{:S(2)}) collective-permute-start(bf16[2,8,8,256]{3,2,1,0:T(8,128)(2,1)S(1)} %get-tuple-element.13), channel_id=1, source_target_pairs={{0,24},{2,30},{4,28},{6,26},{8,16},{10,22},{12,20},{14,18},{16,8},... | collective-permute-start | bytes 196616 | tf_op jit(solution)/shard_map/ppermute | solution.py:306
  7.4 0.0 collective-permute-start.1
  7.4 0.6 %collective-permute-start.2 = (bf16[2,8,8,256]{3,2,1,0:T(8,128)(2,1)S(1)}, bf16[2,8,8,256]{3,2,1,0:T(8,128)(2,1)S(1)}, u32[]{:S(2)}, u32[]{:S(2)}) collective-permute-start(bf16[2,8,8,256]{3,2,1,0:T(8,128)(2,1)S(1)} %get-tuple-element.12), channel_id=1, source_target_pairs={{0,16},{2,22},{4,20},{6,18},{8,24},{10,30},{12,28},{14,26},{16,0},... | collective-permute-start | bytes 196616 | tf_op jit(solution)/shard_map/ppermute | solution.py:306
  8.0 2.4 %collective-permute-done.3.refs_4_ = bf16[2,8,8,256]{3,2,1,0:T(8,128)(2,1)S(1)} collective-permute-done((bf16[2,8,8,256]{3,2,1,0:T(8,128)(2,1)S(1)}, bf16[2,8,8,256]{3,2,1,0:T(8,128)(2,1)S(1)}, u32[]{:S(2)}, u32[]{:S(2)}) %collective-permute-start.3) | collective-permute-done | bytes 65568 | tf_op jit(solution)/shard_map/ppermute | solution.py:306
  10.4 2.6 %collective-permute-done.2.refs_3_ = bf16[2,8,8,256]{3,2,1,0:T(8,128)(2,1)S(1)} collective-permute-done((bf16[2,8,8,256]{3,2,1,0:T(8,128)(2,1)S(1)}, bf16[2,8,8,256]{3,2,1,0:T(8,128)(2,1)S(1)}, u32[]{:S(2)}, u32[]{:S(2)}) %collective-permute-start.2) | collective-permute-done | bytes 65568 | tf_op jit(solution)/shard_map/ppermute | solution.py:306
  13.1 0.4 %collective-permute-done.1.refs_2_ = bf16[2,9,8,256]{3,2,1,0:T(8,128)(2,1)S(1)} collective-permute-done((bf16[2,9,8,256]{3,2,1,0:T(8,128)(2,1)S(1)}, bf16[2,9,8,256]{3,2,1,0:T(8,128)(2,1)S(1)}, u32[]{:S(2)}, u32[]{:S(2)}) %collective-permute-start.1) | collective-permute-done | bytes 73760 | tf_op jit(solution)/shard_map/ppermute | solution.py:306
  13.5 0.2 collective-permute-start.4
  13.6 2.3 %collective-permute-start = (bf16[9,8,256]{2,1,0:T(8,128)(2,1)S(1)}, bf16[9,8,256]{2,1,0:T(8,128)(2,1)S(1)}, u32[]{:S(2)}, u32[]{:S(2)}) collective-permute-start(bf16[9,8,256]{2,1,0:T(8,128)(2,1)S(1)} %get-tuple-element.10.refs_0_), channel_id=1, source_target_pairs={{0,4},{4,0},{8,12},{12,8},{16,20},{20,16},{24,28},{28,24},{1,5},{5... | collective-permute-start | bytes 110600 | tf_op jit(solution)/shard_map/ppermute | solution.py:307
  15.9 0.0 copy-start.2
  15.9 0.9 %copy-done.2 = bf16[864,64]{0,1:T(8,128)(2,1)S(1)} copy-done((bf16[864,64]{0,1:T(8,128)(2,1)S(1)}, bf16[864,64]{0,1:T(8,128)(2,1)}, u32[]{:S(2)}) %copy-start.2) | copy-done | bytes 110616
  16.8 0.3 %shard_map.60.refs_6_ = bf16[2304,256]{1,0:T(8,128)(2,1)S(1)} custom-call(bf16[64,864]{1,0:T(8,128)(2,1)S(1)} %bitcast.11), custom_call_target="tpu_custom_call" | custom-call | tf_op jit(solution)/shard_map/pallas_call | solution.py:33
  17.1 0.8 %collective-permute-done.refs_1_ = bf16[9,8,256]{2,1,0:T(8,128)(2,1)S(1)} collective-permute-done((bf16[9,8,256]{2,1,0:T(8,128)(2,1)S(1)}, bf16[9,8,256]{2,1,0:T(8,128)(2,1)S(1)}, u32[]{:S(2)}, u32[]{:S(2)}) %collective-permute-start) | collective-permute-done | bytes 36896 | tf_op jit(solution)/shard_map/ppermute | solution.py:307
  17.9 0.0 collective-permute-done.4.refs_5_
  17.9 0.0 copy-done
  17.9 2.3 %shard_map.61 = (bf16[2,144,128]{2,1,0:T(8,128)(2,1)S(1)}, bf16[2,144,128]{2,1,0:T(8,128)(2,1)S(1)}) custom-call(bf16[9,8,256]{2,1,0:T(8,128)(2,1)S(1)} %get-tuple-element.10.refs_0_, bf16[9,8,256]{2,1,0:T(8,128)(2,1)S(1)} %collective-permute-done.refs_1_, bf16[2,9,8,256]{3,2,1,0:T(8,128)(2,1)S(1)} %collective-permute-done.1.refs_2_, ...), custom_call_target="tpu_custom_call" | custom-call | tf_op jit(solution)/shard_map/pallas_call | solution.py:33
  20.2 0.1 collective-permute-start.5
  20.3 1.2 %collective-permute-done.5 = bf16[2,144,128]{2,1,0:T(8,128)(2,1)S(1)} collective-permute-done((bf16[2,144,128]{2,1,0:T(8,128)(2,1)S(1)}, bf16[2,144,128]{2,1,0:T(8,128)(2,1)S(1)}, u32[]{:S(2)}, u32[]{:S(2)}) %collective-permute-start.5) | collective-permute-done | bytes 73760 | tf_op jit(solution)/shard_map/ppermute | solution.py:334
  21.6 2.3 %collective-permute-start.6 = (bf16[1,144,128]{2,1,0:T(8,128)(2,1)S(1)}, bf16[1,144,128]{2,1,0:T(8,128)(2,1)S(1)}, u32[]{:S(2)}, u32[]{:S(2)}) collective-permute-start(bf16[1,144,128]{2,1,0:T(8,128)(2,1)S(1)} %constant_dynamic-slice_fusion), channel_id=1, source_target_pairs={{0,16},{4,20},{8,24},{12,28},{16,0},{20,4},{24,8},{28,12},{1,17},{... | collective-permute-start | bytes 110600 | tf_op jit(solution)/shard_map/ppermute | solution.py:340
  23.9 3.0 %collective-permute-done.6 = bf16[1,144,128]{2,1,0:T(8,128)(2,1)S(1)} collective-permute-done((bf16[1,144,128]{2,1,0:T(8,128)(2,1)S(1)}, bf16[1,144,128]{2,1,0:T(8,128)(2,1)S(1)}, u32[]{:S(2)}, u32[]{:S(2)}) %collective-permute-start.6) | collective-permute-done | bytes 36896 | tf_op jit(solution)/shard_map/ppermute | solution.py:340
  26.9 1.6 %collective-permute-start.7 = (bf16[144,128]{1,0:T(8,128)(2,1)S(1)}, bf16[144,128]{1,0:T(8,128)(2,1)S(1)}, u32[]{:S(2)}, u32[]{:S(2)}) collective-permute-start(bf16[144,128]{1,0:T(8,128)(2,1)S(1)} %fusion.refs_0_), channel_id=1, source_target_pairs={{0,1},{1,0},{2,3},{3,2},{4,5},{5,4},{6,7},{7,6},{8,9},{9,8},{10,11... | collective-permute-start | bytes 110600 | tf_op jit(solution)/shard_map/ppermute | solution.py:349
  28.5 2.4 %collective-permute-done.7.refs_1_ = bf16[144,128]{1,0:T(8,128)(2,1)S(1)} collective-permute-done((bf16[144,128]{1,0:T(8,128)(2,1)S(1)}, bf16[144,128]{1,0:T(8,128)(2,1)S(1)}, u32[]{:S(2)}, u32[]{:S(2)}) %collective-permute-start.7) | collective-permute-done | bytes 36896 | tf_op jit(solution)/shard_map/ppermute | solution.py:349
  30.9 0.8 %shard_map.62 = (f32[32,108]{1,0:T(8,128)}, f32[64,216]{1,0:T(8,128)}) custom-call(bf16[144,128]{1,0:T(8,128)(2,1)S(1)} %fusion.refs_0_, bf16[144,128]{1,0:T(8,128)(2,1)S(1)} %collective-permute-done.7.refs_1_), custom_call_target="tpu_custom_call" | custom-call | tf_op jit(solution)/shard_map/pallas_call | solution.py:353
  (8 shorter events, 0.1 us)
Async XLA Ops:
  0.6 0.9 %copy-start.1 = (bf16[2,1,2,8,8,256]{5,4,3,2,1,0:T(8,128)(2,1)S(1)}, bf16[2,1,2,8,8,256]{5,4,3,2,1,0:T(8,128)(2,1)}, u32[]{:S(2)}) copy-start(bf16[2,1,2,8,8,256]{5,4,3,2,1,0:T(8,128)(2,1)} %refs_0_.1) | copy-start | bytes 393220
  1.5 0.7 %copy-start.3 = (bf16[2,1,4,1,2,256]{5,4,3,2,1,0:T(2,128)(2,1)S(1)}, bf16[2,1,4,1,2,256]{5,4,3,2,1,0:T(2,128)(2,1)}, u32[]{:S(2)}) copy-start(bf16[2,1,4,1,2,256]{5,4,3,2,1,0:T(2,128)(2,1)} %refs_1_.1) | copy-start | bytes 24580
  2.2 15.7 %copy-start = (bf16[1728,128]{1,0:T(8,128)(2,1)S(1)}, bf16[1728,128]{1,0:T(8,128)(2,1)}, u32[]{:S(2)}) copy-start(bf16[1728,128]{1,0:T(8,128)(2,1)} %refs_7_.1) | copy-start | bytes 1327108
  2.3 8.2 %collective-permute-start.3 = (bf16[2,8,8,256]{3,2,1,0:T(8,128)(2,1)S(1)}, bf16[2,8,8,256]{3,2,1,0:T(8,128)(2,1)S(1)}, u32[]{:S(2)}, u32[]{:S(2)}) collective-permute-start(bf16[2,8,8,256]{3,2,1,0:T(8,128)(2,1)S(1)} %get-tuple-element.13), channel_id=1, source_target_pairs={{0,24},{2,30},{4,28},{6,26},{8,16},{10,22},{12,20},{14,18},{16,8},... | collective-permute-start | bytes 196616 | tf_op jit(solution)/shard_map/ppermute | solution.py:306
  7.4 6.0 %collective-permute-start.1 = (bf16[2,9,8,256]{3,2,1,0:T(8,128)(2,1)S(1)}, bf16[2,9,8,256]{3,2,1,0:T(8,128)(2,1)S(1)}, u32[]{:S(2)}, u32[]{:S(2)}) collective-permute-start(bf16[2,9,8,256]{3,2,1,0:T(8,128)(2,1)S(1)} %get-tuple-element.11), channel_id=1, source_target_pairs={{0,8},{2,14},{4,12},{6,10},{8,0},{10,6},{12,4},{14,2},{16,24},{18,... | collective-permute-start | bytes 221192 | tf_op jit(solution)/shard_map/ppermute | solution.py:306
  7.4 5.7 %collective-permute-start.2 = (bf16[2,8,8,256]{3,2,1,0:T(8,128)(2,1)S(1)}, bf16[2,8,8,256]{3,2,1,0:T(8,128)(2,1)S(1)}, u32[]{:S(2)}, u32[]{:S(2)}) collective-permute-start(bf16[2,8,8,256]{3,2,1,0:T(8,128)(2,1)S(1)} %get-tuple-element.12), channel_id=1, source_target_pairs={{0,16},{2,22},{4,20},{6,18},{8,24},{10,30},{12,28},{14,26},{16,0},... | collective-permute-start | bytes 196616 | tf_op jit(solution)/shard_map/ppermute | solution.py:306
  13.5 4.5 %collective-permute-start.4 = (bf16[25,8,256]{2,1,0:T(8,128)(2,1)S(1)}, bf16[25,8,256]{2,1,0:T(8,128)(2,1)S(1)}, u32[]{:S(2)}, u32[]{:S(2)}) collective-permute-start(bf16[25,8,256]{2,1,0:T(8,128)(2,1)S(1)} %pad_maximum_fusion), channel_id=1, source_target_pairs={{0,2},{2,0},{1,3},{3,1},{4,6},{6,4},{5,7},{7,5},{8,10},{10,8},{9,1... | collective-permute-start | bytes 307208 | tf_op jit(solution)/shard_map/ppermute | solution.py:308
  13.6 4.3 %collective-permute-start = (bf16[9,8,256]{2,1,0:T(8,128)(2,1)S(1)}, bf16[9,8,256]{2,1,0:T(8,128)(2,1)S(1)}, u32[]{:S(2)}, u32[]{:S(2)}) collective-permute-start(bf16[9,8,256]{2,1,0:T(8,128)(2,1)S(1)} %get-tuple-element.10.refs_0_), channel_id=1, source_target_pairs={{0,4},{4,0},{8,12},{12,8},{16,20},{20,16},{24,28},{28,24},{1,5},{5... | collective-permute-start | bytes 110600 | tf_op jit(solution)/shard_map/ppermute | solution.py:307
  15.9 0.9 %copy-start.2 = (bf16[864,64]{0,1:T(8,128)(2,1)S(1)}, bf16[864,64]{0,1:T(8,128)(2,1)}, u32[]{:S(2)}) copy-start(bf16[864,64]{0,1:T(8,128)(2,1)} %param.5) | copy-start | bytes 331780
  20.2 1.3 %collective-permute-start.5 = (bf16[2,144,128]{2,1,0:T(8,128)(2,1)S(1)}, bf16[2,144,128]{2,1,0:T(8,128)(2,1)S(1)}, u32[]{:S(2)}, u32[]{:S(2)}) collective-permute-start(bf16[2,144,128]{2,1,0:T(8,128)(2,1)S(1)} %get-tuple-element.15), channel_id=1, source_target_pairs={{0,2},{2,0},{1,3},{3,1},{4,6},{6,4},{5,7},{7,5},{8,10},{10,8},{9,1... | collective-permute-start | bytes 221192 | tf_op jit(solution)/shard_map/ppermute | solution.py:334
  21.6 5.3 %collective-permute-start.6 = (bf16[1,144,128]{2,1,0:T(8,128)(2,1)S(1)}, bf16[1,144,128]{2,1,0:T(8,128)(2,1)S(1)}, u32[]{:S(2)}, u32[]{:S(2)}) collective-permute-start(bf16[1,144,128]{2,1,0:T(8,128)(2,1)S(1)} %constant_dynamic-slice_fusion), channel_id=1, source_target_pairs={{0,16},{4,20},{8,24},{12,28},{16,0},{20,4},{24,8},{28,12},{1,17},{... | collective-permute-start | bytes 110600 | tf_op jit(solution)/shard_map/ppermute | solution.py:340
  26.9 4.0 %collective-permute-start.7 = (bf16[144,128]{1,0:T(8,128)(2,1)S(1)}, bf16[144,128]{1,0:T(8,128)(2,1)S(1)}, u32[]{:S(2)}, u32[]{:S(2)}) collective-permute-start(bf16[144,128]{1,0:T(8,128)(2,1)S(1)} %fusion.refs_0_), channel_id=1, source_target_pairs={{0,1},{1,0},{2,3},{3,2},{4,5},{5,4},{6,7},{7,6},{8,9},{9,8},{10,11... | collective-permute-start | bytes 110600 | tf_op jit(solution)/shard_map/ppermute | solution.py:349

commit v4 on v3

--- a/solution.py
+++ b/solution.py
@@ -27,13 +27,13 @@
     return lax.dot_general(a, b, (((dim_a,), (dim_b,)), ((), ())), preferred_element_type=F32)
 
 
-def call(body, out_shape, scratch, args):
-    vmem = pl.BlockSpec(memory_space=pltpu.VMEM)
+def call(body, out_shape, scratch, args, in_hbm=0):
+    vmem, hbm = pl.BlockSpec(memory_space=pltpu.VMEM), pl.BlockSpec(memory_space=pl.ANY)
     many = isinstance(out_shape, (list, tuple))
     return pl.pallas_call(
         body,
         out_shape=out_shape,
-        in_specs=[vmem] * len(args),
+        in_specs=[vmem] * (len(args) - in_hbm) + [hbm] * in_hbm,
         out_specs=[vmem] * len(out_shape) if many else vmem,
         scratch_shapes=scratch,
         compiler_params=pltpu.CompilerParams(vmem_limit_bytes=32 << 20),
@@ -66,7 +66,7 @@
             ).astype(BF16)
 
 
-def cut_body(span, pairs, field, upstream, *outs):
+def cut_body(span, pairs, offsets, field, *refs):
     pair = lax.axis_index("space") // 2
     section = lax.axis_index("section")
     width = 2 * span
@@ -76,19 +76,25 @@
         for i in range(2):
             out[pl.ds(i * width, width)] = field[micro, 0, i, pl.ds(first, width)]
         if k < span:
+            upstream = refs[0]
             rows = [upstream[micro, 0, p, 0, pl.ds(j, 1), :] for j in range(2) for p in range(pairs)]
             rows = jnp.concatenate([r.astype(F32) for r in rows], axis=0).astype(BF16)
             out[pl.ds(2 * width, pairs // 4)] = rows.reshape(pairs // 4, 8, 256)
 
-    fill(outs[0], 0, section)
-    for k in range(1, pairs):
-        for micro in range(2):
-            fill(outs[k].at[micro], k, micro)
+    for k, out in zip(offsets, refs[-len(offsets) :]):
+        if k == 0:
+            fill(out, k, section)
+        else:
+            for micro in range(2):
+                fill(out.at[micro], k, micro)
 
 
 def main_body(span, pairs, spread, mine, partner, *refs):
     received = refs[: pairs - 1]
-    swapped, banded, second, keep, send, xf, hid, hgs, us, t2, t1 = refs[pairs - 1 :]
+    swapped, banded, second_hbm, keep, send = refs[pairs - 1 : pairs + 4]
+    second, second_sem, xf, hid, hgs, us, t2, t1 = refs[pairs + 4 :]
+    second_copy = pltpu.make_async_copy(second_hbm, second, second_sem)
+    second_copy.start()
     space = lax.axis_index("space")
     side, pair = space % 2, space // 2
     section = lax.axis_index("section")
@@ -167,6 +173,7 @@
             one_k = jnp.concatenate([jnp.where(low, ra, rb), rb[:, :CB]], axis=1)
             cols.append(jnp.concatenate([zero_k, one_k], axis=0).astype(BF16))
     out = jnp.zeros((2 * half, CC), F32)
+    second_copy.wait()
     for tap in range(9):
         out = out + jnp.dot(
             cols[tap], second[pl.ds(tap * 192, 192), :], preferred_element_type=F32
@@ -293,31 +300,36 @@
     section = lax.axis_index("section")
 
     piece = lambda k: 2 * width + (tail if k < span else 0)
-    mine, *outgoing = call(
-        lambda *refs: cut_body(span, pairs, *refs),
-        [jax.ShapeDtypeStruct((piece(0), 8, 256), BF16)]
-        + [jax.ShapeDtypeStruct((2, piece(k), 8, 256), BF16) for k in range(1, pairs)],
-        [],
-        (input_field, upstream_grad),
-    )
+    pieces = {}
+    for offsets, operands in (
+        (range(span, pairs), (input_field,)),
+        (range(span), (input_field, upstream_grad)),
+    ):
+        if len(offsets) > 0:
+            shapes = [
+                jax.ShapeDtypeStruct(((2,) if k > 0 else ()) + (piece(k), 8, 256), BF16)
+                for k in offsets
+            ]
+            body = lambda *refs, offsets=offsets: cut_body(span, pairs, offsets, *refs)
+            pieces.update(zip(offsets, call(body, shapes, [], operands)))
+    mine = pieces[0]
     received = [None] * (pairs - 1)
-    for k in sorted(range(1, pairs), key=lambda k: (k != 2, -k)):
+    for k in range(pairs - 1, 0, -1):
         route = [(2 * d + c, 2 * (d ^ (2 * k) ^ c) + c) for d in range(spread) for c in range(2)]
-        received[k - 1] = lax.ppermute(outgoing[k - 1], ("space", "section"), route)
+        received[k - 1] = lax.ppermute(pieces[k], ("space", "section"), route)
     partner = lax.ppermute(mine, "space", swap_bit(spread, 0))
-    swapped = lax.ppermute(
-        jnp.concatenate([pick(block, 1 - section, 0) for block in received]),
-        "section",
-        swap_bit(2, 0),
-    )
-
     banded = call(banded_body, jax.ShapeDtypeStruct((9 * 256, 256), BF16), [], (first_weight.T,))
+    outgoing = jnp.concatenate([pick(block, 1 - section, 0) for block in received])
+    outgoing, partner, banded = lax.optimization_barrier((outgoing, partner, banded))
+    swapped = lax.ppermute(outgoing, "section", swap_bit(2, 0))
     h2, h1 = packed_rows(spread)
     block = jax.ShapeDtypeStruct((pairs // span, h2 + h1, 128), BF16)
     kept, outgoing = call(
         lambda *refs: main_body(span, pairs, spread, *refs),
         [block, block],
         [
+            pltpu.VMEM(second_weight.shape, BF16),
+            pltpu.SemaphoreType.DMA,
             pltpu.VMEM((2, 2, (2 * pairs + 1) * width * 8 + 16, 128), F32),
             pltpu.VMEM((2, 2, (pairs + 1) * width * 4 + 16, 128), F32),
             pltpu.VMEM((2, 2, pairs * width * 4, 128), F32),
@@ -326,6 +338,7 @@
             pltpu.VMEM((TAPS * CA + 4 * h1, 128), F32),
         ],
         (mine, partner, *received, swapped, banded, second_weight),
+        in_hbm=1,
     )
 
     def added(a, b):

time: 32 us -> 29.4 us (0.919)
  waiting for transfers between devices: 12.9 us -> 10.6 us
  starting transfers between devices: 12.1 us -> 11.5 us
  Pallas kernels: 3.45 us -> 3.78 us
    ppermute x4, waiting for transfers between devices: 5.38 us -> 3.65 us  [the longest x3 2.58 us: shards(): received[k - 1] = lax.ppermute(pieces[k], ('space', 'section'), route)]
    ppermute x1, waiting for transfers between devices: 0.84 us -> 0.01 us  [shards(): partner = lax.ppermute(mine, 'space', swap_bit(spread, 0))]
    ppermute x1, starting transfers between devices: 2.26 us -> 1.64 us  [shards(): partner = lax.ppermute(mine, 'space', swap_bit(spread, 0))]
    ppermute x1, waiting for transfers between devices: 2.99 us -> 3.48 us  [shards(): lax.ppermute(pick(paired, 1 - here, 1), 'space', swap_bit(spread, bit + 1))]
    ppermute x1, starting transfers between devices: 2.3 us -> 1.88 us  [shards(): lax.ppermute(pick(paired, 1 - here, 1), 'space', swap_bit(spread, bit + 1))]
    pallas_call x3 -> x4, Pallas kernels: 2.63 us -> 2.96 us  [call(): pl.pallas_call(body, out_shape=out_shape, in_specs=[vmem] * (len(args) -...]
  transfers between devices with their start and end apart: 8 -> 8, of which waited for: 7 -> 6; matrix products, arithmetic and copies ran while one was open for 0% -> 0% of each run, Pallas kernels for 1% -> 1%
where the time goes in v4:
time: 29.4 us; the launch traced here: 29.2 us
  starting transfers between devices  11.5 us (39%)
  waiting for transfers between devices  10.6 us (36%)
  Pallas kernels  3.78 us (13%)
  local copies, waits for them, and re-layouts  2.53 us (9%)
  between operations  0.72 us (2%)
    ppermute x3, starting transfers between devices, shards(): received[k - 1] = lax.ppermute(pieces[k], ('space', 'section'), route)  5.82 us
    ppermute x1, waiting for transfers between devices, shards(): lax.ppermute(pick(paired, 1 - here, 1), 'space', swap_bit(spread, bit + 1))  3.48 us
    pallas_call x4, Pallas kernels, call(): pl.pallas_call(body, out_shape=out_shape, in_specs=[vmem] * (len(args) -...  2.96 us
    ppermute x3, waiting for transfers between devices, shards(): received[k - 1] = lax.ppermute(pieces[k], ('space', 'section'), route)  2.58 us
    unnamed x8, local copies, waits for them, and re-layouts  2.5 us
    ppermute x1, waiting for transfers between devices, shards(): came = lax.ppermute(total, 'dp', swap_bit(replicas, bit))  2.44 us
    ppermute x1, starting transfers between devices, shards(): lax.ppermute(pick(paired, 1 - here, 1), 'space', swap_bit(spread, bit + 1))  1.88 us
    ppermute x1, starting transfers between devices, shards(): partner = lax.ppermute(mine, 'space', swap_bit(spread, 0))  1.64 us
  transfers between devices with their start and end apart: 8, of which 6 were waited for; matrix products, arithmetic and copies ran while one was open for 0% of the time, Pallas kernels for 1%

profile of v4, /device:TPU:0, one launch (start us, length us, event | category | flops | bytes accessed | tf_op | source)
XLA Modules:
  0.0 29.2 jit_solution(14935602822657116340)
XLA Ops:
  0.6 0.0 copy-start
  0.6 0.9 %copy-done = bf16[2,1,2,8,8,256]{5,4,3,2,1,0:T(8,128)(2,1)S(1)} copy-done((bf16[2,1,2,8,8,256]{5,4,3,2,1,0:T(8,128)(2,1)S(1)}, bf16[2,1,2,8,8,256]{5,4,3,2,1,0:T(8,128)(2,1)}, u32[]{:S(2)}) %copy-start) | copy-done | bytes 131096
  1.5 0.0 copy-start.1
  1.6 5.1 %collective-permute-start.2 = (bf16[2,8,8,256]{3,2,1,0:T(8,128)(2,1)S(1)}, bf16[2,8,8,256]{3,2,1,0:T(8,128)(2,1)S(1)}, u32[]{:S(2)}, u32[]{:S(2)}) collective-permute-start(bf16[2,8,8,256]{3,2,1,0:T(8,128)(2,1)S(1)} %get-tuple-element.16), channel_id=1, source_target_pairs={{0,24},{2,30},{4,28},{6,26},{8,16},{10,22},{12,20},{14,18},{16,8},... | collective-permute-start | bytes 196616 | tf_op jit(solution)/shard_map/ppermute | solution.py:319
  6.7 0.0 collective-permute-start.1
  6.7 0.0 copy-start.3
  6.7 0.7 %copy-done.3 = bf16[2,1,4,1,2,256]{5,4,3,2,1,0:T(2,128)(2,1)S(1)} copy-done((bf16[2,1,4,1,2,256]{5,4,3,2,1,0:T(2,128)(2,1)S(1)}, bf16[2,1,4,1,2,256]{5,4,3,2,1,0:T(2,128)(2,1)}, u32[]{:S(2)}) %copy-start.3) | copy-done | bytes 8216
  7.4 0.7 %collective-permute-start = (bf16[2,9,8,256]{3,2,1,0:T(8,128)(2,1)S(1)}, bf16[2,9,8,256]{3,2,1,0:T(8,128)(2,1)S(1)}, u32[]{:S(2)}, u32[]{:S(2)}) collective-permute-start(bf16[2,9,8,256]{3,2,1,0:T(8,128)(2,1)S(1)} %get-tuple-element.14), channel_id=1, source_target_pairs={{0,8},{2,14},{4,12},{6,10},{8,0},{10,6},{12,4},{14,2},{16,24},{18,... | collective-permute-start | bytes 221192 | tf_op jit(solution)/shard_map/ppermute | solution.py:319
  8.1 1.6 %collective-permute-start.3 = (bf16[9,8,256]{2,1,0:T(8,128)(2,1)S(1)}, bf16[9,8,256]{2,1,0:T(8,128)(2,1)S(1)}, u32[]{:S(2)}, u32[]{:S(2)}) collective-permute-start(bf16[9,8,256]{2,1,0:T(8,128)(2,1)S(1)} %get-tuple-element.13.refs_0_), channel_id=1, source_target_pairs={{0,4},{4,0},{8,12},{12,8},{16,20},{20,16},{24,28},{28,24},{1,5},{5... | collective-permute-start | bytes 110600 | tf_op jit(solution)/shard_map/ppermute | solution.py:320
  9.7 0.0 copy-start.2
  9.7 0.9 %copy-done.2 = bf16[864,64]{0,1:T(8,128)(2,1)S(1)} copy-done((bf16[864,64]{0,1:T(8,128)(2,1)S(1)}, bf16[864,64]{0,1:T(8,128)(2,1)}, u32[]{:S(2)}) %copy-start.2) | copy-done | bytes 110616
  10.6 0.3 %shard_map.61.refs_6_ = bf16[2304,256]{1,0:T(8,128)(2,1)S(1)} custom-call(bf16[64,864]{1,0:T(8,128)(2,1)S(1)} %bitcast.11), custom_call_target="tpu_custom_call" | custom-call | tf_op jit(solution)/shard_map/pallas_call | solution.py:33
  11.0 0.0 collective-permute-done.2.refs_4_
  11.0 2.1 %collective-permute-done.1.refs_3_ = bf16[2,8,8,256]{3,2,1,0:T(8,128)(2,1)S(1)} collective-permute-done((bf16[2,8,8,256]{3,2,1,0:T(8,128)(2,1)S(1)}, bf16[2,8,8,256]{3,2,1,0:T(8,128)(2,1)S(1)}, u32[]{:S(2)}, u32[]{:S(2)}) %collective-permute-start.1) | collective-permute-done | bytes 65568 | tf_op jit(solution)/shard_map/ppermute | solution.py:319
  13.2 0.4 %collective-permute-done.refs_2_ = bf16[2,9,8,256]{3,2,1,0:T(8,128)(2,1)S(1)} collective-permute-done((bf16[2,9,8,256]{3,2,1,0:T(8,128)(2,1)S(1)}, bf16[2,9,8,256]{3,2,1,0:T(8,128)(2,1)S(1)}, u32[]{:S(2)}, u32[]{:S(2)}) %collective-permute-start) | collective-permute-done | bytes 73760 | tf_op jit(solution)/shard_map/ppermute | solution.py:319
  13.6 0.0 collective-permute-done.3.refs_1_
  13.6 0.3 %collective-permute-start.4 = (bf16[25,8,256]{2,1,0:T(8,128)(2,1)S(1)}, bf16[25,8,256]{2,1,0:T(8,128)(2,1)S(1)}, u32[]{:S(2)}, u32[]{:S(2)}) collective-permute-start(bf16[25,8,256]{2,1,0:T(8,128)(2,1)S(1)} %pad_maximum_fusion), channel_id=1, source_target_pairs={{0,2},{2,0},{1,3},{3,1},{4,6},{6,4},{5,7},{7,5},{8,10},{10,8},{9,1... | collective-permute-start | bytes 307208 | tf_op jit(solution)/shard_map/ppermute | solution.py:324
  13.9 1.1 %collective-permute-done.4.refs_5_ = bf16[25,8,256]{2,1,0:T(8,128)(2,1)S(1)} collective-permute-done((bf16[25,8,256]{2,1,0:T(8,128)(2,1)S(1)}, bf16[25,8,256]{2,1,0:T(8,128)(2,1)S(1)}, u32[]{:S(2)}, u32[]{:S(2)}) %collective-permute-start.4) | collective-permute-done | bytes 102432 | tf_op jit(solution)/shard_map/ppermute | solution.py:324
  15.0 0.0 copy-done.1
  15.0 2.6 %shard_map.62 = (bf16[2,144,128]{2,1,0:T(8,128)(2,1)S(1)}, bf16[2,144,128]{2,1,0:T(8,128)(2,1)S(1)}) custom-call(bf16[9,8,256]{2,1,0:T(8,128)(2,1)S(1)} %get-tuple-element.13.refs_0_, bf16[9,8,256]{2,1,0:T(8,128)(2,1)S(1)} %collective-permute-done.3.refs_1_, bf16[2,9,8,256]{3,2,1,0:T(8,128)(2,1)S(1)} %collective-permute-done.refs_2_, ...), custom_call_target="tpu_custom_call" | custom-call | tf_op jit(solution)/shard_map/pallas_call | solution.py:33
  17.6 0.3 collective-permute-start.5
  17.9 1.0 %collective-permute-done.5 = bf16[2,144,128]{2,1,0:T(8,128)(2,1)S(1)} collective-permute-done((bf16[2,144,128]{2,1,0:T(8,128)(2,1)S(1)}, bf16[2,144,128]{2,1,0:T(8,128)(2,1)S(1)}, u32[]{:S(2)}, u32[]{:S(2)}) %collective-permute-start.5) | collective-permute-done | bytes 73760 | tf_op jit(solution)/shard_map/ppermute | solution.py:347
  19.0 1.9 %collective-permute-start.6 = (bf16[1,144,128]{2,1,0:T(8,128)(2,1)S(1)}, bf16[1,144,128]{2,1,0:T(8,128)(2,1)S(1)}, u32[]{:S(2)}, u32[]{:S(2)}) collective-permute-start(bf16[1,144,128]{2,1,0:T(8,128)(2,1)S(1)} %constant_dynamic-slice_fusion), channel_id=1, source_target_pairs={{0,16},{4,20},{8,24},{12,28},{16,0},{20,4},{24,8},{28,12},{1,17},{... | collective-permute-start | bytes 110600 | tf_op jit(solution)/shard_map/ppermute | solution.py:353
  20.8 3.5 %collective-permute-done.6 = bf16[1,144,128]{2,1,0:T(8,128)(2,1)S(1)} collective-permute-done((bf16[1,144,128]{2,1,0:T(8,128)(2,1)S(1)}, bf16[1,144,128]{2,1,0:T(8,128)(2,1)S(1)}, u32[]{:S(2)}, u32[]{:S(2)}) %collective-permute-start.6) | collective-permute-done | bytes 36896 | tf_op jit(solution)/shard_map/ppermute | solution.py:353
  24.3 1.6 %collective-permute-start.7 = (bf16[144,128]{1,0:T(8,128)(2,1)S(1)}, bf16[144,128]{1,0:T(8,128)(2,1)S(1)}, u32[]{:S(2)}, u32[]{:S(2)}) collective-permute-start(bf16[144,128]{1,0:T(8,128)(2,1)S(1)} %fusion.refs_0_), channel_id=1, source_target_pairs={{0,1},{1,0},{2,3},{3,2},{4,5},{5,4},{6,7},{7,6},{8,9},{9,8},{10,11... | collective-permute-start | bytes 110600 | tf_op jit(solution)/shard_map/ppermute | solution.py:362
  25.9 2.4 %collective-permute-done.7.refs_1_ = bf16[144,128]{1,0:T(8,128)(2,1)S(1)} collective-permute-done((bf16[144,128]{1,0:T(8,128)(2,1)S(1)}, bf16[144,128]{1,0:T(8,128)(2,1)S(1)}, u32[]{:S(2)}, u32[]{:S(2)}) %collective-permute-start.7) | collective-permute-done | bytes 36896 | tf_op jit(solution)/shard_map/ppermute | solution.py:362
  28.4 0.8 %shard_map.63 = (f32[32,108]{1,0:T(8,128)}, f32[64,216]{1,0:T(8,128)}) custom-call(bf16[144,128]{1,0:T(8,128)(2,1)S(1)} %fusion.refs_0_, bf16[144,128]{1,0:T(8,128)(2,1)S(1)} %collective-permute-done.7.refs_1_), custom_call_target="tpu_custom_call" | custom-call | tf_op jit(solution)/shard_map/pallas_call | solution.py:366
  (9 shorter events, 0.1 us)
Async XLA Ops:
  0.6 0.9 %copy-start = (bf16[2,1,2,8,8,256]{5,4,3,2,1,0:T(8,128)(2,1)S(1)}, bf16[2,1,2,8,8,256]{5,4,3,2,1,0:T(8,128)(2,1)}, u32[]{:S(2)}) copy-start(bf16[2,1,2,8,8,256]{5,4,3,2,1,0:T(8,128)(2,1)} %refs_0_.3) | copy-start | bytes 393220
  1.5 13.5 %copy-start.1 = (bf16[1728,128]{1,0:T(8,128)(2,1)S(1)}, bf16[1728,128]{1,0:T(8,128)(2,1)}, u32[]{:S(2)}) copy-start(bf16[1728,128]{1,0:T(8,128)(2,1)} %refs_7_.1) | copy-start | bytes 1327108
  1.6 9.4 %collective-permute-start.2 = (bf16[2,8,8,256]{3,2,1,0:T(8,128)(2,1)S(1)}, bf16[2,8,8,256]{3,2,1,0:T(8,128)(2,1)S(1)}, u32[]{:S(2)}, u32[]{:S(2)}) collective-permute-start(bf16[2,8,8,256]{3,2,1,0:T(8,128)(2,1)S(1)} %get-tuple-element.16), channel_id=1, source_target_pairs={{0,24},{2,30},{4,28},{6,26},{8,16},{10,22},{12,20},{14,18},{16,8},... | collective-permute-start | bytes 196616 | tf_op jit(solution)/shard_map/ppermute | solution.py:319
  6.7 6.5 %collective-permute-start.1 = (bf16[2,8,8,256]{3,2,1,0:T(8,128)(2,1)S(1)}, bf16[2,8,8,256]{3,2,1,0:T(8,128)(2,1)S(1)}, u32[]{:S(2)}, u32[]{:S(2)}) collective-permute-start(bf16[2,8,8,256]{3,2,1,0:T(8,128)(2,1)S(1)} %get-tuple-element.15), channel_id=1, source_target_pairs={{0,16},{2,22},{4,20},{6,18},{8,24},{10,30},{12,28},{14,26},{16,0},... | collective-permute-start | bytes 196616 | tf_op jit(solution)/shard_map/ppermute | solution.py:319
  6.7 0.7 %copy-start.3 = (bf16[2,1,4,1,2,256]{5,4,3,2,1,0:T(2,128)(2,1)S(1)}, bf16[2,1,4,1,2,256]{5,4,3,2,1,0:T(2,128)(2,1)}, u32[]{:S(2)}) copy-start(bf16[2,1,4,1,2,256]{5,4,3,2,1,0:T(2,128)(2,1)} %refs_1_.1) | copy-start | bytes 24580
  7.4 6.2 %collective-permute-start = (bf16[2,9,8,256]{3,2,1,0:T(8,128)(2,1)S(1)}, bf16[2,9,8,256]{3,2,1,0:T(8,128)(2,1)S(1)}, u32[]{:S(2)}, u32[]{:S(2)}) collective-permute-start(bf16[2,9,8,256]{3,2,1,0:T(8,128)(2,1)S(1)} %get-tuple-element.14), channel_id=1, source_target_pairs={{0,8},{2,14},{4,12},{6,10},{8,0},{10,6},{12,4},{14,2},{16,24},{18,... | collective-permute-start | bytes 221192 | tf_op jit(solution)/shard_map/ppermute | solution.py:319
  8.1 5.5 %collective-permute-start.3 = (bf16[9,8,256]{2,1,0:T(8,128)(2,1)S(1)}, bf16[9,8,256]{2,1,0:T(8,128)(2,1)S(1)}, u32[]{:S(2)}, u32[]{:S(2)}) collective-permute-start(bf16[9,8,256]{2,1,0:T(8,128)(2,1)S(1)} %get-tuple-element.13.refs_0_), channel_id=1, source_target_pairs={{0,4},{4,0},{8,12},{12,8},{16,20},{20,16},{24,28},{28,24},{1,5},{5... | collective-permute-start | bytes 110600 | tf_op jit(solution)/shard_map/ppermute | solution.py:320
  9.7 0.9 %copy-start.2 = (bf16[864,64]{0,1:T(8,128)(2,1)S(1)}, bf16[864,64]{0,1:T(8,128)(2,1)}, u32[]{:S(2)}) copy-start(bf16[864,64]{0,1:T(8,128)(2,1)} %param.5) | copy-start | bytes 331780
  13.6 1.4 %collective-permute-start.4 = (bf16[25,8,256]{2,1,0:T(8,128)(2,1)S(1)}, bf16[25,8,256]{2,1,0:T(8,128)(2,1)S(1)}, u32[]{:S(2)}, u32[]{:S(2)}) collective-permute-start(bf16[25,8,256]{2,1,0:T(8,128)(2,1)S(1)} %pad_maximum_fusion), channel_id=1, source_target_pairs={{0,2},{2,0},{1,3},{3,1},{4,6},{6,4},{5,7},{7,5},{8,10},{10,8},{9,1... | collective-permute-start | bytes 307208 | tf_op jit(solution)/shard_map/ppermute | solution.py:324
  17.6 1.3 %collective-permute-start.5 = (bf16[2,144,128]{2,1,0:T(8,128)(2,1)S(1)}, bf16[2,144,128]{2,1,0:T(8,128)(2,1)S(1)}, u32[]{:S(2)}, u32[]{:S(2)}) collective-permute-start(bf16[2,144,128]{2,1,0:T(8,128)(2,1)S(1)} %get-tuple-element.21), channel_id=1, source_target_pairs={{0,2},{2,0},{1,3},{3,1},{4,6},{6,4},{5,7},{7,5},{8,10},{10,8},{9,1... | collective-permute-start | bytes 221192 | tf_op jit(solution)/shard_map/ppermute | solution.py:347
  19.0 5.4 %collective-permute-start.6 = (bf16[1,144,128]{2,1,0:T(8,128)(2,1)S(1)}, bf16[1,144,128]{2,1,0:T(8,128)(2,1)S(1)}, u32[]{:S(2)}, u32[]{:S(2)}) collective-permute-start(bf16[1,144,128]{2,1,0:T(8,128)(2,1)S(1)} %constant_dynamic-slice_fusion), channel_id=1, source_target_pairs={{0,16},{4,20},{8,24},{12,28},{16,0},{20,4},{24,8},{28,12},{1,17},{... | collective-permute-start | bytes 110600 | tf_op jit(solution)/shard_map/ppermute | solution.py:353
  24.3 4.0 %collective-permute-start.7 = (bf16[144,128]{1,0:T(8,128)(2,1)S(1)}, bf16[144,128]{1,0:T(8,128)(2,1)S(1)}, u32[]{:S(2)}, u32[]{:S(2)}) collective-permute-start(bf16[144,128]{1,0:T(8,128)(2,1)S(1)} %fusion.refs_0_), channel_id=1, source_target_pairs={{0,1},{1,0},{2,3},{3,2},{4,5},{5,4},{6,7},{7,6},{8,9},{9,8},{10,11... | collective-permute-start | bytes 110600 | tf_op jit(solution)/shard_map/ppermute | solution.py:362

commit v5 on v3

--- a/solution.py
+++ b/solution.py
@@ -66,10 +66,20 @@
             ).astype(BF16)
 
 
-def cut_body(span, pairs, field, upstream, *outs):
+def cut_body(span, pairs, field_hbm, upstream_hbm, *refs):
+    *outs, field, upstream, sems = refs
     pair = lax.axis_index("space") // 2
     section = lax.axis_index("section")
     width = 2 * span
+    copies = [
+        pltpu.make_async_copy(field_hbm.at[0], field.at[0], sems.at[0]),
+        pltpu.make_async_copy(field_hbm.at[1], field.at[1], sems.at[1]),
+        pltpu.make_async_copy(upstream_hbm, upstream, sems.at[2]),
+    ]
+    for copy in copies:
+        copy.start()
+    for copy in copies:
+        copy.wait()
 
     def fill(out, k, micro):
         first = ((pair ^ k) // span) * width
@@ -119,7 +129,7 @@
     place(lambda at, size: mine[pl.ds(at, size)], 0, side)
     place(lambda at, size: partner[pl.ds(at, size)], 0, 1 - side)
     offset = 0
-    for k in range(1, pairs):
+    for k in swap_order(span, pairs):
         ref = received[k - 1]
         place(lambda at, size: ref[section, pl.ds(at, size)], k, side ^ section)
         start = offset
@@ -253,6 +263,10 @@
         send[n, h2 : h2 + h1, :] = sent.astype(BF16)
 
 
+def swap_order(span, pairs):
+    return [*range(pairs - 1, span, -1), *range(1, span + 1)]
+
+
 def packed_rows(spread):
     r2, r1 = TAPS * CB // spread, TAPS * CA // spread
     return round_up(-(-r2 // 2), 16), round_up(-(-r1 // 4), 16)
@@ -293,25 +307,35 @@
     section = lax.axis_index("section")
 
     piece = lambda k: 2 * width + (tail if k < span else 0)
-    mine, *outgoing = call(
+    hbm = pl.BlockSpec(memory_space=pltpu.HBM)
+    pieces = pl.pallas_call(
         lambda *refs: cut_body(span, pairs, *refs),
-        [jax.ShapeDtypeStruct((piece(0), 8, 256), BF16)]
-        + [jax.ShapeDtypeStruct((2, piece(k), 8, 256), BF16) for k in range(1, pairs)],
-        [],
-        (input_field, upstream_grad),
+        out_shape=[
+            jax.ShapeDtypeStruct(((2,) if k > 0 else ()) + (piece(k), 8, 256), BF16)
+            for k in range(pairs)
+        ],
+        in_specs=[hbm, hbm],
+        out_specs=[pl.BlockSpec(memory_space=pltpu.VMEM)] * pairs,
+        scratch_shapes=[
+            pltpu.VMEM(input_field.shape, BF16),
+            pltpu.VMEM(upstream_grad.shape, BF16),
+            pltpu.SemaphoreType.DMA((3,)),
+        ],
+        compiler_params=pltpu.CompilerParams(vmem_limit_bytes=16 << 20),
+    )(
+        pltpu.with_memory_space_constraint(input_field, pltpu.HBM),
+        pltpu.with_memory_space_constraint(upstream_grad, pltpu.HBM),
     )
+    mine = pieces[0]
     received = [None] * (pairs - 1)
-    for k in sorted(range(1, pairs), key=lambda k: (k != 2, -k)):
+    for k in sorted(range(1, pairs), key=lambda k: (k < span, k)):
         route = [(2 * d + c, 2 * (d ^ (2 * k) ^ c) + c) for d in range(spread) for c in range(2)]
-        received[k - 1] = lax.ppermute(outgoing[k - 1], ("space", "section"), route)
+        received[k - 1] = lax.ppermute(pieces[k], ("space", "section"), route)
     partner = lax.ppermute(mine, "space", swap_bit(spread, 0))
-    swapped = lax.ppermute(
-        jnp.concatenate([pick(block, 1 - section, 0) for block in received]),
-        "section",
-        swap_bit(2, 0),
-    )
-
     banded = call(banded_body, jax.ShapeDtypeStruct((9 * 256, 256), BF16), [], (first_weight.T,))
+    outgoing = jnp.concatenate([pick(received[k - 1], 1 - section, 0) for k in swap_order(span, pairs)])
+    outgoing, partner, banded = lax.optimization_barrier((outgoing, partner, banded))
+    swapped = lax.ppermute(outgoing, "section", swap_bit(2, 0))
     h2, h1 = packed_rows(spread)
     block = jax.ShapeDtypeStruct((pairs // span, h2 + h1, 128), BF16)
     kept, outgoing = call(
@@ -349,7 +373,7 @@
     came = lax.ppermute(total, "dp", swap_bit(replicas, bit))
     first_out = (CB // 2, TAPS * CA // spread)
     second_out = (CC // 2, TAPS * CB // spread)
-    vmem, hbm = pl.BlockSpec(memory_space=pltpu.VMEM), pl.BlockSpec(memory_space=pl.ANY)
+    vmem = pl.BlockSpec(memory_space=pltpu.VMEM)
     first_grad, second_grad = pl.pallas_call(
         lambda *refs: unpack_body(spread, *refs),
         out_shape=[jax.ShapeDtypeStruct(first_out, F32), jax.ShapeDtypeStruct(second_out, F32)],

time: 32 us -> 27.9 us (0.87)
  waiting for transfers between devices: 12.9 us -> 9.26 us
  local copies, waits for them, and re-layouts: 2.52 us -> 0.93 us
  Pallas kernels: 3.45 us -> 4.4 us
    ppermute x4, waiting for transfers between devices: 5.38 us -> 3.68 us  [the longest x3 2.49 us: shards(): received[k - 1] = lax.ppermute(pieces[k], ('space', 'section'), route)]
    unnamed x8 -> x4, local copies, waits for them, and re-layouts: 2.5 us -> 0.9 us
    pallas_call x0 -> x1, Pallas kernels: none -> 0.98 us  [shards(): pl.pallas_call(lambda *refs: cut_body(span, pairs, *refs), out_shape=[jax...]
    ppermute x1, waiting for transfers between devices: 0.84 us -> 0.13 us  [shards(): partner = lax.ppermute(mine, 'space', swap_bit(spread, 0))]
    ppermute x1, waiting for transfers between devices: 2.99 us -> 2.3 us  [shards(): lax.ppermute(pick(paired, 1 - here, 1), 'space', swap_bit(spread, bit + 1))]
    ppermute x1, starting transfers between devices: 2.26 us -> 1.64 us  [shards(): partner = lax.ppermute(mine, 'space', swap_bit(spread, 0))]
    ppermute x1, waiting for transfers between devices: 2.44 us -> 2.03 us  [shards(): came = lax.ppermute(total, 'dp', swap_bit(replicas, bit))]
    ppermute x1, starting transfers between devices: 1.58 us -> 1.99 us  [shards(): came = lax.ppermute(total, 'dp', swap_bit(replicas, bit))]
where the time goes in v5:
time: 27.9 us; the launch traced here: 27.7 us
  starting transfers between devices  12.3 us (44%)
  waiting for transfers between devices  9.26 us (33%)
  Pallas kernels  4.4 us (16%)
  local copies, waits for them, and re-layouts  0.93 us (3%)
  between operations  0.7 us (3%)
    ppermute x3, starting transfers between devices, shards(): received[k - 1] = lax.ppermute(pieces[k], ('space', 'section'), route)  5.75 us
    ppermute x1, starting transfers between devices, shards(): lax.ppermute(pick(paired, 1 - here, 1), 'space', swap_bit(spread, bit + 1))  2.64 us
    pallas_call x2, Pallas kernels, call(): pl.pallas_call(body, out_shape=out_shape, in_specs=[vmem] * len(args), ou...  2.59 us
    ppermute x3, waiting for transfers between devices, shards(): received[k - 1] = lax.ppermute(pieces[k], ('space', 'section'), route)  2.49 us
    ppermute x1, waiting for transfers between devices, shards(): lax.ppermute(pick(paired, 1 - here, 1), 'space', swap_bit(spread, bit + 1))  2.3 us
    ppermute x1, waiting for transfers between devices, shards(): came = lax.ppermute(total, 'dp', swap_bit(replicas, bit))  2.03 us
    ppermute x1, starting transfers between devices, shards(): came = lax.ppermute(total, 'dp', swap_bit(replicas, bit))  1.99 us
    ppermute x1, starting transfers between devices, shards(): partner = lax.ppermute(mine, 'space', swap_bit(spread, 0))  1.64 us
  transfers between devices with their start and end apart: 8, of which 7 were waited for; matrix products, arithmetic and copies ran while one was open for 0% of the time, Pallas kernels for 1%

profile of v5, /device:TPU:0, one launch (start us, length us, event | category | flops | bytes accessed | tf_op | source)
XLA Modules:
  0.0 27.7 jit_solution(617244665933081356)
XLA Ops:
  0.6 0.0 copy-start
  0.6 1.0 %shard_map.59 = (bf16[9,8,256]{2,1,0:T(8,128)(2,1)S(1)}, bf16[2,9,8,256]{3,2,1,0:T(8,128)(2,1)S(1)}, bf16[2,8,8,256]{3,2,1,0:T(8,128)(2,1)S(1)}, bf16[2,8,8,256]{3,2,1,0:T(8,128)(2,1)S(1)}) custom-call(bf16[2,1,2,8,8,256]{5,4,3,2,1,0:T(8,128)(2,1)} %refs_0_.1, bf16[2,1,4,1,2,256]{5,4,3,2,1,0:T(2,128)(2,1)} %refs_1_.1), custom_call_target="tpu_custom_call" | custom-call | tf_op jit(solution)/shard_map/pallas_call | solution.py:311
  1.6 5.1 %collective-permute-start = (bf16[2,8,8,256]{3,2,1,0:T(8,128)(2,1)S(1)}, bf16[2,8,8,256]{3,2,1,0:T(8,128)(2,1)S(1)}, u32[]{:S(2)}, u32[]{:S(2)}) collective-permute-start(bf16[2,8,8,256]{3,2,1,0:T(8,128)(2,1)S(1)} %get-tuple-element.14), channel_id=1, source_target_pairs={{0,24},{2,30},{4,28},{6,26},{8,16},{10,22},{12,20},{14,18},{16,8},... | collective-permute-start | bytes 196616 | tf_op jit(solution)/shard_map/ppermute | solution.py:333
  6.7 0.0 collective-permute-start.1
  6.7 0.6 %collective-permute-start.2 = (bf16[2,8,8,256]{3,2,1,0:T(8,128)(2,1)S(1)}, bf16[2,8,8,256]{3,2,1,0:T(8,128)(2,1)S(1)}, u32[]{:S(2)}, u32[]{:S(2)}) collective-permute-start(bf16[2,8,8,256]{3,2,1,0:T(8,128)(2,1)S(1)} %get-tuple-element.16), channel_id=1, source_target_pairs={{0,16},{2,22},{4,20},{6,18},{8,24},{10,30},{12,28},{14,26},{16,0},... | collective-permute-start | bytes 196616 | tf_op jit(solution)/shard_map/ppermute | solution.py:333
  7.4 1.6 %collective-permute-start.3 = (bf16[9,8,256]{2,1,0:T(8,128)(2,1)S(1)}, bf16[9,8,256]{2,1,0:T(8,128)(2,1)S(1)}, u32[]{:S(2)}, u32[]{:S(2)}) collective-permute-start(bf16[9,8,256]{2,1,0:T(8,128)(2,1)S(1)} %get-tuple-element.13.refs_0_), channel_id=1, source_target_pairs={{0,4},{4,0},{8,12},{12,8},{16,20},{20,16},{24,28},{28,24},{1,5},{5... | collective-permute-start | bytes 110600 | tf_op jit(solution)/shard_map/ppermute | solution.py:334
  9.0 0.0 copy-start.1
  9.0 0.9 %copy-done.1 = bf16[864,64]{0,1:T(8,128)(2,1)S(1)} copy-done((bf16[864,64]{0,1:T(8,128)(2,1)S(1)}, bf16[864,64]{0,1:T(8,128)(2,1)}, u32[]{:S(2)}) %copy-start.1) | copy-done | bytes 110616
  9.9 0.3 %shard_map.60.refs_6_ = bf16[2304,256]{1,0:T(8,128)(2,1)S(1)} custom-call(bf16[64,864]{1,0:T(8,128)(2,1)S(1)} %bitcast.11), custom_call_target="tpu_custom_call" | custom-call | tf_op jit(solution)/shard_map/pallas_call | solution.py:33
  10.3 0.0 collective-permute-done.refs_4_
  10.3 2.1 %collective-permute-done.2.refs_3_ = bf16[2,8,8,256]{3,2,1,0:T(8,128)(2,1)S(1)} collective-permute-done((bf16[2,8,8,256]{3,2,1,0:T(8,128)(2,1)S(1)}, bf16[2,8,8,256]{3,2,1,0:T(8,128)(2,1)S(1)}, u32[]{:S(2)}, u32[]{:S(2)}) %collective-permute-start.2) | collective-permute-done | bytes 65568 | tf_op jit(solution)/shard_map/ppermute | solution.py:333
  12.4 0.4 %collective-permute-done.1.refs_2_ = bf16[2,9,8,256]{3,2,1,0:T(8,128)(2,1)S(1)} collective-permute-done((bf16[2,9,8,256]{3,2,1,0:T(8,128)(2,1)S(1)}, bf16[2,9,8,256]{3,2,1,0:T(8,128)(2,1)S(1)}, u32[]{:S(2)}, u32[]{:S(2)}) %collective-permute-start.1) | collective-permute-done | bytes 73760 | tf_op jit(solution)/shard_map/ppermute | solution.py:333
  12.8 0.1 collective-permute-done.3.refs_1_
  12.9 0.1 collective-permute-start.4
  13.0 1.2 %collective-permute-done.4.refs_5_ = bf16[25,8,256]{2,1,0:T(8,128)(2,1)S(1)} collective-permute-done((bf16[25,8,256]{2,1,0:T(8,128)(2,1)S(1)}, bf16[25,8,256]{2,1,0:T(8,128)(2,1)S(1)}, u32[]{:S(2)}, u32[]{:S(2)}) %collective-permute-start.4) | collective-permute-done | bytes 102432 | tf_op jit(solution)/shard_map/ppermute | solution.py:338
  14.2 0.0 copy-done
  14.2 2.3 %shard_map.61 = (bf16[2,144,128]{2,1,0:T(8,128)(2,1)S(1)}, bf16[2,144,128]{2,1,0:T(8,128)(2,1)S(1)}) custom-call(bf16[9,8,256]{2,1,0:T(8,128)(2,1)S(1)} %get-tuple-element.13.refs_0_, bf16[9,8,256]{2,1,0:T(8,128)(2,1)S(1)} %collective-permute-done.3.refs_1_, bf16[2,9,8,256]{3,2,1,0:T(8,128)(2,1)S(1)} %collective-permute-done.1.refs_2_, ...), custom_call_target="tpu_custom_call" | custom-call | tf_op jit(solution)/shard_map/pallas_call | solution.py:33
  16.5 0.2 collective-permute-start.5
  16.7 1.1 %collective-permute-done.5 = bf16[2,144,128]{2,1,0:T(8,128)(2,1)S(1)} collective-permute-done((bf16[2,144,128]{2,1,0:T(8,128)(2,1)S(1)}, bf16[2,144,128]{2,1,0:T(8,128)(2,1)S(1)}, u32[]{:S(2)}, u32[]{:S(2)}) %collective-permute-start.5) | collective-permute-done | bytes 73760 | tf_op jit(solution)/shard_map/ppermute | solution.py:358
  17.9 2.6 %collective-permute-start.6 = (bf16[1,144,128]{2,1,0:T(8,128)(2,1)S(1)}, bf16[1,144,128]{2,1,0:T(8,128)(2,1)S(1)}, u32[]{:S(2)}, u32[]{:S(2)}) collective-permute-start(bf16[1,144,128]{2,1,0:T(8,128)(2,1)S(1)} %constant_dynamic-slice_fusion), channel_id=1, source_target_pairs={{0,16},{4,20},{8,24},{12,28},{16,0},{20,4},{24,8},{28,12},{1,17},{... | collective-permute-start | bytes 110600 | tf_op jit(solution)/shard_map/ppermute | solution.py:364
  20.5 2.3 %collective-permute-done.6 = bf16[1,144,128]{2,1,0:T(8,128)(2,1)S(1)} collective-permute-done((bf16[1,144,128]{2,1,0:T(8,128)(2,1)S(1)}, bf16[1,144,128]{2,1,0:T(8,128)(2,1)S(1)}, u32[]{:S(2)}, u32[]{:S(2)}) %collective-permute-start.6) | collective-permute-done | bytes 36896 | tf_op jit(solution)/shard_map/ppermute | solution.py:364
  22.8 2.0 %collective-permute-start.7 = (bf16[144,128]{1,0:T(8,128)(2,1)S(1)}, bf16[144,128]{1,0:T(8,128)(2,1)S(1)}, u32[]{:S(2)}, u32[]{:S(2)}) collective-permute-start(bf16[144,128]{1,0:T(8,128)(2,1)S(1)} %fusion.refs_0_), channel_id=1, source_target_pairs={{0,1},{1,0},{2,3},{3,2},{4,5},{5,4},{6,7},{7,6},{8,9},{9,8},{10,11... | collective-permute-start | bytes 110600 | tf_op jit(solution)/shard_map/ppermute | solution.py:373
  24.8 2.0 %collective-permute-done.7.refs_1_ = bf16[144,128]{1,0:T(8,128)(2,1)S(1)} collective-permute-done((bf16[144,128]{1,0:T(8,128)(2,1)S(1)}, bf16[144,128]{1,0:T(8,128)(2,1)S(1)}, u32[]{:S(2)}, u32[]{:S(2)}) %collective-permute-start.7) | collective-permute-done | bytes 36896 | tf_op jit(solution)/shard_map/ppermute | solution.py:373
  26.9 0.8 %shard_map.62 = (f32[32,108]{1,0:T(8,128)}, f32[64,216]{1,0:T(8,128)}) custom-call(bf16[144,128]{1,0:T(8,128)(2,1)S(1)} %fusion.refs_0_, bf16[144,128]{1,0:T(8,128)(2,1)S(1)} %collective-permute-done.7.refs_1_), custom_call_target="tpu_custom_call" | custom-call | tf_op jit(solution)/shard_map/pallas_call | solution.py:377
  (7 shorter events, 0.1 us)
Async XLA Ops:
  0.6 13.6 %copy-start = (bf16[1728,128]{1,0:T(8,128)(2,1)S(1)}, bf16[1728,128]{1,0:T(8,128)(2,1)}, u32[]{:S(2)}) copy-start(bf16[1728,128]{1,0:T(8,128)(2,1)} %refs_7_.1) | copy-start | bytes 1327108
  1.6 8.6 %collective-permute-start = (bf16[2,8,8,256]{3,2,1,0:T(8,128)(2,1)S(1)}, bf16[2,8,8,256]{3,2,1,0:T(8,128)(2,1)S(1)}, u32[]{:S(2)}, u32[]{:S(2)}) collective-permute-start(bf16[2,8,8,256]{3,2,1,0:T(8,128)(2,1)S(1)} %get-tuple-element.14), channel_id=1, source_target_pairs={{0,24},{2,30},{4,28},{6,26},{8,16},{10,22},{12,20},{14,18},{16,8},... | collective-permute-start | bytes 196616 | tf_op jit(solution)/shard_map/ppermute | solution.py:333
  6.7 6.0 %collective-permute-start.1 = (bf16[2,9,8,256]{3,2,1,0:T(8,128)(2,1)S(1)}, bf16[2,9,8,256]{3,2,1,0:T(8,128)(2,1)S(1)}, u32[]{:S(2)}, u32[]{:S(2)}) collective-permute-start(bf16[2,9,8,256]{3,2,1,0:T(8,128)(2,1)S(1)} %get-tuple-element.15), channel_id=1, source_target_pairs={{0,8},{2,14},{4,12},{6,10},{8,0},{10,6},{12,4},{14,2},{16,24},{18,... | collective-permute-start | bytes 221192 | tf_op jit(solution)/shard_map/ppermute | solution.py:333
  6.7 5.7 %collective-permute-start.2 = (bf16[2,8,8,256]{3,2,1,0:T(8,128)(2,1)S(1)}, bf16[2,8,8,256]{3,2,1,0:T(8,128)(2,1)S(1)}, u32[]{:S(2)}, u32[]{:S(2)}) collective-permute-start(bf16[2,8,8,256]{3,2,1,0:T(8,128)(2,1)S(1)} %get-tuple-element.16), channel_id=1, source_target_pairs={{0,16},{2,22},{4,20},{6,18},{8,24},{10,30},{12,28},{14,26},{16,0},... | collective-permute-start | bytes 196616 | tf_op jit(solution)/shard_map/ppermute | solution.py:333
  7.4 5.5 %collective-permute-start.3 = (bf16[9,8,256]{2,1,0:T(8,128)(2,1)S(1)}, bf16[9,8,256]{2,1,0:T(8,128)(2,1)S(1)}, u32[]{:S(2)}, u32[]{:S(2)}) collective-permute-start(bf16[9,8,256]{2,1,0:T(8,128)(2,1)S(1)} %get-tuple-element.13.refs_0_), channel_id=1, source_target_pairs={{0,4},{4,0},{8,12},{12,8},{16,20},{20,16},{24,28},{28,24},{1,5},{5... | collective-permute-start | bytes 110600 | tf_op jit(solution)/shard_map/ppermute | solution.py:334
  9.0 0.9 %copy-start.1 = (bf16[864,64]{0,1:T(8,128)(2,1)S(1)}, bf16[864,64]{0,1:T(8,128)(2,1)}, u32[]{:S(2)}) copy-start(bf16[864,64]{0,1:T(8,128)(2,1)} %param.5) | copy-start | bytes 331780
  12.9 1.3 %collective-permute-start.4 = (bf16[25,8,256]{2,1,0:T(8,128)(2,1)S(1)}, bf16[25,8,256]{2,1,0:T(8,128)(2,1)S(1)}, u32[]{:S(2)}, u32[]{:S(2)}) collective-permute-start(bf16[25,8,256]{2,1,0:T(8,128)(2,1)S(1)} %pad_maximum_fusion), channel_id=1, source_target_pairs={{0,2},{2,0},{1,3},{3,1},{4,6},{6,4},{5,7},{7,5},{8,10},{10,8},{9,1... | collective-permute-start | bytes 307208 | tf_op jit(solution)/shard_map/ppermute | solution.py:338
  16.5 1.3 %collective-permute-start.5 = (bf16[2,144,128]{2,1,0:T(8,128)(2,1)S(1)}, bf16[2,144,128]{2,1,0:T(8,128)(2,1)S(1)}, u32[]{:S(2)}, u32[]{:S(2)}) collective-permute-start(bf16[2,144,128]{2,1,0:T(8,128)(2,1)S(1)} %get-tuple-element.21), channel_id=1, source_target_pairs={{0,2},{2,0},{1,3},{3,1},{4,6},{6,4},{5,7},{7,5},{8,10},{10,8},{9,1... | collective-permute-start | bytes 221192 | tf_op jit(solution)/shard_map/ppermute | solution.py:358
  17.9 4.9 %collective-permute-start.6 = (bf16[1,144,128]{2,1,0:T(8,128)(2,1)S(1)}, bf16[1,144,128]{2,1,0:T(8,128)(2,1)S(1)}, u32[]{:S(2)}, u32[]{:S(2)}) collective-permute-start(bf16[1,144,128]{2,1,0:T(8,128)(2,1)S(1)} %constant_dynamic-slice_fusion), channel_id=1, source_target_pairs={{0,16},{4,20},{8,24},{12,28},{16,0},{20,4},{24,8},{28,12},{1,17},{... | collective-permute-start | bytes 110600 | tf_op jit(solution)/shard_map/ppermute | solution.py:364
  22.8 4.0 %collective-permute-start.7 = (bf16[144,128]{1,0:T(8,128)(2,1)S(1)}, bf16[144,128]{1,0:T(8,128)(2,1)S(1)}, u32[]{:S(2)}, u32[]{:S(2)}) collective-permute-start(bf16[144,128]{1,0:T(8,128)(2,1)S(1)} %fusion.refs_0_), channel_id=1, source_target_pairs={{0,1},{1,0},{2,3},{3,2},{4,5},{5,4},{6,7},{7,6},{8,9},{9,8},{10,11... | collective-permute-start | bytes 110600 | tf_op jit(solution)/shard_map/ppermute | solution.py:373

commit v6 on v5

--- a/solution.py
+++ b/solution.py
@@ -10,7 +10,6 @@
 CC = 128
 TAPS = 27
 SLOPE = 0.3
-SPAN = 2
 BF16 = jnp.bfloat16
 F32 = jnp.float32
 
@@ -66,11 +65,14 @@
             ).astype(BF16)
 
 
-def cut_body(span, pairs, field_hbm, upstream_hbm, *refs):
+def group_of(pair, pairs):
+    return jnp.minimum(pair, pairs - 1 - pair)
+
+
+def cut_body(pairs, field_hbm, upstream_hbm, *refs):
     *outs, field, upstream, sems = refs
     pair = lax.axis_index("space") // 2
     section = lax.axis_index("section")
-    width = 2 * span
     copies = [
         pltpu.make_async_copy(field_hbm.at[0], field.at[0], sems.at[0]),
         pltpu.make_async_copy(field_hbm.at[1], field.at[1], sems.at[1]),
@@ -82,13 +84,16 @@
         copy.wait()
 
     def fill(out, k, micro):
-        first = ((pair ^ k) // span) * width
+        lower = group_of(pair ^ k, pairs)
         for i in range(2):
-            out[pl.ds(i * width, width)] = field[micro, 0, i, pl.ds(first, width)]
-        if k < span:
+            for upper, member in enumerate((lower, pairs - 1 - lower)):
+                out[pl.ds(4 * i + 2 * upper, 2)] = field[micro, 0, i, pl.ds(2 * member, 2)]
+        if k in (0, pairs - 1):
             rows = [upstream[micro, 0, p, 0, pl.ds(j, 1), :] for j in range(2) for p in range(pairs)]
             rows = jnp.concatenate([r.astype(F32) for r in rows], axis=0).astype(BF16)
-            out[pl.ds(2 * width, pairs // 4)] = rows.reshape(pairs // 4, 8, 256)
+            out[pl.ds(8, pairs // 4)] = rows.reshape(pairs // 4, 8, 256)
+        else:
+            out[pl.ds(8, pairs // 4)] = jnp.zeros((pairs // 4, 8, 256), BF16)
 
     fill(outs[0], 0, section)
     for k in range(1, pairs):
@@ -96,13 +101,13 @@
             fill(outs[k].at[micro], k, micro)
 
 
-def main_body(span, pairs, spread, mine, partner, *refs):
+def main_body(pairs, spread, mine, partner, *refs):
     received = refs[: pairs - 1]
     swapped, banded, second, keep, send, xf, hid, hgs, us, t2, t1 = refs[pairs - 1 :]
     space = lax.axis_index("space")
     side, pair = space % 2, space // 2
     section = lax.axis_index("section")
-    width = 2 * span
+    width = 4
     tail = pairs // 4
     base = width * 8 + 8
     total = 2 * pairs * width * 8
@@ -117,9 +122,9 @@
             tiles = load(i * width, width).reshape(width * 8, 256).astype(F32)
             for h in range(2):
                 xf[i, h, pl.ds(start, width * 8), :] = tiles[:, h * 128 : h * 128 + 128]
-        if k < span:
+        if k in (0, pairs - 1):
             rows = load(2 * width, tail).reshape(2 * pairs, 256).astype(F32)
-            volume = 2 * (there % span) + at_side
+            volume = 2 * (there // (pairs // 2)) + at_side
             for j in range(2):
                 for h in range(2):
                     us[h, pl.ds(2 * volume + j, pairs, stride=2 * width), :] = rows[
@@ -129,7 +134,7 @@
     place(lambda at, size: mine[pl.ds(at, size)], 0, side)
     place(lambda at, size: partner[pl.ds(at, size)], 0, 1 - side)
     offset = 0
-    for k in swap_order(span, pairs):
+    for k in swap_order(pairs):
         ref = received[k - 1]
         place(lambda at, size: ref[section, pl.ds(at, size)], k, side ^ section)
         start = offset
@@ -238,16 +243,19 @@
     t1[pl.ds(TAPS * CA, t1.shape[0] - TAPS * CA), :] = jnp.zeros((t1.shape[0] - TAPS * CA, 128), F32)
     low2 = lax.broadcasted_iota(jnp.int32, (h2, 128), 1) < CB
     quarter = lax.broadcasted_iota(jnp.int32, (h1, 128), 1) // 32
-    within = space % width
+    upper = pair // (pairs // 2)
 
     def block(ref, n, stride, start, size):
-        found = ref[pl.ds(n * width * stride + start, size), :]
-        for other in range(1, width):
-            more = ref[pl.ds((n * width + other) * stride + start, size), :]
-            found = jnp.where(within == other, more, found)
+        found = None
+        for member in range(2):
+            for x in range(2):
+                d = 2 * (pairs - 1 - n if member else n) + x
+                more = ref[pl.ds(d * stride + start, size), :]
+                here = jnp.logical_and(upper == member, side == x)
+                found = more if found is None else jnp.where(here, more, found)
         return found
 
-    for n in range(pairs // span):
+    for n in range(pairs // 2):
         a = block(t2, n, r2, 0, h2)
         b = block(t2, n, r2, h2, h2)
         keep[n, 0:h2, :] = jnp.where(low2, a, pltpu.roll(b, 64, 1)).astype(BF16)
@@ -263,8 +271,8 @@
         send[n, h2 : h2 + h1, :] = sent.astype(BF16)
 
 
-def swap_order(span, pairs):
-    return [*range(pairs - 1, span, -1), *range(1, span + 1)]
+def swap_order(pairs):
+    return [1, 3, 2] if pairs == 4 else [*range(1, pairs)]
 
 
 def packed_rows(spread):
@@ -300,16 +308,14 @@
 def shards(input_field, first_weight, second_weight, upstream_grad):
     spread = lax.axis_size("space")
     pairs = spread // 2
-    span = SPAN
-    width = 2 * span
     tail = pairs // 4
     pair = lax.axis_index("space") // 2
     section = lax.axis_index("section")
 
-    piece = lambda k: 2 * width + (tail if k < span else 0)
+    piece = lambda k: 8 + tail
     hbm = pl.BlockSpec(memory_space=pltpu.HBM)
     pieces = pl.pallas_call(
-        lambda *refs: cut_body(span, pairs, *refs),
+        lambda *refs: cut_body(pairs, *refs),
         out_shape=[
             jax.ShapeDtypeStruct(((2,) if k > 0 else ()) + (piece(k), 8, 256), BF16)
             for k in range(pairs)
@@ -328,24 +334,24 @@
     )
     mine = pieces[0]
     received = [None] * (pairs - 1)
-    for k in sorted(range(1, pairs), key=lambda k: (k < span, k)):
+    for k in range(1, pairs):
         route = [(2 * d + c, 2 * (d ^ (2 * k) ^ c) + c) for d in range(spread) for c in range(2)]
         received[k - 1] = lax.ppermute(pieces[k], ("space", "section"), route)
     partner = lax.ppermute(mine, "space", swap_bit(spread, 0))
     banded = call(banded_body, jax.ShapeDtypeStruct((9 * 256, 256), BF16), [], (first_weight.T,))
-    outgoing = jnp.concatenate([pick(received[k - 1], 1 - section, 0) for k in swap_order(span, pairs)])
+    outgoing = jnp.concatenate([pick(received[k - 1], 1 - section, 0) for k in swap_order(pairs)])
     outgoing, partner, banded = lax.optimization_barrier((outgoing, partner, banded))
     swapped = lax.ppermute(outgoing, "section", swap_bit(2, 0))
     h2, h1 = packed_rows(spread)
-    block = jax.ShapeDtypeStruct((pairs // span, h2 + h1, 128), BF16)
+    block = jax.ShapeDtypeStruct((pairs // 2, h2 + h1, 128), BF16)
     kept, outgoing = call(
-        lambda *refs: main_body(span, pairs, spread, *refs),
+        lambda *refs: main_body(pairs, spread, *refs),
         [block, block],
         [
-            pltpu.VMEM((2, 2, (2 * pairs + 1) * width * 8 + 16, 128), F32),
-            pltpu.VMEM((2, 2, (pairs + 1) * width * 4 + 16, 128), F32),
-            pltpu.VMEM((2, 2, pairs * width * 4, 128), F32),
-            pltpu.VMEM((2, pairs * width * 2, 128), F32),
+            pltpu.VMEM((2, 2, (2 * pairs + 1) * 32 + 16, 128), F32),
+            pltpu.VMEM((2, 2, (pairs + 1) * 16 + 16, 128), F32),
+            pltpu.VMEM((2, 2, pairs * 16, 128), F32),
+            pltpu.VMEM((2, pairs * 8, 128), F32),
             pltpu.VMEM((TAPS * CB + 2 * h2, 128), F32),
             pltpu.VMEM((TAPS * CA + 4 * h1, 128), F32),
         ],
@@ -356,10 +362,10 @@
         return (a.astype(F32) + b.astype(F32)).astype(BF16)
 
     total = added(kept, lax.ppermute(outgoing, "section", swap_bit(2, 0)))
-    bit = span.bit_length() - 1
+    bit = 0
     while total.shape[0] > 1:
         paired = total.reshape(total.shape[0] // 2, 2, *total.shape[1:])
-        here = (pair >> bit) & 1
+        here = (group_of(pair, pairs) >> bit) & 1
         kept = pick(paired, here, 1)
         came = lax.ppermute(pick(paired, 1 - here, 1), "space", swap_bit(spread, bit + 1))
         total = added(kept, came)

time: 27.9 us -> 27.3 us (0.978)
  starting transfers between devices: 12.3 us -> 10.9 us
  waiting for transfers between devices: 9.26 us -> 10.1 us
    ppermute x1, starting transfers between devices: 2.64 us -> 1.6 us  [shards(): lax.ppermute(pick(paired, 1 - here, 1), 'space', swap_bit(spread, bit + 1))]
    ppermute x1, waiting for transfers between devices: 2.03 us -> 2.42 us  [shards(): came = lax.ppermute(total, 'dp', swap_bit(replicas, bit))]
    ppermute x1, starting transfers between devices: 1.99 us -> 1.6 us  [shards(): came = lax.ppermute(total, 'dp', swap_bit(replicas, bit))]
    ppermute x3, waiting for transfers between devices: 2.49 us -> 2.85 us  [shards(): received[k - 1] = lax.ppermute(pieces[k], ('space', 'section'), route)]
  transfers between devices with their start and end apart: 8 -> 8, of which waited for: 7 -> 5; matrix products, arithmetic and copies ran while one was open for 0% -> 0% of each run, Pallas kernels for 1% -> 1%
where the time goes in v6:
time: 27.3 us; the launch traced here: 27.1 us
  starting transfers between devices  10.9 us (40%)
  waiting for transfers between devices  10.1 us (37%)
  Pallas kernels  4.39 us (16%)
  local copies, waits for them, and re-layouts  0.94 us (3%)
  between operations  0.73 us (3%)
    ppermute x3, starting transfers between devices, shards(): received[k - 1] = lax.ppermute(pieces[k], ('space', 'section'), route)  5.75 us
    ppermute x3, waiting for transfers between devices, shards(): received[k - 1] = lax.ppermute(pieces[k], ('space', 'section'), route)  2.85 us
    pallas_call x2, Pallas kernels, call(): pl.pallas_call(body, out_shape=out_shape, in_specs=[vmem] * len(args), ou...  2.59 us
    ppermute x1, waiting for transfers between devices, shards(): lax.ppermute(pick(paired, 1 - here, 1), 'space', swap_bit(spread, bit + 1))  2.43 us
    ppermute x1, waiting for transfers between devices, shards(): came = lax.ppermute(total, 'dp', swap_bit(replicas, bit))  2.42 us
    ppermute x1, starting transfers between devices, shards(): partner = lax.ppermute(mine, 'space', swap_bit(spread, 0))  1.64 us
    ppermute x1, starting transfers between devices, shards(): came = lax.ppermute(total, 'dp', swap_bit(replicas, bit))  1.6 us
    ppermute x1, starting transfers between devices, shards(): lax.ppermute(pick(paired, 1 - here, 1), 'space', swap_bit(spread, bit + 1))  1.6 us
  transfers between devices with their start and end apart: 8, of which 5 were waited for; matrix products, arithmetic and copies ran while one was open for 0% of the time, Pallas kernels for 1%

profile of v6, /device:TPU:0, one launch (start us, length us, event | category | flops | bytes accessed | tf_op | source)
XLA Modules:
  0.0 27.1 jit_solution(15793496507614398434)
XLA Ops:
  0.6 0.0 copy-start
  0.6 1.0 %shard_map.59 = (bf16[9,8,256]{2,1,0:T(8,128)(2,1)S(1)}, bf16[2,9,8,256]{3,2,1,0:T(8,128)(2,1)S(1)}, bf16[2,9,8,256]{3,2,1,0:T(8,128)(2,1)S(1)}, bf16[2,9,8,256]{3,2,1,0:T(8,128)(2,1)S(1)}) custom-call(bf16[2,1,2,8,8,256]{5,4,3,2,1,0:T(8,128)(2,1)} %refs_0_.1, bf16[2,1,4,1,2,256]{5,4,3,2,1,0:T(2,128)(2,1)} %refs_1_.1), custom_call_target="tpu_custom_call" | custom-call | tf_op jit(solution)/shard_map/pallas_call | solution.py:317
  1.6 5.1 %collective-permute-start.1 = (bf16[2,9,8,256]{3,2,1,0:T(8,128)(2,1)S(1)}, bf16[2,9,8,256]{3,2,1,0:T(8,128)(2,1)S(1)}, u32[]{:S(2)}, u32[]{:S(2)}) collective-permute-start(bf16[2,9,8,256]{3,2,1,0:T(8,128)(2,1)S(1)} %get-tuple-element.15), channel_id=1, source_target_pairs={{0,24},{2,30},{4,28},{6,26},{8,16},{10,22},{12,20},{14,18},{16,8},... | collective-permute-start | bytes 221192 | tf_op jit(solution)/shard_map/ppermute | solution.py:339
  6.7 0.0 collective-permute-start
  6.7 0.6 %collective-permute-start.2 = (bf16[2,9,8,256]{3,2,1,0:T(8,128)(2,1)S(1)}, bf16[2,9,8,256]{3,2,1,0:T(8,128)(2,1)S(1)}, u32[]{:S(2)}, u32[]{:S(2)}) collective-permute-start(bf16[2,9,8,256]{3,2,1,0:T(8,128)(2,1)S(1)} %get-tuple-element.16), channel_id=1, source_target_pairs={{0,16},{2,22},{4,20},{6,18},{8,24},{10,30},{12,28},{14,26},{16,0},... | collective-permute-start | bytes 221192 | tf_op jit(solution)/shard_map/ppermute | solution.py:339
  7.4 1.6 %collective-permute-start.3 = (bf16[9,8,256]{2,1,0:T(8,128)(2,1)S(1)}, bf16[9,8,256]{2,1,0:T(8,128)(2,1)S(1)}, u32[]{:S(2)}, u32[]{:S(2)}) collective-permute-start(bf16[9,8,256]{2,1,0:T(8,128)(2,1)S(1)} %get-tuple-element.13.refs_0_), channel_id=1, source_target_pairs={{0,4},{4,0},{8,12},{12,8},{16,20},{20,16},{24,28},{28,24},{1,5},{5... | collective-permute-start | bytes 110600 | tf_op jit(solution)/shard_map/ppermute | solution.py:340
  9.0 0.0 copy-start.1
  9.0 0.9 %copy-done.1 = bf16[864,64]{0,1:T(8,128)(2,1)S(1)} copy-done((bf16[864,64]{0,1:T(8,128)(2,1)S(1)}, bf16[864,64]{0,1:T(8,128)(2,1)}, u32[]{:S(2)}) %copy-start.1) | copy-done | bytes 110616
  9.9 0.3 %shard_map.60.refs_6_ = bf16[2304,256]{1,0:T(8,128)(2,1)S(1)} custom-call(bf16[64,864]{1,0:T(8,128)(2,1)S(1)} %bitcast.11), custom_call_target="tpu_custom_call" | custom-call | tf_op jit(solution)/shard_map/pallas_call | solution.py:32
  10.3 0.0 collective-permute-done.1.refs_4_
  10.3 2.8 %collective-permute-done.refs_2_ = bf16[2,9,8,256]{3,2,1,0:T(8,128)(2,1)S(1)} collective-permute-done((bf16[2,9,8,256]{3,2,1,0:T(8,128)(2,1)S(1)}, bf16[2,9,8,256]{3,2,1,0:T(8,128)(2,1)S(1)}, u32[]{:S(2)}, u32[]{:S(2)}) %collective-permute-start) | collective-permute-done | bytes 73760 | tf_op jit(solution)/shard_map/ppermute | solution.py:339
  13.1 0.0 collective-permute-done.2.refs_3_
  13.2 0.0 collective-permute-done.3.refs_1_
  13.2 0.1 collective-permute-start.4
  13.3 1.3 %collective-permute-done.4.refs_5_ = bf16[27,8,256]{2,1,0:T(8,128)(2,1)S(1)} collective-permute-done((bf16[27,8,256]{2,1,0:T(8,128)(2,1)S(1)}, bf16[27,8,256]{2,1,0:T(8,128)(2,1)S(1)}, u32[]{:S(2)}, u32[]{:S(2)}) %collective-permute-start.4) | collective-permute-done | bytes 110624 | tf_op jit(solution)/shard_map/ppermute | solution.py:344
  14.6 0.0 copy-done
  14.6 2.3 %shard_map.61 = (bf16[2,144,128]{2,1,0:T(8,128)(2,1)S(1)}, bf16[2,144,128]{2,1,0:T(8,128)(2,1)S(1)}) custom-call(bf16[9,8,256]{2,1,0:T(8,128)(2,1)S(1)} %get-tuple-element.13.refs_0_, bf16[9,8,256]{2,1,0:T(8,128)(2,1)S(1)} %collective-permute-done.3.refs_1_, bf16[2,9,8,256]{3,2,1,0:T(8,128)(2,1)S(1)} %collective-permute-done.refs_2_, ...), custom_call_target="tpu_custom_call" | custom-call | tf_op jit(solution)/shard_map/pallas_call | solution.py:32
  16.8 0.2 collective-permute-start.5
  17.1 1.1 %collective-permute-done.5 = bf16[2,144,128]{2,1,0:T(8,128)(2,1)S(1)} collective-permute-done((bf16[2,144,128]{2,1,0:T(8,128)(2,1)S(1)}, bf16[2,144,128]{2,1,0:T(8,128)(2,1)S(1)}, u32[]{:S(2)}, u32[]{:S(2)}) %collective-permute-start.5) | collective-permute-done | bytes 73760 | tf_op jit(solution)/shard_map/ppermute | solution.py:364
  18.2 1.6 %collective-permute-start.6 = (bf16[1,144,128]{2,1,0:T(8,128)(2,1)S(1)}, bf16[1,144,128]{2,1,0:T(8,128)(2,1)S(1)}, u32[]{:S(2)}, u32[]{:S(2)}) collective-permute-start(bf16[1,144,128]{2,1,0:T(8,128)(2,1)S(1)} %constant_dynamic-slice_fusion), channel_id=1, source_target_pairs={{0,8},{4,12},{8,0},{12,4},{16,24},{20,28},{24,16},{28,20},{1,9},{5... | collective-permute-start | bytes 110600 | tf_op jit(solution)/shard_map/ppermute | solution.py:370
  19.8 2.4 %collective-permute-done.6 = bf16[1,144,128]{2,1,0:T(8,128)(2,1)S(1)} collective-permute-done((bf16[1,144,128]{2,1,0:T(8,128)(2,1)S(1)}, bf16[1,144,128]{2,1,0:T(8,128)(2,1)S(1)}, u32[]{:S(2)}, u32[]{:S(2)}) %collective-permute-start.6) | collective-permute-done | bytes 36896 | tf_op jit(solution)/shard_map/ppermute | solution.py:370
  22.3 1.6 %collective-permute-start.7 = (bf16[144,128]{1,0:T(8,128)(2,1)S(1)}, bf16[144,128]{1,0:T(8,128)(2,1)S(1)}, u32[]{:S(2)}, u32[]{:S(2)}) collective-permute-start(bf16[144,128]{1,0:T(8,128)(2,1)S(1)} %fusion.refs_0_), channel_id=1, source_target_pairs={{0,1},{1,0},{2,3},{3,2},{4,5},{5,4},{6,7},{7,6},{8,9},{9,8},{10,11... | collective-permute-start | bytes 110600 | tf_op jit(solution)/shard_map/ppermute | solution.py:379
  23.9 2.4 %collective-permute-done.7.refs_1_ = bf16[144,128]{1,0:T(8,128)(2,1)S(1)} collective-permute-done((bf16[144,128]{1,0:T(8,128)(2,1)S(1)}, bf16[144,128]{1,0:T(8,128)(2,1)S(1)}, u32[]{:S(2)}, u32[]{:S(2)}) %collective-permute-start.7) | collective-permute-done | bytes 36896 | tf_op jit(solution)/shard_map/ppermute | solution.py:379
  26.3 0.8 %shard_map.62 = (f32[32,108]{1,0:T(8,128)}, f32[64,216]{1,0:T(8,128)}) custom-call(bf16[144,128]{1,0:T(8,128)(2,1)S(1)} %fusion.refs_0_, bf16[144,128]{1,0:T(8,128)(2,1)S(1)} %collective-permute-done.7.refs_1_), custom_call_target="tpu_custom_call" | custom-call | tf_op jit(solution)/shard_map/pallas_call | solution.py:383
  (7 shorter events, 0.1 us)
Async XLA Ops:
  0.6 13.9 %copy-start = (bf16[1728,128]{1,0:T(8,128)(2,1)S(1)}, bf16[1728,128]{1,0:T(8,128)(2,1)}, u32[]{:S(2)}) copy-start(bf16[1728,128]{1,0:T(8,128)(2,1)} %refs_7_.1) | copy-start | bytes 1327108
  1.6 8.6 %collective-permute-start.1 = (bf16[2,9,8,256]{3,2,1,0:T(8,128)(2,1)S(1)}, bf16[2,9,8,256]{3,2,1,0:T(8,128)(2,1)S(1)}, u32[]{:S(2)}, u32[]{:S(2)}) collective-permute-start(bf16[2,9,8,256]{3,2,1,0:T(8,128)(2,1)S(1)} %get-tuple-element.15), channel_id=1, source_target_pairs={{0,24},{2,30},{4,28},{6,26},{8,16},{10,22},{12,20},{14,18},{16,8},... | collective-permute-start | bytes 221192 | tf_op jit(solution)/shard_map/ppermute | solution.py:339
  6.7 6.4 %collective-permute-start = (bf16[2,9,8,256]{3,2,1,0:T(8,128)(2,1)S(1)}, bf16[2,9,8,256]{3,2,1,0:T(8,128)(2,1)S(1)}, u32[]{:S(2)}, u32[]{:S(2)}) collective-permute-start(bf16[2,9,8,256]{3,2,1,0:T(8,128)(2,1)S(1)} %get-tuple-element.14), channel_id=1, source_target_pairs={{0,8},{2,14},{4,12},{6,10},{8,0},{10,6},{12,4},{14,2},{16,24},{18,... | collective-permute-start | bytes 221192 | tf_op jit(solution)/shard_map/ppermute | solution.py:339
  6.7 6.4 %collective-permute-start.2 = (bf16[2,9,8,256]{3,2,1,0:T(8,128)(2,1)S(1)}, bf16[2,9,8,256]{3,2,1,0:T(8,128)(2,1)S(1)}, u32[]{:S(2)}, u32[]{:S(2)}) collective-permute-start(bf16[2,9,8,256]{3,2,1,0:T(8,128)(2,1)S(1)} %get-tuple-element.16), channel_id=1, source_target_pairs={{0,16},{2,22},{4,20},{6,18},{8,24},{10,30},{12,28},{14,26},{16,0},... | collective-permute-start | bytes 221192 | tf_op jit(solution)/shard_map/ppermute | solution.py:339
  7.4 5.8 %collective-permute-start.3 = (bf16[9,8,256]{2,1,0:T(8,128)(2,1)S(1)}, bf16[9,8,256]{2,1,0:T(8,128)(2,1)S(1)}, u32[]{:S(2)}, u32[]{:S(2)}) collective-permute-start(bf16[9,8,256]{2,1,0:T(8,128)(2,1)S(1)} %get-tuple-element.13.refs_0_), channel_id=1, source_target_pairs={{0,4},{4,0},{8,12},{12,8},{16,20},{20,16},{24,28},{28,24},{1,5},{5... | collective-permute-start | bytes 110600 | tf_op jit(solution)/shard_map/ppermute | solution.py:340
  9.0 0.9 %copy-start.1 = (bf16[864,64]{0,1:T(8,128)(2,1)S(1)}, bf16[864,64]{0,1:T(8,128)(2,1)}, u32[]{:S(2)}) copy-start(bf16[864,64]{0,1:T(8,128)(2,1)} %param.5) | copy-start | bytes 331780
  13.2 1.4 %collective-permute-start.4 = (bf16[27,8,256]{2,1,0:T(8,128)(2,1)S(1)}, bf16[27,8,256]{2,1,0:T(8,128)(2,1)S(1)}, u32[]{:S(2)}, u32[]{:S(2)}) collective-permute-start(bf16[27,8,256]{2,1,0:T(8,128)(2,1)S(1)} %pad_maximum_fusion), channel_id=1, source_target_pairs={{0,2},{2,0},{1,3},{3,1},{4,6},{6,4},{5,7},{7,5},{8,10},{10,8},{9,1... | collective-permute-start | bytes 331784 | tf_op jit(solution)/shard_map/ppermute | solution.py:344
  16.8 1.3 %collective-permute-start.5 = (bf16[2,144,128]{2,1,0:T(8,128)(2,1)S(1)}, bf16[2,144,128]{2,1,0:T(8,128)(2,1)S(1)}, u32[]{:S(2)}, u32[]{:S(2)}) collective-permute-start(bf16[2,144,128]{2,1,0:T(8,128)(2,1)S(1)} %get-tuple-element.21), channel_id=1, source_target_pairs={{0,2},{2,0},{1,3},{3,1},{4,6},{6,4},{5,7},{7,5},{8,10},{10,8},{9,1... | collective-permute-start | bytes 221192 | tf_op jit(solution)/shard_map/ppermute | solution.py:364
  18.2 4.0 %collective-permute-start.6 = (bf16[1,144,128]{2,1,0:T(8,128)(2,1)S(1)}, bf16[1,144,128]{2,1,0:T(8,128)(2,1)S(1)}, u32[]{:S(2)}, u32[]{:S(2)}) collective-permute-start(bf16[1,144,128]{2,1,0:T(8,128)(2,1)S(1)} %constant_dynamic-slice_fusion), channel_id=1, source_target_pairs={{0,8},{4,12},{8,0},{12,4},{16,24},{20,28},{24,16},{28,20},{1,9},{5... | collective-permute-start | bytes 110600 | tf_op jit(solution)/shard_map/ppermute | solution.py:370
  22.3 4.0 %collective-permute-start.7 = (bf16[144,128]{1,0:T(8,128)(2,1)S(1)}, bf16[144,128]{1,0:T(8,128)(2,1)S(1)}, u32[]{:S(2)}, u32[]{:S(2)}) collective-permute-start(bf16[144,128]{1,0:T(8,128)(2,1)S(1)} %fusion.refs_0_), channel_id=1, source_target_pairs={{0,1},{1,0},{2,3},{3,2},{4,5},{5,4},{6,7},{7,6},{8,9},{9,8},{10,11... | collective-permute-start | bytes 110600 | tf_op jit(solution)/shard_map/ppermute | solution.py:379

commit v7 on v6

--- a/solution.py
+++ b/solution.py
@@ -72,7 +72,6 @@
 def cut_body(pairs, field_hbm, upstream_hbm, *refs):
     *outs, field, upstream, sems = refs
     pair = lax.axis_index("space") // 2
-    section = lax.axis_index("section")
     copies = [
         pltpu.make_async_copy(field_hbm.at[0], field.at[0], sems.at[0]),
         pltpu.make_async_copy(field_hbm.at[1], field.at[1], sems.at[1]),
@@ -95,19 +94,19 @@
         else:
             out[pl.ds(8, pairs // 4)] = jnp.zeros((pairs // 4, 8, 256), BF16)
 
-    fill(outs[0], 0, section)
-    for k in range(1, pairs):
+    for k in range(pairs):
         for micro in range(2):
             fill(outs[k].at[micro], k, micro)
+    outs[pairs][...] = outs[0][lax.axis_index("section")]
 
 
 def main_body(pairs, spread, mine, partner, *refs):
     received = refs[: pairs - 1]
-    swapped, banded, second, keep, send, xf, hid, hgs, us, t2, t1 = refs[pairs - 1 :]
+    swapped, banded, second, keep, xf, hid, hgs, us, t2, t1 = refs[pairs - 1 :]
     space = lax.axis_index("space")
     side, pair = space % 2, space // 2
     section = lax.axis_index("section")
-    width = 4
+    width = 8
     tail = pairs // 4
     base = width * 8 + 8
     total = 2 * pairs * width * 8
@@ -118,28 +117,41 @@
     def place(load, k, at_side):
         there = pair ^ k
         start = pl.multiple_of(base + (2 * there + at_side) * (width * 8), 8)
-        for i in range(2):
-            tiles = load(i * width, width).reshape(width * 8, 256).astype(F32)
-            for h in range(2):
-                xf[i, h, pl.ds(start, width * 8), :] = tiles[:, h * 128 : h * 128 + 128]
-        if k in (0, pairs - 1):
-            rows = load(2 * width, tail).reshape(2 * pairs, 256).astype(F32)
-            volume = 2 * (there // (pairs // 2)) + at_side
-            for j in range(2):
+        for micro in range(2):
+            for i in range(2):
+                tiles = load(micro, i * 4, 4).reshape(32, 256).astype(F32)
                 for h in range(2):
-                    us[h, pl.ds(2 * volume + j, pairs, stride=2 * width), :] = rows[
-                        j * pairs : j * pairs + pairs, h * 128 : h * 128 + 128
-                    ]
-
-    place(lambda at, size: mine[pl.ds(at, size)], 0, side)
-    place(lambda at, size: partner[pl.ds(at, size)], 0, 1 - side)
+                    xf[i, h, pl.ds(start + micro * 32, 32), :] = tiles[:, h * 128 : h * 128 + 128]
+            if k in (0, pairs - 1):
+                rows = load(micro, 8, tail).reshape(2 * pairs, 256).astype(F32)
+                volume = 4 * micro + 2 * (there // (pairs // 2)) + at_side
+                for j in range(2):
+                    for h in range(2):
+                        us[h, pl.ds(2 * volume + j, pairs, stride=2 * width), :] = rows[
+                            j * pairs : j * pairs + pairs, h * 128 : h * 128 + 128
+                        ]
+
+    place(lambda micro, at, size: mine[micro, pl.ds(at, size)], 0, side)
+    size_of = mine.shape[1]
+    last = 2 * size_of * (pairs - 1)
+    place(
+        lambda micro, at, size: jnp.where(
+            section == micro, partner[pl.ds(at, size)], swapped[pl.ds(last + at, size)]
+        ),
+        0,
+        1 - side,
+    )
     offset = 0
     for k in swap_order(pairs):
         ref = received[k - 1]
-        place(lambda at, size: ref[section, pl.ds(at, size)], k, side ^ section)
+        place(lambda micro, at, size: ref[micro, pl.ds(at, size)], k, side ^ section)
         start = offset
-        place(lambda at, size: swapped[pl.ds(start + at, size)], k, 1 - (side ^ section))
-        offset += ref.shape[1]
+        place(
+            lambda micro, at, size: swapped[pl.ds(start + micro * size_of + at, size)],
+            k,
+            1 - (side ^ section),
+        )
+        offset += 2 * size_of
 
     rows = total // 2
     row = lax.broadcasted_iota(jnp.int32, (rows, 256), 0)
@@ -189,7 +201,9 @@
     up = jnp.concatenate([us[0], us[1]], axis=0)
     delta = leaky(out, up)
     delta_b = delta.astype(BF16)
-    turned = jnp.where(section == 0, delta, pltpu.roll(delta, 64, 1)).astype(BF16)
+    other = pltpu.roll(delta, 64, 1)
+    low3 = lax.broadcasted_iota(jnp.int32, (2 * half, 128), 1) < CB
+    turned = jnp.where(low3 == (section == 0), delta, other).astype(BF16)
     for tap in range(9):
         t2[pl.ds(tap * 192, 192), :] = contract(cols[tap], turned, 0, 0)
     row3 = lax.broadcasted_iota(jnp.int32, (2 * half, 128), 0)
@@ -227,16 +241,20 @@
         axis=1,
     )
     hidden_grad = hidden_grad.astype(BF16).astype(F32)
-    delta_a = leaky(hidden, hidden_grad).astype(BF16)
-    wide = lax.broadcasted_iota(jnp.int32, (96, 128), 1) < CB
+    delta_a = leaky(hidden, hidden_grad)
+    quarters = lax.broadcasted_iota(jnp.int32, (rows, 128), 1) // 32
+    even, late = delta_a[:, :128], delta_a[:, 128:]
+    even = jnp.where(section == 0, even, pltpu.roll(even, 96, 1))
+    late = jnp.where(section == 0, pltpu.roll(late, 32, 1), late)
+    delta_a = jnp.where(quarters % 2 == 0, even, late).astype(BF16)
+    quarter = lax.broadcasted_iota(jnp.int32, (96, 128), 1) // 32
     for tap in range(9):
         grid = contract(columns[tap], delta_a, 0, 0)
-        g0, g1 = grid[:, :128], grid[:, 128:]
-        left = jnp.concatenate([g1[96:128], g0[0:64] + g1[128:192]], axis=0)
-        right = g0[32:128] + g1[160:256]
-        fold = jnp.where(wide, left, right)
+        fold = jnp.concatenate([jnp.zeros((32, 128), F32), grid[0:64]], axis=0)
+        for q, k in ((1, 2), (2, 1), (3, 3)):
+            fold = jnp.where(quarter == q, grid[64 * k - 32 : 64 * k + 64], fold)
         fold = fold + pltpu.roll(fold, 64, 1)
-        t1[pl.ds(tap * 96, 96), :] = jnp.where(section == 0, fold, pltpu.roll(fold, 32, 1))
+        t1[pl.ds(tap * 96, 96), :] = fold + pltpu.roll(fold, 32, 1)
     r2, r1 = TAPS * CB // spread, TAPS * CA // spread
     h2, h1 = packed_rows(spread)
     t2[pl.ds(TAPS * CB, t2.shape[0] - TAPS * CB), :] = jnp.zeros((t2.shape[0] - TAPS * CB, 128), F32)
@@ -258,21 +276,15 @@
     for n in range(pairs // 2):
         a = block(t2, n, r2, 0, h2)
         b = block(t2, n, r2, h2, h2)
-        keep[n, 0:h2, :] = jnp.where(low2, a, pltpu.roll(b, 64, 1)).astype(BF16)
-        send[n, 0:h2, :] = jnp.where(low2, pltpu.roll(a, 64, 1), b).astype(BF16)
-        kept, sent = None, None
-        for g in range(4):
-            straight = block(t1, n, r1, g * h1, h1)
-            turn = pltpu.roll(straight, 32, 1)
-            k, o = (straight, turn) if g % 2 == 0 else (turn, straight)
-            kept = k if g == 0 else jnp.where(quarter == g, k, kept)
-            sent = o if g == 0 else jnp.where(quarter == g, o, sent)
+        keep[n, 0:h2, :] = jnp.where(low2, a, b).astype(BF16)
+        kept = block(t1, n, r1, 0, h1)
+        for g in range(1, 4):
+            kept = jnp.where(quarter == g, block(t1, n, r1, g * h1, h1), kept)
         keep[n, h2 : h2 + h1, :] = kept.astype(BF16)
-        send[n, h2 : h2 + h1, :] = sent.astype(BF16)
 
 
 def swap_order(pairs):
-    return [1, 3, 2] if pairs == 4 else [*range(1, pairs)]
+    return [*range(2, 0, -1), *range(3, pairs)]
 
 
 def packed_rows(spread):
@@ -310,18 +322,17 @@
     pairs = spread // 2
     tail = pairs // 4
     pair = lax.axis_index("space") // 2
-    section = lax.axis_index("section")
-
-    piece = lambda k: 8 + tail
+
     hbm = pl.BlockSpec(memory_space=pltpu.HBM)
     pieces = pl.pallas_call(
         lambda *refs: cut_body(pairs, *refs),
         out_shape=[
-            jax.ShapeDtypeStruct(((2,) if k > 0 else ()) + (piece(k), 8, 256), BF16)
+            jax.ShapeDtypeStruct((2, 8 + tail, 8, 256), BF16)
             for k in range(pairs)
-        ],
+        ]
+        + [jax.ShapeDtypeStruct((8 + tail, 8, 256), BF16)],
         in_specs=[hbm, hbm],
-        out_specs=[pl.BlockSpec(memory_space=pltpu.VMEM)] * pairs,
+        out_specs=[pl.BlockSpec(memory_space=pltpu.VMEM)] * (pairs + 1),
         scratch_shapes=[
             pltpu.VMEM(input_field.shape, BF16),
             pltpu.VMEM(upstream_grad.shape, BF16),
@@ -337,21 +348,20 @@
     for k in range(1, pairs):
         route = [(2 * d + c, 2 * (d ^ (2 * k) ^ c) + c) for d in range(spread) for c in range(2)]
         received[k - 1] = lax.ppermute(pieces[k], ("space", "section"), route)
-    partner = lax.ppermute(mine, "space", swap_bit(spread, 0))
+    partner = lax.ppermute(pieces[pairs], "space", swap_bit(spread, 0))
     banded = call(banded_body, jax.ShapeDtypeStruct((9 * 256, 256), BF16), [], (first_weight.T,))
-    outgoing = jnp.concatenate([pick(received[k - 1], 1 - section, 0) for k in swap_order(pairs)])
-    outgoing, partner, banded = lax.optimization_barrier((outgoing, partner, banded))
+    outgoing = [received[k - 1].reshape(-1, 8, 256) for k in swap_order(pairs)] + [partner]
+    outgoing, partner, banded = lax.optimization_barrier((jnp.concatenate(outgoing), partner, banded))
     swapped = lax.ppermute(outgoing, "section", swap_bit(2, 0))
     h2, h1 = packed_rows(spread)
-    block = jax.ShapeDtypeStruct((pairs // 2, h2 + h1, 128), BF16)
-    kept, outgoing = call(
+    total = call(
         lambda *refs: main_body(pairs, spread, *refs),
-        [block, block],
+        jax.ShapeDtypeStruct((pairs // 2, h2 + h1, 128), BF16),
         [
-            pltpu.VMEM((2, 2, (2 * pairs + 1) * 32 + 16, 128), F32),
-            pltpu.VMEM((2, 2, (pairs + 1) * 16 + 16, 128), F32),
-            pltpu.VMEM((2, 2, pairs * 16, 128), F32),
-            pltpu.VMEM((2, pairs * 8, 128), F32),
+            pltpu.VMEM((2, 2, (2 * pairs + 1) * 64 + 16, 128), F32),
+            pltpu.VMEM((2, 2, (pairs + 1) * 32 + 16, 128), F32),
+            pltpu.VMEM((2, 2, pairs * 32, 128), F32),
+            pltpu.VMEM((2, pairs * 16, 128), F32),
             pltpu.VMEM((TAPS * CB + 2 * h2, 128), F32),
             pltpu.VMEM((TAPS * CA + 4 * h1, 128), F32),
         ],
@@ -361,7 +371,6 @@
     def added(a, b):
         return (a.astype(F32) + b.astype(F32)).astype(BF16)
 
-    total = added(kept, lax.ppermute(outgoing, "section", swap_bit(2, 0)))
     bit = 0
     while total.shape[0] > 1:
         paired = total.reshape(total.shape[0] // 2, 2, *total.shape[1:])

time: 27.3 us -> 26.7 us (0.978)
  waiting for transfers between devices: 10.1 us -> 9.12 us
  Pallas kernels: 4.39 us -> 4.98 us
    ppermute x3, waiting for transfers between devices: 2.85 us -> 0.02 us  [shards(): received[k - 1] = lax.ppermute(pieces[k], ('space', 'section'), route)]
    ppermute x2 -> x1, waiting for transfers between devices: 1.11 us -> 2.85 us  [shards(): partner = lax.ppermute(pieces[pairs], 'space', swap_bit(spread, 0))]
    pallas_call x2, Pallas kernels: 2.59 us -> 3.17 us  [call(): pl.pallas_call(body, out_shape=out_shape, in_specs=[vmem] * len(args), ou...]
    ppermute x2 -> x1, starting transfers between devices: 1.86 us -> 1.64 us  [shards(): partner = lax.ppermute(pieces[pairs], 'space', swap_bit(spread, 0))]
  transfers between devices with their start and end apart: 8 -> 7, of which waited for: 5 -> 4; matrix products, arithmetic and copies ran while one was open for 0% -> 0% of each run, Pallas kernels for 1% -> 1%
where the time goes in v7:
time: 26.7 us; the launch traced here: 26.5 us
  starting transfers between devices  10.8 us (40%)
  waiting for transfers between devices  9.12 us (34%)
  Pallas kernels  4.98 us (19%)
  local copies, waits for them, and re-layouts  0.91 us (3%)
  between operations  0.68 us (3%)
    ppermute x3, starting transfers between devices, shards(): received[k - 1] = lax.ppermute(pieces[k], ('space', 'section'), route)  5.75 us
    pallas_call x2, Pallas kernels, call(): pl.pallas_call(body, out_shape=out_shape, in_specs=[vmem] * len(args), ou...  3.17 us
    ppermute x1, waiting for transfers between devices, shards(): partner = lax.ppermute(pieces[pairs], 'space', swap_bit(spread, 0))  2.85 us
    ppermute x1, waiting for transfers between devices, shards(): came = lax.ppermute(total, 'dp', swap_bit(replicas, bit))  2.42 us
    ppermute x1, waiting for transfers between devices, shards(): lax.ppermute(pick(paired, 1 - here, 1), 'space', swap_bit(spread, bit + 1))  2.4 us
    ppermute x1, starting transfers between devices, shards(): partner = lax.ppermute(pieces[pairs], 'space', swap_bit(spread, 0))  1.64 us
    ppermute x1, starting transfers between devices, shards(): lax.ppermute(pick(paired, 1 - here, 1), 'space', swap_bit(spread, bit + 1))  1.62 us
    ppermute x1, starting transfers between devices, shards(): came = lax.ppermute(total, 'dp', swap_bit(replicas, bit))  1.6 us
  transfers between devices with their start and end apart: 7, of which 4 were waited for; matrix products, arithmetic and copies ran while one was open for 0% of the time, Pallas kernels for 1%

profile of v7, /device:TPU:0, one launch (start us, length us, event | category | flops | bytes accessed | tf_op | source)
XLA Modules:
  0.0 26.5 jit_solution(4982101583480066545)
XLA Ops:
  0.6 0.0 copy-start
  0.6 1.0 %shard_map.59 = (bf16[2,9,8,256]{3,2,1,0:T(8,128)(2,1)S(1)}, bf16[2,9,8,256]{3,2,1,0:T(8,128)(2,1)S(1)}, bf16[2,9,8,256]{3,2,1,0:T(8,128)(2,1)S(1)}, bf16[2,9,8,...) custom-call(bf16[2,1,2,8,8,256]{5,4,3,2,1,0:T(8,128)(2,1)} %refs_0_.1, bf16[2,1,4,1,2,256]{5,4,3,2,1,0:T(2,128)(2,1)} %refs_1_.1), custom_call_target="tpu_custom_call" | custom-call | tf_op jit(solution)/shard_map/pallas_call | solution.py:327
  1.6 5.1 %collective-permute-start.2 = (bf16[2,9,8,256]{3,2,1,0:T(8,128)(2,1)S(1)}, bf16[2,9,8,256]{3,2,1,0:T(8,128)(2,1)S(1)}, u32[]{:S(2)}, u32[]{:S(2)}) collective-permute-start(bf16[2,9,8,256]{3,2,1,0:T(8,128)(2,1)S(1)} %get-tuple-element.15), channel_id=1, source_target_pairs={{0,24},{2,30},{4,28},{6,26},{8,16},{10,22},{12,20},{14,18},{16,8},... | collective-permute-start | bytes 221192 | tf_op jit(solution)/shard_map/ppermute | solution.py:350
  6.7 0.0 collective-permute-start.1
  6.7 0.6 %collective-permute-start = (bf16[2,9,8,256]{3,2,1,0:T(8,128)(2,1)S(1)}, bf16[2,9,8,256]{3,2,1,0:T(8,128)(2,1)S(1)}, u32[]{:S(2)}, u32[]{:S(2)}) collective-permute-start(bf16[2,9,8,256]{3,2,1,0:T(8,128)(2,1)S(1)} %get-tuple-element.13), channel_id=1, source_target_pairs={{0,16},{2,22},{4,20},{6,18},{8,24},{10,30},{12,28},{14,26},{16,0},... | collective-permute-start | bytes 221192 | tf_op jit(solution)/shard_map/ppermute | solution.py:350
  7.4 1.6 %collective-permute-start.3 = (bf16[9,8,256]{2,1,0:T(8,128)(2,1)S(1)}, bf16[9,8,256]{2,1,0:T(8,128)(2,1)S(1)}, u32[]{:S(2)}, u32[]{:S(2)}) collective-permute-start(bf16[9,8,256]{2,1,0:T(8,128)(2,1)S(1)} %get-tuple-element.16), channel_id=1, source_target_pairs={{0,4},{4,0},{8,12},{12,8},{16,20},{20,16},{24,28},{28,24},{1,5},{5... | collective-permute-start | bytes 110600 | tf_op jit(solution)/shard_map/ppermute | solution.py:351
  9.0 0.0 copy-start.1
  9.0 0.9 %copy-done.1 = bf16[864,64]{0,1:T(8,128)(2,1)S(1)} copy-done((bf16[864,64]{0,1:T(8,128)(2,1)S(1)}, bf16[864,64]{0,1:T(8,128)(2,1)}, u32[]{:S(2)}) %copy-start.1) | copy-done | bytes 110616
  9.9 0.3 %shard_map.60.refs_6_ = bf16[2304,256]{1,0:T(8,128)(2,1)S(1)} custom-call(bf16[64,864]{1,0:T(8,128)(2,1)S(1)} %bitcast.11), custom_call_target="tpu_custom_call" | custom-call | tf_op jit(solution)/shard_map/pallas_call | solution.py:32
  10.3 2.9 %collective-permute-done.3.refs_1_ = bf16[9,8,256]{2,1,0:T(8,128)(2,1)S(1)} collective-permute-done((bf16[9,8,256]{2,1,0:T(8,128)(2,1)S(1)}, bf16[9,8,256]{2,1,0:T(8,128)(2,1)S(1)}, u32[]{:S(2)}, u32[]{:S(2)}) %collective-permute-start.3) | collective-permute-done | bytes 36896 | tf_op jit(solution)/shard_map/ppermute | solution.py:351
  13.1 0.0 collective-permute-done.2.refs_4_
  13.1 0.0 collective-permute-done.1.refs_2_
  13.1 0.0 collective-permute-done.refs_3_
  13.2 0.2 collective-permute-start.4
  13.4 1.4 %collective-permute-done.4.refs_5_ = bf16[63,8,256]{2,1,0:T(8,128)(2,1)S(1)} collective-permute-done((bf16[63,8,256]{2,1,0:T(8,128)(2,1)S(1)}, bf16[63,8,256]{2,1,0:T(8,128)(2,1)S(1)}, u32[]{:S(2)}, u32[]{:S(2)}) %collective-permute-start.4) | collective-permute-done | bytes 258080 | tf_op jit(solution)/shard_map/ppermute | solution.py:355
  14.8 0.0 copy-done
  14.8 2.9 %shard_map.61 = bf16[2,144,128]{2,1,0:T(8,128)(2,1)S(1)} custom-call(bf16[2,9,8,256]{3,2,1,0:T(8,128)(2,1)S(1)} %get-tuple-element.12.refs_0_, bf16[9,8,256]{2,1,0:T(8,128)(2,1)S(1)} %collective-permute-done.3.refs_1_, bf16[2,9,8,256]{3,2,1,0:T(8,128)(2,1)S(1)} %collective-permute-done.1.refs_2_, bf16[2,9,8,256]{3,2,1,0:T(8,128)(2,1)S(1)} %collective-permute-done.refs_3_, ...), custom_call_target="tpu_custom_call" | custom-call | tf_op jit(solution)/shard_map/pallas_call | solution.py:32
  17.6 1.6 %collective-permute-start.5 = (bf16[1,144,128]{2,1,0:T(8,128)(2,1)S(1)}, bf16[1,144,128]{2,1,0:T(8,128)(2,1)S(1)}, u32[]{:S(2)}, u32[]{:S(2)}) collective-permute-start(bf16[1,144,128]{2,1,0:T(8,128)(2,1)S(1)} %constant_dynamic-slice_fusion), channel_id=1, source_target_pairs={{0,8},{4,12},{8,0},{12,4},{16,24},{20,28},{24,16},{28,20},{1,9},{5... | collective-permute-start | bytes 110600 | tf_op jit(solution)/shard_map/ppermute | solution.py:379
  19.3 2.4 %collective-permute-done.5 = bf16[1,144,128]{2,1,0:T(8,128)(2,1)S(1)} collective-permute-done((bf16[1,144,128]{2,1,0:T(8,128)(2,1)S(1)}, bf16[1,144,128]{2,1,0:T(8,128)(2,1)S(1)}, u32[]{:S(2)}, u32[]{:S(2)}) %collective-permute-start.5) | collective-permute-done | bytes 36896 | tf_op jit(solution)/shard_map/ppermute | solution.py:379
  21.7 1.6 %collective-permute-start.6 = (bf16[144,128]{1,0:T(8,128)(2,1)S(1)}, bf16[144,128]{1,0:T(8,128)(2,1)S(1)}, u32[]{:S(2)}, u32[]{:S(2)}) collective-permute-start(bf16[144,128]{1,0:T(8,128)(2,1)S(1)} %fusion.refs_0_), channel_id=1, source_target_pairs={{0,1},{1,0},{2,3},{3,2},{4,5},{5,4},{6,7},{7,6},{8,9},{9,8},{10,11... | collective-permute-start | bytes 110600 | tf_op jit(solution)/shard_map/ppermute | solution.py:388
  23.3 2.4 %collective-permute-done.6.refs_1_ = bf16[144,128]{1,0:T(8,128)(2,1)S(1)} collective-permute-done((bf16[144,128]{1,0:T(8,128)(2,1)S(1)}, bf16[144,128]{1,0:T(8,128)(2,1)S(1)}, u32[]{:S(2)}, u32[]{:S(2)}) %collective-permute-start.6) | collective-permute-done | bytes 36896 | tf_op jit(solution)/shard_map/ppermute | solution.py:388
  25.7 0.8 %shard_map.62 = (f32[32,108]{1,0:T(8,128)}, f32[64,216]{1,0:T(8,128)}) custom-call(bf16[144,128]{1,0:T(8,128)(2,1)S(1)} %fusion.refs_0_, bf16[144,128]{1,0:T(8,128)(2,1)S(1)} %collective-permute-done.6.refs_1_), custom_call_target="tpu_custom_call" | custom-call | tf_op jit(solution)/shard_map/pallas_call | solution.py:392
  (3 shorter events, 0.1 us)
Async XLA Ops:
  0.6 14.1 %copy-start = (bf16[1728,128]{1,0:T(8,128)(2,1)S(1)}, bf16[1728,128]{1,0:T(8,128)(2,1)}, u32[]{:S(2)}) copy-start(bf16[1728,128]{1,0:T(8,128)(2,1)} %refs_7_.1) | copy-start | bytes 1327108
  1.6 11.5 %collective-permute-start.2 = (bf16[2,9,8,256]{3,2,1,0:T(8,128)(2,1)S(1)}, bf16[2,9,8,256]{3,2,1,0:T(8,128)(2,1)S(1)}, u32[]{:S(2)}, u32[]{:S(2)}) collective-permute-start(bf16[2,9,8,256]{3,2,1,0:T(8,128)(2,1)S(1)} %get-tuple-element.15), channel_id=1, source_target_pairs={{0,24},{2,30},{4,28},{6,26},{8,16},{10,22},{12,20},{14,18},{16,8},... | collective-permute-start | bytes 221192 | tf_op jit(solution)/shard_map/ppermute | solution.py:350
  6.7 6.4 %collective-permute-start.1 = (bf16[2,9,8,256]{3,2,1,0:T(8,128)(2,1)S(1)}, bf16[2,9,8,256]{3,2,1,0:T(8,128)(2,1)S(1)}, u32[]{:S(2)}, u32[]{:S(2)}) collective-permute-start(bf16[2,9,8,256]{3,2,1,0:T(8,128)(2,1)S(1)} %get-tuple-element.14), channel_id=1, source_target_pairs={{0,8},{2,14},{4,12},{6,10},{8,0},{10,6},{12,4},{14,2},{16,24},{18,... | collective-permute-start | bytes 221192 | tf_op jit(solution)/shard_map/ppermute | solution.py:350
  6.7 6.4 %collective-permute-start = (bf16[2,9,8,256]{3,2,1,0:T(8,128)(2,1)S(1)}, bf16[2,9,8,256]{3,2,1,0:T(8,128)(2,1)S(1)}, u32[]{:S(2)}, u32[]{:S(2)}) collective-permute-start(bf16[2,9,8,256]{3,2,1,0:T(8,128)(2,1)S(1)} %get-tuple-element.13), channel_id=1, source_target_pairs={{0,16},{2,22},{4,20},{6,18},{8,24},{10,30},{12,28},{14,26},{16,0},... | collective-permute-start | bytes 221192 | tf_op jit(solution)/shard_map/ppermute | solution.py:350
  7.4 5.7 %collective-permute-start.3 = (bf16[9,8,256]{2,1,0:T(8,128)(2,1)S(1)}, bf16[9,8,256]{2,1,0:T(8,128)(2,1)S(1)}, u32[]{:S(2)}, u32[]{:S(2)}) collective-permute-start(bf16[9,8,256]{2,1,0:T(8,128)(2,1)S(1)} %get-tuple-element.16), channel_id=1, source_target_pairs={{0,4},{4,0},{8,12},{12,8},{16,20},{20,16},{24,28},{28,24},{1,5},{5... | collective-permute-start | bytes 110600 | tf_op jit(solution)/shard_map/ppermute | solution.py:351
  9.0 0.9 %copy-start.1 = (bf16[864,64]{0,1:T(8,128)(2,1)S(1)}, bf16[864,64]{0,1:T(8,128)(2,1)}, u32[]{:S(2)}) copy-start(bf16[864,64]{0,1:T(8,128)(2,1)} %param.5) | copy-start | bytes 331780
  13.2 1.6 %collective-permute-start.4 = (bf16[63,8,256]{2,1,0:T(8,128)(2,1)S(1)}, bf16[63,8,256]{2,1,0:T(8,128)(2,1)S(1)}, u32[]{:S(2)}, u32[]{:S(2)}) collective-permute-start(bf16[63,8,256]{2,1,0:T(8,128)(2,1)S(1)} %pad_maximum_fusion), channel_id=1, source_target_pairs={{0,2},{2,0},{1,3},{3,1},{4,6},{6,4},{5,7},{7,5},{8,10},{10,8},{9,1... | collective-permute-start | bytes 774152 | tf_op jit(solution)/shard_map/ppermute | solution.py:355
  17.6 4.0 %collective-permute-start.5 = (bf16[1,144,128]{2,1,0:T(8,128)(2,1)S(1)}, bf16[1,144,128]{2,1,0:T(8,128)(2,1)S(1)}, u32[]{:S(2)}, u32[]{:S(2)}) collective-permute-start(bf16[1,144,128]{2,1,0:T(8,128)(2,1)S(1)} %constant_dynamic-slice_fusion), channel_id=1, source_target_pairs={{0,8},{4,12},{8,0},{12,4},{16,24},{20,28},{24,16},{28,20},{1,9},{5... | collective-permute-start | bytes 110600 | tf_op jit(solution)/shard_map/ppermute | solution.py:379
  21.7 4.0 %collective-permute-start.6 = (bf16[144,128]{1,0:T(8,128)(2,1)S(1)}, bf16[144,128]{1,0:T(8,128)(2,1)S(1)}, u32[]{:S(2)}, u32[]{:S(2)}) collective-permute-start(bf16[144,128]{1,0:T(8,128)(2,1)S(1)} %fusion.refs_0_), channel_id=1, source_target_pairs={{0,1},{1,0},{2,3},{3,2},{4,5},{5,4},{6,7},{7,6},{8,9},{9,8},{10,11... | collective-permute-start | bytes 110600 | tf_op jit(solution)/shard_map/ppermute | solution.py:388

commit v8 on v7

--- a/solution.py
+++ b/solution.py
@@ -39,7 +39,11 @@
     )(*args)
 
 
-def banded_body(weight, banded):
+def weights_body(weight, second, banded, ordered):
+    for tap in range(9):
+        ordered[pl.ds(tap * 128, 128), :] = second[pl.ds(tap * 192, 128), :]
+        ordered[pl.ds(1152 + tap * CB, CB), :] = second[pl.ds(tap * 192 + 128, CB), :]
+    ordered[pl.ds(1152 + 9 * CB, CB), :] = jnp.zeros((CB, CC), BF16)
     lane = lax.broadcasted_iota(jnp.int32, (CA, 2 * CB), 1)
     zero = jnp.zeros((CA, 2 * CB), F32)
     turned = weight[...].astype(F32).T
@@ -73,10 +77,11 @@
     *outs, field, upstream, sems = refs
     pair = lax.axis_index("space") // 2
     copies = [
-        pltpu.make_async_copy(field_hbm.at[0], field.at[0], sems.at[0]),
-        pltpu.make_async_copy(field_hbm.at[1], field.at[1], sems.at[1]),
-        pltpu.make_async_copy(upstream_hbm, upstream, sems.at[2]),
+        pltpu.make_async_copy(field_hbm.at[m, 0, i], field.at[m, 0, i], sems.at[2 * m + i])
+        for m in range(2)
+        for i in range(2)
     ]
+    copies.append(pltpu.make_async_copy(upstream_hbm, upstream, sems.at[4]))
     for copy in copies:
         copy.start()
     for copy in copies:
@@ -91,8 +96,6 @@
             rows = [upstream[micro, 0, p, 0, pl.ds(j, 1), :] for j in range(2) for p in range(pairs)]
             rows = jnp.concatenate([r.astype(F32) for r in rows], axis=0).astype(BF16)
             out[pl.ds(8, pairs // 4)] = rows.reshape(pairs // 4, 8, 256)
-        else:
-            out[pl.ds(8, pairs // 4)] = jnp.zeros((pairs // 4, 8, 256), BF16)
 
     for k in range(pairs):
         for micro in range(2):
@@ -102,7 +105,7 @@
 
 def main_body(pairs, spread, mine, partner, *refs):
     received = refs[: pairs - 1]
-    swapped, banded, second, keep, xf, hid, hgs, us, t2, t1 = refs[pairs - 1 :]
+    swapped, banded, ordered, keep, xf, hid, hgs, us, t2, t1 = refs[pairs - 1 :]
     space = lax.axis_index("space")
     side, pair = space % 2, space // 2
     section = lax.axis_index("section")
@@ -132,8 +135,7 @@
                         ]
 
     place(lambda micro, at, size: mine[micro, pl.ds(at, size)], 0, side)
-    size_of = mine.shape[1]
-    last = 2 * size_of * (pairs - 1)
+    last = 2 * sum(ref.shape[1] for ref in received)
     place(
         lambda micro, at, size: jnp.where(
             section == micro, partner[pl.ds(at, size)], swapped[pl.ds(last + at, size)]
@@ -147,11 +149,11 @@
         place(lambda micro, at, size: ref[micro, pl.ds(at, size)], k, side ^ section)
         start = offset
         place(
-            lambda micro, at, size: swapped[pl.ds(start + micro * size_of + at, size)],
+            lambda micro, at, size: swapped[pl.ds(start + micro * ref.shape[1] + at, size)],
             k,
             1 - (side ^ section),
         )
-        offset += 2 * size_of
+        offset += 2 * ref.shape[1]
 
     rows = total // 2
     row = lax.broadcasted_iota(jnp.int32, (rows, 256), 0)
@@ -180,7 +182,7 @@
     half = pairs * width * 2
     low = lax.broadcasted_iota(jnp.int32, (half, 128), 1) < CB
     row2 = lax.broadcasted_iota(jnp.int32, (half, 128), 0)
-    cols = []
+    cols, thirds = [], []
     for kx in range(3):
         for ky in range(3):
             start = base2 + ky - 1 - (step if kx == 0 else 0)
@@ -190,30 +192,42 @@
                 b = jnp.where(row2 % 2 == 0, 0.0, b)
             ra = pltpu.roll(a, 64, 1)
             rb = pltpu.roll(b, 64, 1)
-            zero_k = jnp.concatenate([jnp.where(low, 0.0, ra), ra[:, :CB]], axis=1)
-            one_k = jnp.concatenate([jnp.where(low, ra, rb), rb[:, :CB]], axis=1)
-            cols.append(jnp.concatenate([zero_k, one_k], axis=0).astype(BF16))
-    out = jnp.zeros((2 * half, CC), F32)
-    for tap in range(9):
-        out = out + jnp.dot(
-            cols[tap], second[pl.ds(tap * 192, 192), :], preferred_element_type=F32
-        )
+            pair_k = [jnp.where(low, 0.0, ra), jnp.where(low, ra, rb)]
+            cols.append(jnp.concatenate(pair_k, axis=0).astype(BF16))
+            thirds.append((a, b) if len(thirds) % 2 else (ra, rb))
+    thirds.append((0.0, 0.0))
+    for p in range(5):
+        pair_k = [jnp.where(low, f, l) for f, l in zip(thirds[2 * p], thirds[2 * p + 1])]
+        cols.append(jnp.concatenate(pair_k, axis=0).astype(BF16))
+    cols = jnp.concatenate(cols, axis=1)
+    out = jnp.dot(cols, ordered[...], preferred_element_type=F32)
     up = jnp.concatenate([us[0], us[1]], axis=0)
     delta = leaky(out, up)
     delta_b = delta.astype(BF16)
     other = pltpu.roll(delta, 64, 1)
     low3 = lax.broadcasted_iota(jnp.int32, (2 * half, 128), 1) < CB
     turned = jnp.where(low3 == (section == 0), delta, other).astype(BF16)
-    for tap in range(9):
-        t2[pl.ds(tap * 192, 192), :] = contract(cols[tap], turned, 0, 0)
+    for two in range(7):
+        grid = contract(cols[:, two * 256 : two * 256 + 256], turned, 0, 0)
+        for tile in range(2):
+            tap = 2 * two + tile
+            if tap < 9:
+                t2[pl.ds(tap * 192, 128), :] = grid[tile * 128 : tile * 128 + 128]
+                continue
+            for h in range(2):
+                tap = 2 * (2 * two + tile - 9) + h
+                if tap < 9:
+                    row0 = tile * 128 + h * CB
+                    t2[pl.ds(tap * 192 + 128, CB), :] = grid[row0 : row0 + CB]
     row3 = lax.broadcasted_iota(jnp.int32, (2 * half, 128), 0)
     next_y = row3 % 2 == 0
     next_x = row3 % half < half - 2 * width
+    grid = contract(delta_b, ordered[...], 1, 1)
     grads = []
     for tap in range(9):
-        c0 = contract(delta_b, second[pl.ds(tap * 192, 128), :], 1, 1)
-        c1 = contract(delta_b, second[pl.ds(tap * 192 + 128, 64), :], 1, 1)
-        grads.append([c0, jnp.concatenate([c1, c1], axis=1)])
+        c1 = grid[:, 1152 + tap // 2 * 128 : 1280 + tap // 2 * 128]
+        c1 = c1 if tap % 2 else pltpu.roll(c1, 64, 1)
+        grads.append([grid[:, tap * 128 : tap * 128 + 128], c1])
 
     def joined(late, early, distance, valid):
         return [
@@ -327,7 +341,7 @@
     pieces = pl.pallas_call(
         lambda *refs: cut_body(pairs, *refs),
         out_shape=[
-            jax.ShapeDtypeStruct((2, 8 + tail, 8, 256), BF16)
+            jax.ShapeDtypeStruct((2, 8 + (tail if k in (0, pairs - 1) else 0), 8, 256), BF16)
             for k in range(pairs)
         ]
         + [jax.ShapeDtypeStruct((8 + tail, 8, 256), BF16)],
@@ -336,7 +350,7 @@
         scratch_shapes=[
             pltpu.VMEM(input_field.shape, BF16),
             pltpu.VMEM(upstream_grad.shape, BF16),
-            pltpu.SemaphoreType.DMA((3,)),
+            pltpu.SemaphoreType.DMA((5,)),
         ],
         compiler_params=pltpu.CompilerParams(vmem_limit_bytes=16 << 20),
     )(
@@ -349,7 +363,15 @@
         route = [(2 * d + c, 2 * (d ^ (2 * k) ^ c) + c) for d in range(spread) for c in range(2)]
         received[k - 1] = lax.ppermute(pieces[k], ("space", "section"), route)
     partner = lax.ppermute(pieces[pairs], "space", swap_bit(spread, 0))
-    banded = call(banded_body, jax.ShapeDtypeStruct((9 * 256, 256), BF16), [], (first_weight.T,))
+    banded, ordered = call(
+        weights_body,
+        [
+            jax.ShapeDtypeStruct((9 * 256, 256), BF16),
+            jax.ShapeDtypeStruct((14 * 128, 128), BF16),
+        ],
+        [],
+        (first_weight.T, second_weight),
+    )
     outgoing = [received[k - 1].reshape(-1, 8, 256) for k in swap_order(pairs)] + [partner]
     outgoing, partner, banded = lax.optimization_barrier((jnp.concatenate(outgoing), partner, banded))
     swapped = lax.ppermute(outgoing, "section", swap_bit(2, 0))
@@ -365,7 +387,7 @@
             pltpu.VMEM((TAPS * CB + 2 * h2, 128), F32),
             pltpu.VMEM((TAPS * CA + 4 * h1, 128), F32),
         ],
-        (mine, partner, *received, swapped, banded, second_weight),
+        (mine, partner, *received, swapped, banded, ordered),
     )
 
     def added(a, b):

time: 26.7 us -> 26.3 us (0.985)
  waiting for transfers between devices: 9.12 us -> 7.85 us
  local copies, waits for them, and re-layouts: 0.91 us -> 1.92 us
    ppermute x1, waiting for transfers between devices: 2.85 us -> 1.64 us  [shards(): partner = lax.ppermute(pieces[pairs], 'space', swap_bit(spread, 0))]
    unnamed x4, local copies, waits for them, and re-layouts: 0.9 us -> 1.91 us
where the time goes in v8:
time: 26.3 us; the launch traced here: 26.1 us
  starting transfers between devices  10.8 us (41%)
  waiting for transfers between devices  7.85 us (30%)
  Pallas kernels  4.74 us (18%)
  local copies, waits for them, and re-layouts  1.92 us (7%)
  between operations  0.68 us (3%)
    ppermute x3, starting transfers between devices, shards(): received[k - 1] = lax.ppermute(pieces[k], ('space', 'section'), route)  5.75 us
    pallas_call x2, Pallas kernels, call(): pl.pallas_call(body, out_shape=out_shape, in_specs=[vmem] * len(args), ou...  3.03 us
    ppermute x1, waiting for transfers between devices, shards(): came = lax.ppermute(total, 'dp', swap_bit(replicas, bit))  2.42 us
    ppermute x1, waiting for transfers between devices, shards(): lax.ppermute(pick(paired, 1 - here, 1), 'space', swap_bit(spread, bit + 1))  2.39 us
    unnamed x4, local copies, waits for them, and re-layouts  1.91 us
    ppermute x1, waiting for transfers between devices, shards(): partner = lax.ppermute(pieces[pairs], 'space', swap_bit(spread, 0))  1.64 us
    ppermute x1, starting transfers between devices, shards(): partner = lax.ppermute(pieces[pairs], 'space', swap_bit(spread, 0))  1.64 us
    ppermute x1, starting transfers between devices, shards(): lax.ppermute(pick(paired, 1 - here, 1), 'space', swap_bit(spread, bit + 1))  1.64 us
  transfers between devices with their start and end apart: 7, of which 4 were waited for; matrix products, arithmetic and copies ran while one was open for 0% of the time, Pallas kernels for 1%

profile of v8, /device:TPU:0, one launch (start us, length us, event | category | flops | bytes accessed | tf_op | source)
XLA Modules:
  0.0 26.1 jit_solution(17724730371162130360)
XLA Ops:
  0.6 0.9 %shard_map.59 = (bf16[2,9,8,256]{3,2,1,0:T(8,128)(2,1)S(1)}, bf16[2,8,8,256]{3,2,1,0:T(8,128)(2,1)S(1)}, bf16[2,8,8,256]{3,2,1,0:T(8,128)(2,1)S(1)}, bf16[2,9,8,...) custom-call(bf16[2,1,2,8,8,256]{5,4,3,2,1,0:T(8,128)(2,1)} %refs_0_.1, bf16[2,1,4,1,2,256]{5,4,3,2,1,0:T(2,128)(2,1)} %refs_1_.1), custom_call_target="tpu_custom_call" | custom-call | tf_op jit(solution)/shard_map/pallas_call | solution.py:341
  1.5 5.1 %collective-permute-start.2 = (bf16[2,9,8,256]{3,2,1,0:T(8,128)(2,1)S(1)}, bf16[2,9,8,256]{3,2,1,0:T(8,128)(2,1)S(1)}, u32[]{:S(2)}, u32[]{:S(2)}) collective-permute-start(bf16[2,9,8,256]{3,2,1,0:T(8,128)(2,1)S(1)} %get-tuple-element.17), channel_id=1, source_target_pairs={{0,24},{2,30},{4,28},{6,26},{8,16},{10,22},{12,20},{14,18},{16,8},... | collective-permute-start | bytes 221192 | tf_op jit(solution)/shard_map/ppermute | solution.py:364
  6.6 0.0 collective-permute-start.1
  6.6 0.6 %collective-permute-start = (bf16[2,8,8,256]{3,2,1,0:T(8,128)(2,1)S(1)}, bf16[2,8,8,256]{3,2,1,0:T(8,128)(2,1)S(1)}, u32[]{:S(2)}, u32[]{:S(2)}) collective-permute-start(bf16[2,8,8,256]{3,2,1,0:T(8,128)(2,1)S(1)} %get-tuple-element.15), channel_id=1, source_target_pairs={{0,16},{2,22},{4,20},{6,18},{8,24},{10,30},{12,28},{14,26},{16,0},... | collective-permute-start | bytes 196616 | tf_op jit(solution)/shard_map/ppermute | solution.py:364
  7.3 1.6 %collective-permute-start.3 = (bf16[9,8,256]{2,1,0:T(8,128)(2,1)S(1)}, bf16[9,8,256]{2,1,0:T(8,128)(2,1)S(1)}, u32[]{:S(2)}, u32[]{:S(2)}) collective-permute-start(bf16[9,8,256]{2,1,0:T(8,128)(2,1)S(1)} %get-tuple-element.18), channel_id=1, source_target_pairs={{0,4},{4,0},{8,12},{12,8},{16,20},{20,16},{24,28},{28,24},{1,5},{5... | collective-permute-start | bytes 110600 | tf_op jit(solution)/shard_map/ppermute | solution.py:365
  8.9 0.0 copy-start
  8.9 1.0 %copy-done = bf16[1728,128]{1,0:T(8,128)(2,1)S(1)} copy-done((bf16[1728,128]{1,0:T(8,128)(2,1)S(1)}, bf16[1728,128]{1,0:T(8,128)(2,1)}, u32[]{:S(2)}) %copy-start) | copy-done | bytes 442392
  9.9 0.0 copy-start.1
  9.9 0.9 %copy-done.1 = bf16[864,64]{0,1:T(8,128)(2,1)S(1)} copy-done((bf16[864,64]{0,1:T(8,128)(2,1)S(1)}, bf16[864,64]{0,1:T(8,128)(2,1)}, u32[]{:S(2)}) %copy-start.1) | copy-done | bytes 110616
  10.8 0.3 %shard_map.60 = (bf16[2304,256]{1,0:T(8,128)(2,1)S(1)}, bf16[1792,128]{1,0:T(8,128)(2,1)S(1)}) custom-call(bf16[64,864]{1,0:T(8,128)(2,1)S(1)} %bitcast.11, bf16[1728,128]{1,0:T(8,128)(2,1)S(1)} %copy-done), custom_call_target="tpu_custom_call" | custom-call | tf_op jit(solution)/shard_map/pallas_call | solution.py:32
  11.2 1.6 %collective-permute-done.3.refs_1_ = bf16[9,8,256]{2,1,0:T(8,128)(2,1)S(1)} collective-permute-done((bf16[9,8,256]{2,1,0:T(8,128)(2,1)S(1)}, bf16[9,8,256]{2,1,0:T(8,128)(2,1)S(1)}, u32[]{:S(2)}, u32[]{:S(2)}) %collective-permute-start.3) | collective-permute-done | bytes 36896 | tf_op jit(solution)/shard_map/ppermute | solution.py:365
  12.8 0.0 collective-permute-done.1.refs_2_
  12.8 0.0 collective-permute-done.refs_3_
  12.8 0.0 collective-permute-done.2.refs_4_
  12.9 0.2 collective-permute-start.4
  13.1 1.4 %collective-permute-done.4.refs_5_ = bf16[59,8,256]{2,1,0:T(8,128)(2,1)S(1)} collective-permute-done((bf16[59,8,256]{2,1,0:T(8,128)(2,1)S(1)}, bf16[59,8,256]{2,1,0:T(8,128)(2,1)S(1)}, u32[]{:S(2)}, u32[]{:S(2)}) %collective-permute-start.4) | collective-permute-done | bytes 241696 | tf_op jit(solution)/shard_map/ppermute | solution.py:377
  14.4 2.7 %shard_map.61 = bf16[2,144,128]{2,1,0:T(8,128)(2,1)S(1)} custom-call(bf16[2,9,8,256]{3,2,1,0:T(8,128)(2,1)S(1)} %get-tuple-element.14.refs_0_, bf16[9,8,256]{2,1,0:T(8,128)(2,1)S(1)} %collective-permute-done.3.refs_1_, bf16[2,8,8,256]{3,2,1,0:T(8,128)(2,1)S(1)} %collective-permute-done.1.refs_2_, bf16[2,8,8,256]{3,2,1,0:T(8,128)(2,1)S(1)} %collective-permute-done.refs_3_, ...), custom_call_target="tpu_custom_call" | custom-call | tf_op jit(solution)/shard_map/pallas_call | solution.py:32
  17.2 1.6 %collective-permute-start.5 = (bf16[1,144,128]{2,1,0:T(8,128)(2,1)S(1)}, bf16[1,144,128]{2,1,0:T(8,128)(2,1)S(1)}, u32[]{:S(2)}, u32[]{:S(2)}) collective-permute-start(bf16[1,144,128]{2,1,0:T(8,128)(2,1)S(1)} %constant_dynamic-slice_fusion), channel_id=1, source_target_pairs={{0,8},{4,12},{8,0},{12,4},{16,24},{20,28},{24,16},{28,20},{1,9},{5... | collective-permute-start | bytes 110600 | tf_op jit(solution)/shard_map/ppermute | solution.py:401
  18.8 2.4 %collective-permute-done.5 = bf16[1,144,128]{2,1,0:T(8,128)(2,1)S(1)} collective-permute-done((bf16[1,144,128]{2,1,0:T(8,128)(2,1)S(1)}, bf16[1,144,128]{2,1,0:T(8,128)(2,1)S(1)}, u32[]{:S(2)}, u32[]{:S(2)}) %collective-permute-start.5) | collective-permute-done | bytes 36896 | tf_op jit(solution)/shard_map/ppermute | solution.py:401
  21.2 1.6 %collective-permute-start.6 = (bf16[144,128]{1,0:T(8,128)(2,1)S(1)}, bf16[144,128]{1,0:T(8,128)(2,1)S(1)}, u32[]{:S(2)}, u32[]{:S(2)}) collective-permute-start(bf16[144,128]{1,0:T(8,128)(2,1)S(1)} %fusion.refs_0_), channel_id=1, source_target_pairs={{0,1},{1,0},{2,3},{3,2},{4,5},{5,4},{6,7},{7,6},{8,9},{9,8},{10,11... | collective-permute-start | bytes 110600 | tf_op jit(solution)/shard_map/ppermute | solution.py:410
  22.8 2.4 %collective-permute-done.6.refs_1_ = bf16[144,128]{1,0:T(8,128)(2,1)S(1)} collective-permute-done((bf16[144,128]{1,0:T(8,128)(2,1)S(1)}, bf16[144,128]{1,0:T(8,128)(2,1)S(1)}, u32[]{:S(2)}, u32[]{:S(2)}) %collective-permute-start.6) | collective-permute-done | bytes 36896 | tf_op jit(solution)/shard_map/ppermute | solution.py:410
  25.2 0.8 %shard_map.62 = (f32[32,108]{1,0:T(8,128)}, f32[64,216]{1,0:T(8,128)}) custom-call(bf16[144,128]{1,0:T(8,128)(2,1)S(1)} %fusion.refs_0_, bf16[144,128]{1,0:T(8,128)(2,1)S(1)} %collective-permute-done.6.refs_1_), custom_call_target="tpu_custom_call" | custom-call | tf_op jit(solution)/shard_map/pallas_call | solution.py:414
  (3 shorter events, 0.1 us)
Async XLA Ops:
  1.5 11.3 %collective-permute-start.2 = (bf16[2,9,8,256]{3,2,1,0:T(8,128)(2,1)S(1)}, bf16[2,9,8,256]{3,2,1,0:T(8,128)(2,1)S(1)}, u32[]{:S(2)}, u32[]{:S(2)}) collective-permute-start(bf16[2,9,8,256]{3,2,1,0:T(8,128)(2,1)S(1)} %get-tuple-element.17), channel_id=1, source_target_pairs={{0,24},{2,30},{4,28},{6,26},{8,16},{10,22},{12,20},{14,18},{16,8},... | collective-permute-start | bytes 221192 | tf_op jit(solution)/shard_map/ppermute | solution.py:364
  6.6 6.2 %collective-permute-start.1 = (bf16[2,8,8,256]{3,2,1,0:T(8,128)(2,1)S(1)}, bf16[2,8,8,256]{3,2,1,0:T(8,128)(2,1)S(1)}, u32[]{:S(2)}, u32[]{:S(2)}) collective-permute-start(bf16[2,8,8,256]{3,2,1,0:T(8,128)(2,1)S(1)} %get-tuple-element.16), channel_id=1, source_target_pairs={{0,8},{2,14},{4,12},{6,10},{8,0},{10,6},{12,4},{14,2},{16,24},{18,... | collective-permute-start | bytes 196616 | tf_op jit(solution)/shard_map/ppermute | solution.py:364
  6.6 6.2 %collective-permute-start = (bf16[2,8,8,256]{3,2,1,0:T(8,128)(2,1)S(1)}, bf16[2,8,8,256]{3,2,1,0:T(8,128)(2,1)S(1)}, u32[]{:S(2)}, u32[]{:S(2)}) collective-permute-start(bf16[2,8,8,256]{3,2,1,0:T(8,128)(2,1)S(1)} %get-tuple-element.15), channel_id=1, source_target_pairs={{0,16},{2,22},{4,20},{6,18},{8,24},{10,30},{12,28},{14,26},{16,0},... | collective-permute-start | bytes 196616 | tf_op jit(solution)/shard_map/ppermute | solution.py:364
  7.3 5.5 %collective-permute-start.3 = (bf16[9,8,256]{2,1,0:T(8,128)(2,1)S(1)}, bf16[9,8,256]{2,1,0:T(8,128)(2,1)S(1)}, u32[]{:S(2)}, u32[]{:S(2)}) collective-permute-start(bf16[9,8,256]{2,1,0:T(8,128)(2,1)S(1)} %get-tuple-element.18), channel_id=1, source_target_pairs={{0,4},{4,0},{8,12},{12,8},{16,20},{20,16},{24,28},{28,24},{1,5},{5... | collective-permute-start | bytes 110600 | tf_op jit(solution)/shard_map/ppermute | solution.py:365
  8.9 1.0 %copy-start = (bf16[1728,128]{1,0:T(8,128)(2,1)S(1)}, bf16[1728,128]{1,0:T(8,128)(2,1)}, u32[]{:S(2)}) copy-start(bf16[1728,128]{1,0:T(8,128)(2,1)} %second.1) | copy-start | bytes 1327108
  9.9 0.9 %copy-start.1 = (bf16[864,64]{0,1:T(8,128)(2,1)S(1)}, bf16[864,64]{0,1:T(8,128)(2,1)}, u32[]{:S(2)}) copy-start(bf16[864,64]{0,1:T(8,128)(2,1)} %param.5) | copy-start | bytes 331780
  12.9 1.6 %collective-permute-start.4 = (bf16[59,8,256]{2,1,0:T(8,128)(2,1)S(1)}, bf16[59,8,256]{2,1,0:T(8,128)(2,1)S(1)}, u32[]{:S(2)}, u32[]{:S(2)}) collective-permute-start(bf16[59,8,256]{2,1,0:T(8,128)(2,1)S(1)} %pad_maximum_fusion), channel_id=1, source_target_pairs={{0,2},{2,0},{1,3},{3,1},{4,6},{6,4},{5,7},{7,5},{8,10},{10,8},{9,1... | collective-permute-start | bytes 725000 | tf_op jit(solution)/shard_map/ppermute | solution.py:377
  17.2 4.0 %collective-permute-start.5 = (bf16[1,144,128]{2,1,0:T(8,128)(2,1)S(1)}, bf16[1,144,128]{2,1,0:T(8,128)(2,1)S(1)}, u32[]{:S(2)}, u32[]{:S(2)}) collective-permute-start(bf16[1,144,128]{2,1,0:T(8,128)(2,1)S(1)} %constant_dynamic-slice_fusion), channel_id=1, source_target_pairs={{0,8},{4,12},{8,0},{12,4},{16,24},{20,28},{24,16},{28,20},{1,9},{5... | collective-permute-start | bytes 110600 | tf_op jit(solution)/shard_map/ppermute | solution.py:401
  21.2 4.0 %collective-permute-start.6 = (bf16[144,128]{1,0:T(8,128)(2,1)S(1)}, bf16[144,128]{1,0:T(8,128)(2,1)S(1)}, u32[]{:S(2)}, u32[]{:S(2)}) collective-permute-start(bf16[144,128]{1,0:T(8,128)(2,1)S(1)} %fusion.refs_0_), channel_id=1, source_target_pairs={{0,1},{1,0},{2,3},{3,2},{4,5},{5,4},{6,7},{7,6},{8,9},{9,8},{10,11... | collective-permute-start | bytes 110600 | tf_op jit(solution)/shard_map/ppermute | solution.py:410

commit v9 on v8

--- a/solution.py
+++ b/solution.py
@@ -39,7 +39,15 @@
     )(*args)
 
 
-def weights_body(weight, second, banded, ordered):
+def weights_body(weight_hbm, second_hbm, banded, ordered, weight, second, sems):
+    copies = [
+        pltpu.make_async_copy(weight_hbm, weight, sems.at[0]),
+        pltpu.make_async_copy(second_hbm, second, sems.at[1]),
+    ]
+    for copy in copies:
+        copy.start()
+    for copy in copies:
+        copy.wait()
     for tap in range(9):
         ordered[pl.ds(tap * 128, 128), :] = second[pl.ds(tap * 192, 128), :]
         ordered[pl.ds(1152 + tap * CB, CB), :] = second[pl.ds(tap * 192 + 128, CB), :]
@@ -105,7 +113,7 @@
 
 def main_body(pairs, spread, mine, partner, *refs):
     received = refs[: pairs - 1]
-    swapped, banded, ordered, keep, xf, hid, hgs, us, t2, t1 = refs[pairs - 1 :]
+    early, late, banded, ordered, keep, xf, hid, hgs, us, t2, t1 = refs[pairs - 1 :]
     space = lax.axis_index("space")
     side, pair = space % 2, space // 2
     section = lax.axis_index("section")
@@ -135,25 +143,26 @@
                         ]
 
     place(lambda micro, at, size: mine[micro, pl.ds(at, size)], 0, side)
-    last = 2 * sum(ref.shape[1] for ref in received)
+    last = 2 * received[0].shape[1]
     place(
         lambda micro, at, size: jnp.where(
-            section == micro, partner[pl.ds(at, size)], swapped[pl.ds(last + at, size)]
+            section == micro, partner[pl.ds(at, size)], late[pl.ds(last + at, size)]
         ),
         0,
         1 - side,
     )
     offset = 0
-    for k in swap_order(pairs):
+    for k in [1] + swap_order(pairs):
         ref = received[k - 1]
         place(lambda micro, at, size: ref[micro, pl.ds(at, size)], k, side ^ section)
-        start = offset
+        swapped = late if k == 1 else early
+        start = 0 if k == 1 else offset
         place(
             lambda micro, at, size: swapped[pl.ds(start + micro * ref.shape[1] + at, size)],
             k,
             1 - (side ^ section),
         )
-        offset += 2 * ref.shape[1]
+        offset += 0 if k == 1 else 2 * ref.shape[1]
 
     rows = total // 2
     row = lax.broadcasted_iota(jnp.int32, (rows, 256), 0)
@@ -201,7 +210,7 @@
         cols.append(jnp.concatenate(pair_k, axis=0).astype(BF16))
     cols = jnp.concatenate(cols, axis=1)
     out = jnp.dot(cols, ordered[...], preferred_element_type=F32)
-    up = jnp.concatenate([us[0], us[1]], axis=0)
+    up = jnp.concatenate([us[h, 0:half, :] for h in range(2)], axis=0)
     delta = leaky(out, up)
     delta_b = delta.astype(BF16)
     other = pltpu.roll(delta, 64, 1)
@@ -298,7 +307,7 @@
 
 
 def swap_order(pairs):
-    return [*range(2, 0, -1), *range(3, pairs)]
+    return [*range(2, pairs)]
 
 
 def packed_rows(spread):
@@ -363,18 +372,29 @@
         route = [(2 * d + c, 2 * (d ^ (2 * k) ^ c) + c) for d in range(spread) for c in range(2)]
         received[k - 1] = lax.ppermute(pieces[k], ("space", "section"), route)
     partner = lax.ppermute(pieces[pairs], "space", swap_bit(spread, 0))
-    banded, ordered = call(
+    banded, ordered = pl.pallas_call(
         weights_body,
-        [
+        out_shape=[
             jax.ShapeDtypeStruct((9 * 256, 256), BF16),
             jax.ShapeDtypeStruct((14 * 128, 128), BF16),
         ],
-        [],
-        (first_weight.T, second_weight),
-    )
-    outgoing = [received[k - 1].reshape(-1, 8, 256) for k in swap_order(pairs)] + [partner]
-    outgoing, partner, banded = lax.optimization_barrier((jnp.concatenate(outgoing), partner, banded))
-    swapped = lax.ppermute(outgoing, "section", swap_bit(2, 0))
+        in_specs=[hbm, hbm],
+        out_specs=[pl.BlockSpec(memory_space=pltpu.VMEM)] * 2,
+        scratch_shapes=[
+            pltpu.VMEM(first_weight.shape[::-1], BF16),
+            pltpu.VMEM(second_weight.shape, BF16),
+            pltpu.SemaphoreType.DMA((2,)),
+        ],
+        compiler_params=pltpu.CompilerParams(vmem_limit_bytes=16 << 20),
+    )(
+        pltpu.with_memory_space_constraint(first_weight.T, pltpu.HBM),
+        pltpu.with_memory_space_constraint(second_weight, pltpu.HBM),
+    )
+    early = jnp.concatenate([received[k - 1].reshape(-1, 8, 256) for k in swap_order(pairs)])
+    early = lax.ppermute(early, "section", swap_bit(2, 0))
+    late, banded = lax.optimization_barrier((received[0].reshape(-1, 8, 256), banded))
+    late = jnp.concatenate([late, partner])
+    late = lax.ppermute(late, "section", swap_bit(2, 0))
     h2, h1 = packed_rows(spread)
     total = call(
         lambda *refs: main_body(pairs, spread, *refs),
@@ -382,12 +402,12 @@
         [
             pltpu.VMEM((2, 2, (2 * pairs + 1) * 64 + 16, 128), F32),
             pltpu.VMEM((2, 2, (pairs + 1) * 32 + 16, 128), F32),
-            pltpu.VMEM((2, 2, pairs * 32, 128), F32),
-            pltpu.VMEM((2, pairs * 16, 128), F32),
+            pltpu.VMEM((2, 2, pairs * 32 + 8, 128), F32),
+            pltpu.VMEM((2, pairs * 16 + 16, 128), F32),
             pltpu.VMEM((TAPS * CB + 2 * h2, 128), F32),
             pltpu.VMEM((TAPS * CA + 4 * h1, 128), F32),
         ],
-        (mine, partner, *received, swapped, banded, ordered),
+        (mine, partner, *received, early, late, banded, ordered),
     )
 
     def added(a, b):

time: 26.3 us -> 26.1 us (level)
  local copies, waits for them, and re-layouts: 1.92 us -> 0.01 us
  Pallas kernels: 4.74 us -> 5.84 us
  starting transfers between devices: 10.8 us -> 11.4 us
    ppermute x3, waiting for transfers between devices: 0.01 us -> 2.32 us  [shards(): received[k - 1] = lax.ppermute(pieces[k], ('space', 'section'), route)]
    unnamed x4 -> x0, local copies, waits for them, and re-layouts: 1.91 us -> none
    ppermute x1, waiting for transfers between devices: 1.64 us -> 0.01 us  [shards(): partner = lax.ppermute(pieces[pairs], 'space', swap_bit(spread, 0))]
    pallas_call x0 -> x1, Pallas kernels: none -> 1.43 us  [shards(): pl.pallas_call(weights_body, out_shape=[jax.ShapeDtypeStruct((9 * 256, 25...]
    ppermute x1 -> x2, starting transfers between devices: 0.18 us -> 0.64 us  [the longest x1 0.52 us: shards(): late = lax.ppermute(late, 'section', swap_bit(2, 0))]
    ppermute x1 -> x2, waiting for transfers between devices: 1.39 us -> 0.95 us  [the longest x1 0.95 us: shards(): late = lax.ppermute(late, 'section', swap_bit(2, 0))]
    pallas_call x2 -> x1, Pallas kernels: 3.03 us -> 2.7 us  [call(): pl.pallas_call(body, out_shape=out_shape, in_specs=[vmem] * len(args), ou...]
  transfers between devices with their start and end apart: 7 -> 8, of which waited for: 4 -> 4; matrix products, arithmetic and copies ran while one was open for 0% -> 0% of each run, Pallas kernels for 1% -> 6%
where the time goes in v9:
time: 26.1 us; the launch traced here: 25.9 us
  starting transfers between devices  11.4 us (44%)
  waiting for transfers between devices  7.92 us (30%)
  Pallas kernels  5.84 us (22%)
  between operations  0.68 us (3%)
    ppermute x3, starting transfers between devices, shards(): received[k - 1] = lax.ppermute(pieces[k], ('space', 'section'), route)  5.75 us
    pallas_call x1, Pallas kernels, call(): pl.pallas_call(body, out_shape=out_shape, in_specs=[vmem] * len(args), ou...  2.7 us
    ppermute x1, waiting for transfers between devices, shards(): came = lax.ppermute(total, 'dp', swap_bit(replicas, bit))  2.41 us
    ppermute x3, waiting for transfers between devices, shards(): received[k - 1] = lax.ppermute(pieces[k], ('space', 'section'), route)  2.32 us
    ppermute x1, waiting for transfers between devices, shards(): lax.ppermute(pick(paired, 1 - here, 1), 'space', swap_bit(spread, bit + 1))  2.23 us
    ppermute x1, starting transfers between devices, shards(): lax.ppermute(pick(paired, 1 - here, 1), 'space', swap_bit(spread, bit + 1))  1.79 us
    ppermute x1, starting transfers between devices, shards(): partner = lax.ppermute(pieces[pairs], 'space', swap_bit(spread, 0))  1.64 us
    ppermute x1, starting transfers between devices, shards(): came = lax.ppermute(total, 'dp', swap_bit(replicas, bit))  1.61 us
  transfers between devices with their start and end apart: 8, of which 4 were waited for; matrix products, arithmetic and copies ran while one was open for 0% of the time, Pallas kernels for 6%

profile of v9, /device:TPU:0, one launch (start us, length us, event | category | flops | bytes accessed | tf_op | source)
XLA Modules:
  0.0 25.9 jit_solution(13560288684918176972)
XLA Ops:
  0.6 0.9 %shard_map.59 = (bf16[2,9,8,256]{3,2,1,0:T(8,128)(2,1)S(1)}, bf16[2,8,8,256]{3,2,1,0:T(8,128)(2,1)S(1)}, bf16[2,8,8,256]{3,2,1,0:T(8,128)(2,1)S(1)}, bf16[2,9,8,...) custom-call(bf16[2,1,2,8,8,256]{5,4,3,2,1,0:T(8,128)(2,1)} %refs_0_.1, bf16[2,1,4,1,2,256]{5,4,3,2,1,0:T(2,128)(2,1)} %refs_1_.1), custom_call_target="tpu_custom_call" | custom-call | tf_op jit(solution)/shard_map/pallas_call | solution.py:350
  1.5 5.1 %collective-permute-start.3 = (bf16[2,9,8,256]{3,2,1,0:T(8,128)(2,1)S(1)}, bf16[2,9,8,256]{3,2,1,0:T(8,128)(2,1)S(1)}, u32[]{:S(2)}, u32[]{:S(2)}) collective-permute-start(bf16[2,9,8,256]{3,2,1,0:T(8,128)(2,1)S(1)} %get-tuple-element.17), channel_id=1, source_target_pairs={{0,24},{2,30},{4,28},{6,26},{8,16},{10,22},{12,20},{14,18},{16,8},... | collective-permute-start | bytes 221192 | tf_op jit(solution)/shard_map/ppermute | solution.py:373
  6.6 0.0 collective-permute-start.1
  6.6 0.6 %collective-permute-start.2 = (bf16[2,8,8,256]{3,2,1,0:T(8,128)(2,1)S(1)}, bf16[2,8,8,256]{3,2,1,0:T(8,128)(2,1)S(1)}, u32[]{:S(2)}, u32[]{:S(2)}) collective-permute-start(bf16[2,8,8,256]{3,2,1,0:T(8,128)(2,1)S(1)} %get-tuple-element.16), channel_id=1, source_target_pairs={{0,16},{2,22},{4,20},{6,18},{8,24},{10,30},{12,28},{14,26},{16,0},... | collective-permute-start | bytes 196616 | tf_op jit(solution)/shard_map/ppermute | solution.py:373
  7.3 1.6 %collective-permute-start = (bf16[9,8,256]{2,1,0:T(8,128)(2,1)S(1)}, bf16[9,8,256]{2,1,0:T(8,128)(2,1)S(1)}, u32[]{:S(2)}, u32[]{:S(2)}) collective-permute-start(bf16[9,8,256]{2,1,0:T(8,128)(2,1)S(1)} %get-tuple-element.14), channel_id=1, source_target_pairs={{0,4},{4,0},{8,12},{12,8},{16,20},{20,16},{24,28},{28,24},{1,5},{5... | collective-permute-start | bytes 110600 | tf_op jit(solution)/shard_map/ppermute | solution.py:374
  8.9 1.4 %shard_map.60 = (bf16[2304,256]{1,0:T(8,128)(2,1)S(1)}, bf16[1792,128]{1,0:T(8,128)(2,1)S(1)}) custom-call(bf16[64,864]{1,0:T(8,128)(2,1)} %bitcast.11, bf16[1728,128]{1,0:T(8,128)(2,1)} %second_hbm.1), custom_call_target="tpu_custom_call" | custom-call | tf_op jit(solution)/shard_map/pallas_call | solution.py:375
  10.4 2.3 %collective-permute-done.1.refs_2_ = bf16[2,8,8,256]{3,2,1,0:T(8,128)(2,1)S(1)} collective-permute-done((bf16[2,8,8,256]{3,2,1,0:T(8,128)(2,1)S(1)}, bf16[2,8,8,256]{3,2,1,0:T(8,128)(2,1)S(1)}, u32[]{:S(2)}, u32[]{:S(2)}) %collective-permute-start.1) | collective-permute-done | bytes 65568 | tf_op jit(solution)/shard_map/ppermute | solution.py:373
  12.7 0.0 collective-permute-done.2.refs_3_
  12.7 0.0 collective-permute-done.3.refs_4_
  12.7 0.1 collective-permute-start.4
  12.8 0.0 collective-permute-done.refs_1_
  12.8 0.5 %collective-permute-start.5 = (bf16[25,8,256]{2,1,0:T(8,128)(2,1)S(1)}, bf16[25,8,256]{2,1,0:T(8,128)(2,1)S(1)}, u32[]{:S(2)}, u32[]{:S(2)}) collective-permute-start(bf16[25,8,256]{2,1,0:T(8,128)(2,1)S(1)} %pad_maximum_fusion.1), channel_id=1, source_target_pairs={{0,2},{2,0},{1,3},{3,1},{4,6},{6,4},{5,7},{7,5},{8,10},{10,8},{9,1... | collective-permute-start | bytes 307208 | tf_op jit(solution)/shard_map/ppermute | solution.py:397
  13.4 0.9 %collective-permute-done.5.refs_6_ = bf16[25,8,256]{2,1,0:T(8,128)(2,1)S(1)} collective-permute-done((bf16[25,8,256]{2,1,0:T(8,128)(2,1)S(1)}, bf16[25,8,256]{2,1,0:T(8,128)(2,1)S(1)}, u32[]{:S(2)}, u32[]{:S(2)}) %collective-permute-start.5) | collective-permute-done | bytes 102432 | tf_op jit(solution)/shard_map/ppermute | solution.py:397
  14.3 0.0 collective-permute-done.4.refs_5_
  14.3 2.7 %shard_map.61 = bf16[2,144,128]{2,1,0:T(8,128)(2,1)S(1)} custom-call(bf16[2,9,8,256]{3,2,1,0:T(8,128)(2,1)S(1)} %get-tuple-element.13.refs_0_, bf16[9,8,256]{2,1,0:T(8,128)(2,1)S(1)} %collective-permute-done.refs_1_, bf16[2,8,8,256]{3,2,1,0:T(8,128)(2,1)S(1)} %collective-permute-done.1.refs_2_, bf16[2,8,8,256]{3,2,1,0:T(8,128)(2,1)S(1)} %collective-permute-done.2.refs_3_, ...), custom_call_target="tpu_custom_call" | custom-call | tf_op jit(solution)/shard_map/pallas_call | solution.py:32
  17.0 1.8 %collective-permute-start.6 = (bf16[1,144,128]{2,1,0:T(8,128)(2,1)S(1)}, bf16[1,144,128]{2,1,0:T(8,128)(2,1)S(1)}, u32[]{:S(2)}, u32[]{:S(2)}) collective-permute-start(bf16[1,144,128]{2,1,0:T(8,128)(2,1)S(1)} %constant_dynamic-slice_fusion), channel_id=1, source_target_pairs={{0,8},{4,12},{8,0},{12,4},{16,24},{20,28},{24,16},{28,20},{1,9},{5... | collective-permute-start | bytes 110600 | tf_op jit(solution)/shard_map/ppermute | solution.py:421
  18.8 2.2 %collective-permute-done.6 = bf16[1,144,128]{2,1,0:T(8,128)(2,1)S(1)} collective-permute-done((bf16[1,144,128]{2,1,0:T(8,128)(2,1)S(1)}, bf16[1,144,128]{2,1,0:T(8,128)(2,1)S(1)}, u32[]{:S(2)}, u32[]{:S(2)}) %collective-permute-start.6) | collective-permute-done | bytes 36896 | tf_op jit(solution)/shard_map/ppermute | solution.py:421
  21.1 1.6 %collective-permute-start.7 = (bf16[144,128]{1,0:T(8,128)(2,1)S(1)}, bf16[144,128]{1,0:T(8,128)(2,1)S(1)}, u32[]{:S(2)}, u32[]{:S(2)}) collective-permute-start(bf16[144,128]{1,0:T(8,128)(2,1)S(1)} %fusion.refs_0_), channel_id=1, source_target_pairs={{0,1},{1,0},{2,3},{3,2},{4,5},{5,4},{6,7},{7,6},{8,9},{9,8},{10,11... | collective-permute-start | bytes 110600 | tf_op jit(solution)/shard_map/ppermute | solution.py:430
  22.7 2.4 %collective-permute-done.7.refs_1_ = bf16[144,128]{1,0:T(8,128)(2,1)S(1)} collective-permute-done((bf16[144,128]{1,0:T(8,128)(2,1)S(1)}, bf16[144,128]{1,0:T(8,128)(2,1)S(1)}, u32[]{:S(2)}, u32[]{:S(2)}) %collective-permute-start.7) | collective-permute-done | bytes 36896 | tf_op jit(solution)/shard_map/ppermute | solution.py:430
  25.1 0.8 %shard_map.62 = (f32[32,108]{1,0:T(8,128)}, f32[64,216]{1,0:T(8,128)}) custom-call(bf16[144,128]{1,0:T(8,128)(2,1)S(1)} %fusion.refs_0_, bf16[144,128]{1,0:T(8,128)(2,1)S(1)} %collective-permute-done.7.refs_1_), custom_call_target="tpu_custom_call" | custom-call | tf_op jit(solution)/shard_map/pallas_call | solution.py:434
  (4 shorter events, 0.1 us)
Async XLA Ops:
  1.5 11.2 %collective-permute-start.3 = (bf16[2,9,8,256]{3,2,1,0:T(8,128)(2,1)S(1)}, bf16[2,9,8,256]{3,2,1,0:T(8,128)(2,1)S(1)}, u32[]{:S(2)}, u32[]{:S(2)}) collective-permute-start(bf16[2,9,8,256]{3,2,1,0:T(8,128)(2,1)S(1)} %get-tuple-element.17), channel_id=1, source_target_pairs={{0,24},{2,30},{4,28},{6,26},{8,16},{10,22},{12,20},{14,18},{16,8},... | collective-permute-start | bytes 221192 | tf_op jit(solution)/shard_map/ppermute | solution.py:373
  6.6 6.0 %collective-permute-start.1 = (bf16[2,8,8,256]{3,2,1,0:T(8,128)(2,1)S(1)}, bf16[2,8,8,256]{3,2,1,0:T(8,128)(2,1)S(1)}, u32[]{:S(2)}, u32[]{:S(2)}) collective-permute-start(bf16[2,8,8,256]{3,2,1,0:T(8,128)(2,1)S(1)} %get-tuple-element.15), channel_id=1, source_target_pairs={{0,8},{2,14},{4,12},{6,10},{8,0},{10,6},{12,4},{14,2},{16,24},{18,... | collective-permute-start | bytes 196616 | tf_op jit(solution)/shard_map/ppermute | solution.py:373
  6.6 6.0 %collective-permute-start.2 = (bf16[2,8,8,256]{3,2,1,0:T(8,128)(2,1)S(1)}, bf16[2,8,8,256]{3,2,1,0:T(8,128)(2,1)S(1)}, u32[]{:S(2)}, u32[]{:S(2)}) collective-permute-start(bf16[2,8,8,256]{3,2,1,0:T(8,128)(2,1)S(1)} %get-tuple-element.16), channel_id=1, source_target_pairs={{0,16},{2,22},{4,20},{6,18},{8,24},{10,30},{12,28},{14,26},{16,0},... | collective-permute-start | bytes 196616 | tf_op jit(solution)/shard_map/ppermute | solution.py:373
  7.3 5.5 %collective-permute-start = (bf16[9,8,256]{2,1,0:T(8,128)(2,1)S(1)}, bf16[9,8,256]{2,1,0:T(8,128)(2,1)S(1)}, u32[]{:S(2)}, u32[]{:S(2)}) collective-permute-start(bf16[9,8,256]{2,1,0:T(8,128)(2,1)S(1)} %get-tuple-element.14), channel_id=1, source_target_pairs={{0,4},{4,0},{8,12},{12,8},{16,20},{20,16},{24,28},{28,24},{1,5},{5... | collective-permute-start | bytes 110600 | tf_op jit(solution)/shard_map/ppermute | solution.py:374
  12.7 1.6 %collective-permute-start.4 = (bf16[34,8,256]{2,1,0:T(8,128)(2,1)S(1)}, bf16[34,8,256]{2,1,0:T(8,128)(2,1)S(1)}, u32[]{:S(2)}, u32[]{:S(2)}) collective-permute-start(bf16[34,8,256]{2,1,0:T(8,128)(2,1)S(1)} %pad_maximum_fusion), channel_id=1, source_target_pairs={{0,2},{2,0},{1,3},{3,1},{4,6},{6,4},{5,7},{7,5},{8,10},{10,8},{9,1... | collective-permute-start | bytes 417800 | tf_op jit(solution)/shard_map/ppermute | solution.py:394
  12.8 1.5 %collective-permute-start.5 = (bf16[25,8,256]{2,1,0:T(8,128)(2,1)S(1)}, bf16[25,8,256]{2,1,0:T(8,128)(2,1)S(1)}, u32[]{:S(2)}, u32[]{:S(2)}) collective-permute-start(bf16[25,8,256]{2,1,0:T(8,128)(2,1)S(1)} %pad_maximum_fusion.1), channel_id=1, source_target_pairs={{0,2},{2,0},{1,3},{3,1},{4,6},{6,4},{5,7},{7,5},{8,10},{10,8},{9,1... | collective-permute-start | bytes 307208 | tf_op jit(solution)/shard_map/ppermute | solution.py:397
  17.0 4.0 %collective-permute-start.6 = (bf16[1,144,128]{2,1,0:T(8,128)(2,1)S(1)}, bf16[1,144,128]{2,1,0:T(8,128)(2,1)S(1)}, u32[]{:S(2)}, u32[]{:S(2)}) collective-permute-start(bf16[1,144,128]{2,1,0:T(8,128)(2,1)S(1)} %constant_dynamic-slice_fusion), channel_id=1, source_target_pairs={{0,8},{4,12},{8,0},{12,4},{16,24},{20,28},{24,16},{28,20},{1,9},{5... | collective-permute-start | bytes 110600 | tf_op jit(solution)/shard_map/ppermute | solution.py:421
  21.1 4.0 %collective-permute-start.7 = (bf16[144,128]{1,0:T(8,128)(2,1)S(1)}, bf16[144,128]{1,0:T(8,128)(2,1)S(1)}, u32[]{:S(2)}, u32[]{:S(2)}) collective-permute-start(bf16[144,128]{1,0:T(8,128)(2,1)S(1)} %fusion.refs_0_), channel_id=1, source_target_pairs={{0,1},{1,0},{2,3},{3,2},{4,5},{5,4},{6,7},{7,6},{8,9},{9,8},{10,11... | collective-permute-start | bytes 110600 | tf_op jit(solution)/shard_map/ppermute | solution.py:430

commit v10 on v9

--- a/solution.py
+++ b/solution.py
@@ -230,7 +230,7 @@
                     t2[pl.ds(tap * 192 + 128, CB), :] = grid[row0 : row0 + CB]
     row3 = lax.broadcasted_iota(jnp.int32, (2 * half, 128), 0)
     next_y = row3 % 2 == 0
-    next_x = row3 % half < half - 2 * width
+    gap = jnp.zeros((2 * width, 128), F32)
     grid = contract(delta_b, ordered[...], 1, 1)
     grads = []
     for tap in range(9):
@@ -238,18 +238,23 @@
         c1 = c1 if tap % 2 else pltpu.roll(c1, 64, 1)
         grads.append([grid[:, tap * 128 : tap * 128 + 128], c1])
 
-    def joined(late, early, distance, valid):
-        return [
-            l + jnp.where(valid, pltpu.roll(e, 2 * half - distance, 0), 0.0)
-            for l, e in zip(late, early)
+    def next_cell(late, early):
+        moved = [jnp.where(next_y, pltpu.roll(e, 2 * half - 1, 0), 0.0) for e in early]
+        return [l + e for l, e in zip(late, moved)]
+
+    def next_plane(late, early):
+        moved = [
+            jnp.concatenate([e[2 * width : half], gap, e[half + 2 * width :], gap], axis=0)
+            for e in early
         ]
+        return [l + e for l, e in zip(late, moved)]
 
     for i in range(2):
         if i == 0:
             over_y = grads[3:6]
         else:
-            over_y = [joined(grads[6 + ky], grads[ky], 2 * width, next_x) for ky in range(3)]
-        for parity, (c0, c1) in enumerate((over_y[1], joined(over_y[2], over_y[0], 1, next_y))):
+            over_y = [next_plane(grads[6 + ky], grads[ky]) for ky in range(3)]
+        for parity, (c0, c1) in enumerate((over_y[1], next_cell(over_y[2], over_y[0]))):
             turn = pltpu.roll(c0, 64, 1)
             k0, k1 = turn[:half], turn[half:]
             hgs[i, 0, pl.ds(parity, half, stride=2), :] = jnp.where(low, k0, c1[:half] + k1)
@@ -320,16 +325,21 @@
     h2, h1 = packed_rows(spread)
     total = mine[...].astype(F32) + got[...].astype(F32)
     top = total[:h2].T
-    second_buf[...] = jnp.concatenate([top[:CB], top[CB:]], axis=1)[:, :r2]
-    second_copy = pltpu.make_async_copy(second_buf, second_out, sems.at[0])
-    second_copy.start()
+    copies = []
+    for part in range(2):
+        rows = pl.ds(part * (CB // 2), CB // 2)
+        upper = top[part * (CB // 2) : (part + 1) * (CB // 2)]
+        lower = top[CB + part * (CB // 2) : CB + (part + 1) * (CB // 2)]
+        second_buf[rows, :] = jnp.concatenate([upper, lower], axis=1)[:, :r2]
+        copies.append(pltpu.make_async_copy(second_buf.at[rows], second_out.at[rows], sems.at[part]))
+        copies[-1].start()
     rest = total[h2:].T
     rest = jnp.concatenate([rest[32 * g : 32 * g + 32] for g in range(4)], axis=1)
     first_buf[...] = rest[:, :r1]
-    first_copy = pltpu.make_async_copy(first_buf, first_out, sems.at[1])
-    first_copy.start()
-    second_copy.wait()
-    first_copy.wait()
+    copies.append(pltpu.make_async_copy(first_buf, first_out, sems.at[2]))
+    copies[-1].start()
+    for copy in copies:
+        copy.wait()
 
 
 def swap_bit(count, bit):
@@ -439,7 +449,7 @@
         scratch_shapes=[
             pltpu.VMEM(first_out, F32),
             pltpu.VMEM(second_out, F32),
-            pltpu.SemaphoreType.DMA((2,)),
+            pltpu.SemaphoreType.DMA((3,)),
         ],
         compiler_params=pltpu.CompilerParams(vmem_limit_bytes=16 << 20),
     )(total, came)

time: 26.1 us -> 26.1 us (level)
  no operation moved by 1% of the time
where the time goes in v10:
time: 26.1 us; the launch traced here: 25.9 us
  starting transfers between devices  11.4 us (44%)
  waiting for transfers between devices  7.92 us (30%)
  Pallas kernels  5.84 us (22%)
  between operations  0.68 us (3%)
    ppermute x3, starting transfers between devices, shards(): received[k - 1] = lax.ppermute(pieces[k], ('space', 'section'), route)  5.75 us
    pallas_call x1, Pallas kernels, call(): pl.pallas_call(body, out_shape=out_shape, in_specs=[vmem] * len(args), ou...  2.7 us
    ppermute x1, waiting for transfers between devices, shards(): came = lax.ppermute(total, 'dp', swap_bit(replicas, bit))  2.41 us
    ppermute x3, waiting for transfers between devices, shards(): received[k - 1] = lax.ppermute(pieces[k], ('space', 'section'), route)  2.32 us
    ppermute x1, waiting for transfers between devices, shards(): lax.ppermute(pick(paired, 1 - here, 1), 'space', swap_bit(spread, bit + 1))  2.23 us
    ppermute x1, starting transfers between devices, shards(): lax.ppermute(pick(paired, 1 - here, 1), 'space', swap_bit(spread, bit + 1))  1.79 us
    ppermute x1, starting transfers between devices, shards(): partner = lax.ppermute(pieces[pairs], 'space', swap_bit(spread, 0))  1.64 us
    ppermute x1, starting transfers between devices, shards(): came = lax.ppermute(total, 'dp', swap_bit(replicas, bit))  1.61 us
  transfers between devices with their start and end apart: 8, of which 4 were waited for; matrix products, arithmetic and copies ran while one was open for 0% of the time, Pallas kernels for 6%

profile of v10, /device:TPU:0, one launch (start us, length us, event | category | flops | bytes accessed | tf_op | source)
XLA Modules:
  0.0 25.9 jit_solution(6120392529351383952)
XLA Ops:
  0.6 0.9 %shard_map.59 = (bf16[2,9,8,256]{3,2,1,0:T(8,128)(2,1)S(1)}, bf16[2,8,8,256]{3,2,1,0:T(8,128)(2,1)S(1)}, bf16[2,8,8,256]{3,2,1,0:T(8,128)(2,1)S(1)}, bf16[2,9,8,...) custom-call(bf16[2,1,2,8,8,256]{5,4,3,2,1,0:T(8,128)(2,1)} %refs_0_.1, bf16[2,1,4,1,2,256]{5,4,3,2,1,0:T(2,128)(2,1)} %refs_1_.1), custom_call_target="tpu_custom_call" | custom-call | tf_op jit(solution)/shard_map/pallas_call | solution.py:360
  1.5 5.1 %collective-permute-start.3 = (bf16[2,9,8,256]{3,2,1,0:T(8,128)(2,1)S(1)}, bf16[2,9,8,256]{3,2,1,0:T(8,128)(2,1)S(1)}, u32[]{:S(2)}, u32[]{:S(2)}) collective-permute-start(bf16[2,9,8,256]{3,2,1,0:T(8,128)(2,1)S(1)} %get-tuple-element.17), channel_id=1, source_target_pairs={{0,24},{2,30},{4,28},{6,26},{8,16},{10,22},{12,20},{14,18},{16,8},... | collective-permute-start | bytes 221192 | tf_op jit(solution)/shard_map/ppermute | solution.py:383
  6.6 0.0 collective-permute-start.1
  6.6 0.6 %collective-permute-start.2 = (bf16[2,8,8,256]{3,2,1,0:T(8,128)(2,1)S(1)}, bf16[2,8,8,256]{3,2,1,0:T(8,128)(2,1)S(1)}, u32[]{:S(2)}, u32[]{:S(2)}) collective-permute-start(bf16[2,8,8,256]{3,2,1,0:T(8,128)(2,1)S(1)} %get-tuple-element.16), channel_id=1, source_target_pairs={{0,16},{2,22},{4,20},{6,18},{8,24},{10,30},{12,28},{14,26},{16,0},... | collective-permute-start | bytes 196616 | tf_op jit(solution)/shard_map/ppermute | solution.py:383
  7.3 1.6 %collective-permute-start = (bf16[9,8,256]{2,1,0:T(8,128)(2,1)S(1)}, bf16[9,8,256]{2,1,0:T(8,128)(2,1)S(1)}, u32[]{:S(2)}, u32[]{:S(2)}) collective-permute-start(bf16[9,8,256]{2,1,0:T(8,128)(2,1)S(1)} %get-tuple-element.14), channel_id=1, source_target_pairs={{0,4},{4,0},{8,12},{12,8},{16,20},{20,16},{24,28},{28,24},{1,5},{5... | collective-permute-start | bytes 110600 | tf_op jit(solution)/shard_map/ppermute | solution.py:384
  8.9 1.4 %shard_map.60 = (bf16[2304,256]{1,0:T(8,128)(2,1)S(1)}, bf16[1792,128]{1,0:T(8,128)(2,1)S(1)}) custom-call(bf16[64,864]{1,0:T(8,128)(2,1)} %bitcast.11, bf16[1728,128]{1,0:T(8,128)(2,1)} %second_hbm.1), custom_call_target="tpu_custom_call" | custom-call | tf_op jit(solution)/shard_map/pallas_call | solution.py:385
  10.4 2.3 %collective-permute-done.1.refs_2_ = bf16[2,8,8,256]{3,2,1,0:T(8,128)(2,1)S(1)} collective-permute-done((bf16[2,8,8,256]{3,2,1,0:T(8,128)(2,1)S(1)}, bf16[2,8,8,256]{3,2,1,0:T(8,128)(2,1)S(1)}, u32[]{:S(2)}, u32[]{:S(2)}) %collective-permute-start.1) | collective-permute-done | bytes 65568 | tf_op jit(solution)/shard_map/ppermute | solution.py:383
  12.7 0.0 collective-permute-done.2.refs_3_
  12.7 0.0 collective-permute-done.3.refs_4_
  12.7 0.1 collective-permute-start.4
  12.8 0.0 collective-permute-done.refs_1_
  12.8 0.5 %collective-permute-start.5 = (bf16[25,8,256]{2,1,0:T(8,128)(2,1)S(1)}, bf16[25,8,256]{2,1,0:T(8,128)(2,1)S(1)}, u32[]{:S(2)}, u32[]{:S(2)}) collective-permute-start(bf16[25,8,256]{2,1,0:T(8,128)(2,1)S(1)} %pad_maximum_fusion.1), channel_id=1, source_target_pairs={{0,2},{2,0},{1,3},{3,1},{4,6},{6,4},{5,7},{7,5},{8,10},{10,8},{9,1... | collective-permute-start | bytes 307208 | tf_op jit(solution)/shard_map/ppermute | solution.py:407
  13.4 0.9 %collective-permute-done.5.refs_6_ = bf16[25,8,256]{2,1,0:T(8,128)(2,1)S(1)} collective-permute-done((bf16[25,8,256]{2,1,0:T(8,128)(2,1)S(1)}, bf16[25,8,256]{2,1,0:T(8,128)(2,1)S(1)}, u32[]{:S(2)}, u32[]{:S(2)}) %collective-permute-start.5) | collective-permute-done | bytes 102432 | tf_op jit(solution)/shard_map/ppermute | solution.py:407
  14.3 0.0 collective-permute-done.4.refs_5_
  14.3 2.7 %shard_map.61 = bf16[2,144,128]{2,1,0:T(8,128)(2,1)S(1)} custom-call(bf16[2,9,8,256]{3,2,1,0:T(8,128)(2,1)S(1)} %get-tuple-element.13.refs_0_, bf16[9,8,256]{2,1,0:T(8,128)(2,1)S(1)} %collective-permute-done.refs_1_, bf16[2,8,8,256]{3,2,1,0:T(8,128)(2,1)S(1)} %collective-permute-done.1.refs_2_, bf16[2,8,8,256]{3,2,1,0:T(8,128)(2,1)S(1)} %collective-permute-done.2.refs_3_, ...), custom_call_target="tpu_custom_call" | custom-call | tf_op jit(solution)/shard_map/pallas_call | solution.py:32
  17.0 1.8 %collective-permute-start.6 = (bf16[1,144,128]{2,1,0:T(8,128)(2,1)S(1)}, bf16[1,144,128]{2,1,0:T(8,128)(2,1)S(1)}, u32[]{:S(2)}, u32[]{:S(2)}) collective-permute-start(bf16[1,144,128]{2,1,0:T(8,128)(2,1)S(1)} %constant_dynamic-slice_fusion), channel_id=1, source_target_pairs={{0,8},{4,12},{8,0},{12,4},{16,24},{20,28},{24,16},{28,20},{1,9},{5... | collective-permute-start | bytes 110600 | tf_op jit(solution)/shard_map/ppermute | solution.py:431
  18.8 2.2 %collective-permute-done.6 = bf16[1,144,128]{2,1,0:T(8,128)(2,1)S(1)} collective-permute-done((bf16[1,144,128]{2,1,0:T(8,128)(2,1)S(1)}, bf16[1,144,128]{2,1,0:T(8,128)(2,1)S(1)}, u32[]{:S(2)}, u32[]{:S(2)}) %collective-permute-start.6) | collective-permute-done | bytes 36896 | tf_op jit(solution)/shard_map/ppermute | solution.py:431
  21.1 1.6 %collective-permute-start.7 = (bf16[144,128]{1,0:T(8,128)(2,1)S(1)}, bf16[144,128]{1,0:T(8,128)(2,1)S(1)}, u32[]{:S(2)}, u32[]{:S(2)}) collective-permute-start(bf16[144,128]{1,0:T(8,128)(2,1)S(1)} %fusion.refs_0_), channel_id=1, source_target_pairs={{0,1},{1,0},{2,3},{3,2},{4,5},{5,4},{6,7},{7,6},{8,9},{9,8},{10,11... | collective-permute-start | bytes 110600 | tf_op jit(solution)/shard_map/ppermute | solution.py:440
  22.7 2.4 %collective-permute-done.7.refs_1_ = bf16[144,128]{1,0:T(8,128)(2,1)S(1)} collective-permute-done((bf16[144,128]{1,0:T(8,128)(2,1)S(1)}, bf16[144,128]{1,0:T(8,128)(2,1)S(1)}, u32[]{:S(2)}, u32[]{:S(2)}) %collective-permute-start.7) | collective-permute-done | bytes 36896 | tf_op jit(solution)/shard_map/ppermute | solution.py:440
  25.1 0.8 %shard_map.62 = (f32[32,108]{1,0:T(8,128)}, f32[64,216]{1,0:T(8,128)}) custom-call(bf16[144,128]{1,0:T(8,128)(2,1)S(1)} %fusion.refs_0_, bf16[144,128]{1,0:T(8,128)(2,1)S(1)} %collective-permute-done.7.refs_1_), custom_call_target="tpu_custom_call" | custom-call | tf_op jit(solution)/shard_map/pallas_call | solution.py:444
  (4 shorter events, 0.1 us)
Async XLA Ops:
  1.5 11.2 %collective-permute-start.3 = (bf16[2,9,8,256]{3,2,1,0:T(8,128)(2,1)S(1)}, bf16[2,9,8,256]{3,2,1,0:T(8,128)(2,1)S(1)}, u32[]{:S(2)}, u32[]{:S(2)}) collective-permute-start(bf16[2,9,8,256]{3,2,1,0:T(8,128)(2,1)S(1)} %get-tuple-element.17), channel_id=1, source_target_pairs={{0,24},{2,30},{4,28},{6,26},{8,16},{10,22},{12,20},{14,18},{16,8},... | collective-permute-start | bytes 221192 | tf_op jit(solution)/shard_map/ppermute | solution.py:383
  6.6 6.0 %collective-permute-start.1 = (bf16[2,8,8,256]{3,2,1,0:T(8,128)(2,1)S(1)}, bf16[2,8,8,256]{3,2,1,0:T(8,128)(2,1)S(1)}, u32[]{:S(2)}, u32[]{:S(2)}) collective-permute-start(bf16[2,8,8,256]{3,2,1,0:T(8,128)(2,1)S(1)} %get-tuple-element.15), channel_id=1, source_target_pairs={{0,8},{2,14},{4,12},{6,10},{8,0},{10,6},{12,4},{14,2},{16,24},{18,... | collective-permute-start | bytes 196616 | tf_op jit(solution)/shard_map/ppermute | solution.py:383
  6.6 6.0 %collective-permute-start.2 = (bf16[2,8,8,256]{3,2,1,0:T(8,128)(2,1)S(1)}, bf16[2,8,8,256]{3,2,1,0:T(8,128)(2,1)S(1)}, u32[]{:S(2)}, u32[]{:S(2)}) collective-permute-start(bf16[2,8,8,256]{3,2,1,0:T(8,128)(2,1)S(1)} %get-tuple-element.16), channel_id=1, source_target_pairs={{0,16},{2,22},{4,20},{6,18},{8,24},{10,30},{12,28},{14,26},{16,0},... | collective-permute-start | bytes 196616 | tf_op jit(solution)/shard_map/ppermute | solution.py:383
  7.3 5.5 %collective-permute-start = (bf16[9,8,256]{2,1,0:T(8,128)(2,1)S(1)}, bf16[9,8,256]{2,1,0:T(8,128)(2,1)S(1)}, u32[]{:S(2)}, u32[]{:S(2)}) collective-permute-start(bf16[9,8,256]{2,1,0:T(8,128)(2,1)S(1)} %get-tuple-element.14), channel_id=1, source_target_pairs={{0,4},{4,0},{8,12},{12,8},{16,20},{20,16},{24,28},{28,24},{1,5},{5... | collective-permute-start | bytes 110600 | tf_op jit(solution)/shard_map/ppermute | solution.py:384
  12.7 1.6 %collective-permute-start.4 = (bf16[34,8,256]{2,1,0:T(8,128)(2,1)S(1)}, bf16[34,8,256]{2,1,0:T(8,128)(2,1)S(1)}, u32[]{:S(2)}, u32[]{:S(2)}) collective-permute-start(bf16[34,8,256]{2,1,0:T(8,128)(2,1)S(1)} %pad_maximum_fusion), channel_id=1, source_target_pairs={{0,2},{2,0},{1,3},{3,1},{4,6},{6,4},{5,7},{7,5},{8,10},{10,8},{9,1... | collective-permute-start | bytes 417800 | tf_op jit(solution)/shard_map/ppermute | solution.py:404
  12.8 1.5 %collective-permute-start.5 = (bf16[25,8,256]{2,1,0:T(8,128)(2,1)S(1)}, bf16[25,8,256]{2,1,0:T(8,128)(2,1)S(1)}, u32[]{:S(2)}, u32[]{:S(2)}) collective-permute-start(bf16[25,8,256]{2,1,0:T(8,128)(2,1)S(1)} %pad_maximum_fusion.1), channel_id=1, source_target_pairs={{0,2},{2,0},{1,3},{3,1},{4,6},{6,4},{5,7},{7,5},{8,10},{10,8},{9,1... | collective-permute-start | bytes 307208 | tf_op jit(solution)/shard_map/ppermute | solution.py:407
  17.0 4.0 %collective-permute-start.6 = (bf16[1,144,128]{2,1,0:T(8,128)(2,1)S(1)}, bf16[1,144,128]{2,1,0:T(8,128)(2,1)S(1)}, u32[]{:S(2)}, u32[]{:S(2)}) collective-permute-start(bf16[1,144,128]{2,1,0:T(8,128)(2,1)S(1)} %constant_dynamic-slice_fusion), channel_id=1, source_target_pairs={{0,8},{4,12},{8,0},{12,4},{16,24},{20,28},{24,16},{28,20},{1,9},{5... | collective-permute-start | bytes 110600 | tf_op jit(solution)/shard_map/ppermute | solution.py:431
  21.1 4.0 %collective-permute-start.7 = (bf16[144,128]{1,0:T(8,128)(2,1)S(1)}, bf16[144,128]{1,0:T(8,128)(2,1)S(1)}, u32[]{:S(2)}, u32[]{:S(2)}) collective-permute-start(bf16[144,128]{1,0:T(8,128)(2,1)S(1)} %fusion.refs_0_), channel_id=1, source_target_pairs={{0,1},{1,0},{2,3},{3,2},{4,5},{5,4},{6,7},{7,6},{8,9},{9,8},{10,11... | collective-permute-start | bytes 110600 | tf_op jit(solution)/shard_map/ppermute | solution.py:440
